TPU v7x, 32 devices: a whole 2x2x4 slice. The times are simulated.
32 devices in a mesh: tm: 4 (over y, core), agent: 8 (over z, x).
Axes of the slice: x: 2, y: 2, z: 4, core: 2. Of those that a mesh axis runs over, the one named last changes fastest.
Arguments:
- features: bfloat16 [16, 512, 512], P('agent', 'tm'), may hold values from -6 to 6
- norm_gain: float32 [512], replicated, may hold values from 0.1 to 1.9
- w_query: bfloat16 [512, 512], P('agent'), may hold values from -8 to 8
- w_key: bfloat16 [512, 512], P('agent'), may hold values from -8 to 8
- w_value: bfloat16 [512, 512], P('agent'), may hold values from -1 to 1
- w_out: bfloat16 [512, 512], P('agent'), may hold values from -0.5 to 0.5
- tracks: int32 [16, 2], P('agent'), may hold values from 0 to 512, as said below
Outputs:
- mixed_out: bfloat16 [16, 512, 512], P('agent', 'tm')
Inputs may be any that keep to these rules, and one draw needn't show every extreme that they name: tracks[a, 0] < 256, tracks[a, 1] - tracks[a, 0] >= 128 unless tracks[a, 1] = 512; some agent spans all 512 steps.
All inputs are finite; a program needn't handle non-finite values.
Results may differ from a plain program's by a relative error of at most 0.0082.
Values may be sent and summed in bfloat16 or wider, within the bound.
No kernel may reach another device: no remote copies, remote signals or barrier semaphores. Data moves between devices by JAX's collectives and lax.ppermute only.
A program may use at most 64 MiB of HBM per device.

v0:
```python
import math

import jax
import jax.numpy as jnp
from jax import lax
from jax.sharding import PartitionSpec as P

HEADS = 8


EPSILON = 1e-05
NEGATIVE = -1e30


def normalize(inputs, gain):
    values = inputs.astype(jnp.float32)
    meansq = jnp.mean(values * values, axis=-1, keepdims=True)
    return (values * lax.rsqrt(meansq + EPSILON) * gain).astype(jnp.bfloat16)


def project(normed, weight):
    return jnp.einsum("asd,de->ase", normed, weight, preferred_element_type=jnp.float32).astype(
        jnp.bfloat16
    )


def body(features, norm_gain, w_query, w_key, w_value, w_out, tracks):
    full_query, full_key, full_value, full_out = (
        lax.all_gather(w_query, "agent", axis=0, tiled=True),
        lax.all_gather(w_key, "agent", axis=0, tiled=True),
        lax.all_gather(w_value, "agent", axis=0, tiled=True),
        lax.all_gather(w_out, "agent", axis=0, tiled=True),
    )
    agents_here, rows_here, width = features.shape
    head_dim = width // HEADS
    scale = 1.0 / math.sqrt(head_dim)
    normed = normalize(features, norm_gain)
    starts = tracks[:, 0]
    ends = tracks[:, 1]
    queries = project(normed, full_query).reshape(agents_here, rows_here, HEADS, head_dim)
    first_row = lax.axis_index("tm") * rows_here
    query_pos = first_row + jnp.arange(rows_here, dtype=jnp.int32)
    row_live = (query_pos[None, :] >= starts[:, None]) & (query_pos[None, :] < ends[:, None])
    initial = (
        jnp.full((agents_here, HEADS, rows_here), NEGATIVE, jnp.float32),
        jnp.zeros((agents_here, HEADS, rows_here), jnp.float32),
        jnp.zeros((agents_here, HEADS, rows_here, head_dim), jnp.float32),
    )

    def attend(carry, key_block, value_block, key_start):
        highest, total, summed = carry
        count = key_block.shape[1]
        key_pos = key_start + jnp.arange(count, dtype=jnp.int32)
        scores = (
            jnp.einsum("athd,ashd->ahts", queries, key_block, preferred_element_type=jnp.float32)
            * scale
        )
        allowed = (
            (key_pos[None, None, :] >= starts[:, None, None])
            & (key_pos[None, None, :] <= query_pos[None, :, None])
            & row_live[:, :, None]
        )
        allowed = allowed[:, None]
        masked = jnp.where(allowed, scores, NEGATIVE)
        new_high = jnp.maximum(highest, jnp.max(masked, axis=-1))
        weights = jnp.where(allowed, jnp.exp(scores - new_high[..., None]), 0.0)
        factor = jnp.exp(highest - new_high)
        total = factor * total + jnp.sum(weights, axis=-1)
        summed = factor[..., None] * summed + jnp.einsum(
            "ahts,ashd->ahtd",
            weights.astype(jnp.bfloat16),
            value_block,
            preferred_element_type=jnp.float32,
        )
        return (new_high, total, summed)

    def visit(carry, key_block, value_block, key_start):
        return attend(carry, key_block, value_block, key_start)

    def sweep(carry, key_rows, value_rows, key_start):
        count = key_rows.shape[1]
        span = 512
        if span == count:
            return visit(carry, key_rows, value_rows, key_start)

        def advance(index, state):
            offset = (index * span).astype(jnp.int32)
            key_block = lax.dynamic_slice_in_dim(key_rows, offset, span, 1)
            value_block = lax.dynamic_slice_in_dim(value_rows, offset, span, 1)
            return visit(state, key_block, value_block, key_start + offset)

        return lax.fori_loop(0, count // span, advance, carry)

    piece = lax.all_gather(normed, "tm", axis=1, tiled=True)
    count = piece.shape[1]
    key_rows = project(piece, full_key).reshape(agents_here, count, HEADS, head_dim)
    value_rows = project(piece, full_value).reshape(agents_here, count, HEADS, head_dim)
    final = sweep(initial, key_rows, value_rows, jnp.int32(0))
    highest, total, summed = final
    denom = jnp.where(row_live[:, None, :], total, 1.0)
    attended = summed / denom[..., None] * row_live[:, None, :, None].astype(jnp.float32)
    attended = (
        jnp.transpose(attended, (0, 2, 1, 3))
        .reshape(agents_here, rows_here, width)
        .astype(jnp.bfloat16)
    )
    projected = jnp.einsum(
        "asd,de->aes", attended, full_out, preferred_element_type=jnp.float32
    ).astype(jnp.bfloat16)
    return lax.all_to_all(projected, "tm", split_axis=1, concat_axis=2, tiled=True)


def solution(mesh):
    in_specs = (
        P("agent", "tm", None),
        P(),
        P("agent", None),
        P("agent", None),
        P("agent", None),
        P("agent", None),
        P("agent", None),
    )
    out_specs = P("agent", "tm", None)
    return jax.shard_map(body, mesh=mesh, in_specs=in_specs, out_specs=out_specs, check_vma=False)
```

profile of v0, /device:TPU:0, one launch (start us, length us, event | category | flops | bytes accessed | tf_op | source)
XLA Modules:
  0.0 163.3 jit_solution(18336218210574915154)
XLA Ops:
  6.5 1.1 fusion.24
  7.7 1.8 %fusion.26 = bf16[2,128,512]{2,1,0:T(8,128)(2,1)} fusion(bf16[2,128,512]{2,1,0:T(8,128)(2,1)} %param.7, f32[512]{0:T(512)} %param.8, f32[2,128]{1,0:T(2,128)S(1)} %add_rsqrt_fusion), kind=kLoop, calls=%fused_computation.23 | loop fusion | flops 524288 | bytes 527360 | tf_op jit(solution)/shard_map/convert_element_type | solution.py:18
  9.4 0.0 all-gather.2.cloned.1.call-update
  9.5 1.0 slice_reduce_fusion.1
  10.5 33.5 %all_gather.15 = bf16[512,512]{1,0:T(8,128)(2,1)S(1)} all-gather(bf16[64,512]{1,0:T(8,128)(2,1)} %param.9), channel_id=1, replica_groups=mesh['tm'=4,'agent'=8] {'agent'}, dimensions={0}, use_global_device_ids=true | all-gather | bytes 589824 | tf_op jit(solution)/shard_map/all_gather | solution.py:29
  43.9 1.2 convolution_convert_fusion.3
  45.2 0.2 copy.14
  45.4 0.1 iota_compare_fusion.1
  45.4 0.1 fusion.34
  45.5 0.1 iota_compare_fusion
  45.6 0.1 and_and_fusion
  45.8 31.6 %all_gather.18 = bf16[512,512]{1,0:T(8,128)(2,1)S(1)} all-gather(bf16[64,512]{1,0:T(8,128)(2,1)} %param.11), channel_id=1, replica_groups=mesh['tm'=4,'agent'=8] {'agent'}, dimensions={0}, use_global_device_ids=true | all-gather | bytes 589824 | tf_op jit(solution)/shard_map/all_gather | solution.py:31
  77.4 31.6 %all_gather.17 = bf16[512,512]{1,0:T(8,128)(2,1)S(1)} all-gather(bf16[64,512]{1,0:T(8,128)(2,1)} %param.10), channel_id=1, replica_groups=mesh['tm'=4,'agent'=8] {'agent'}, dimensions={0}, use_global_device_ids=true | all-gather | bytes 589824 | tf_op jit(solution)/shard_map/all_gather | solution.py:30
  108.9 31.4 %all_gather.19 = bf16[512,512]{1,0:T(8,128)(2,1)S(1)} all-gather(bf16[64,512]{1,0:T(8,128)(2,1)S(1)} %copy-done), channel_id=1, replica_groups=mesh['tm'=4,'agent'=8] {'agent'}, dimensions={0}, use_global_device_ids=true | all-gather | bytes 589824 | tf_op jit(solution)/shard_map/all_gather | solution.py:32
  140.3 2.0 %convolution_convert_fusion.1 = bf16[2,512,512]{1,2,0:T(8,128)(2,1)S(1)} fusion(bf16[2,512,512]{2,1,0:T(8,128)(2,1)} %all-gather.2.cloned.1.call-done, bf16[512,512]{1,0:T(8,128)(2,1)S(1)} %all_gather.17), kind=kOutput, calls=%fused_computation.10 | convolution fusion | flops 537395200 | bytes 2621440 | tf_op jit(solution)/shard_map/asd,de->ase/dot_general | solution.py:22
  142.3 0.9 select_reduce_fusion
  143.3 1.2 fusion
  144.5 0.8 convolution_convert_fusion
  145.3 1.1 fusion.21
  146.4 0.3 fusion.14
  146.8 0.2 copy.16
  146.9 8.5 %all_to_all.18 = bf16[2,512,128]{2,0,1:T(2,128)(2,1)S(1)} all-to-all(bf16[2,512,128]{2,0,1:T(2,128)(2,1)S(1)} %copy.16), channel_id=1, replica_groups=mesh['tm'=4,'agent'=8] {'tm'}, dimensions={1} | all-to-all | bytes 524288 | tf_op jit(solution)/shard_map/all_to_all | solution.py:110
  155.5 0.2 copy.17
  155.7 0.8 all_to_all.16
  (10 shorter events, 0.0 us)
Async XLA Ops:
  6.5 102.4 %copy-start = (bf16[64,512]{1,0:T(8,128)(2,1)S(1)}, bf16[64,512]{1,0:T(8,128)(2,1)}, u32[]{:S(2)}) copy-start(bf16[64,512]{1,0:T(8,128)(2,1)} %param.12) | copy-start | bytes 196612
  6.5 133.8 %all-gather.2.cloned.1.call-start = ((), (), s32[]{:S(2)}) async-start(), calls=%async_computation.1 | async-start | bytes 1310720 | tf_op jit(solution)/shard_map/all_gather | solution.py:94
  142.3 2.2 %copy-start.1 = (bf16[2,512,512]{2,1,0:T(8,128)(2,1)S(1)}, bf16[2,512,512]{2,1,0:T(8,128)(2,1)}, u32[]{:S(2)}) copy-start(bf16[2,512,512]{2,1,0:T(8,128)(2,1)} %all-gather.2.cloned.1.call-done) | copy-start | bytes 3145732
Sparse Core Ops, SparseCore 0:
  9.6 19.4 all-gather.1
where the time goes:
time: 164 us; the launch traced here: 163 us
  blocking collectives  137 us (84%)
  between operations  13.5 us (8%)
  matrix products  6.41 us (4%)
  other arithmetic  4.5 us (3%)
  local copies, waits for them, and re-layouts  2.31 us (1%)
    all_gather x1, blocking collectives, body(): lax.all_gather(w_query, 'agent', axis=0, tiled=True)  33.5 us
    all_gather x1, blocking collectives, body(): lax.all_gather(w_value, 'agent', axis=0, tiled=True)  31.6 us
    all_gather x1, blocking collectives, body(): lax.all_gather(w_key, 'agent', axis=0, tiled=True)  31.6 us
    all_gather x1, blocking collectives, body(): lax.all_gather(w_out, 'agent', axis=0, tiled=True)  31.4 us
    all_to_all x1, blocking collectives, body(): lax.all_to_all(projected, 'tm', split_axis=1, concat_axis=2, tiled=True)  8.54 us
    dot_general x3, matrix products, project(): jnp.einsum('asd,de->ase', normed, weight, preferred_element_type=jnp.floa...  3.98 us
  transfers between devices with their start and end apart: 1, of which 0 were waited for; matrix products, arithmetic and copies ran while one was open for 2% of the time, Pallas kernels for 0%

commit v1 on v0

--- a/solution.py
+++ b/solution.py
@@ -1,15 +1,20 @@
+import functools
 import math
 
 import jax
 import jax.numpy as jnp
 from jax import lax
+from jax.experimental import pallas as pl
+from jax.experimental.pallas import tpu as pltpu
 from jax.sharding import PartitionSpec as P
+
 
 HEADS = 8
 
 
 EPSILON = 1e-05
 NEGATIVE = -1e30
+LANES = 128
 
 
 def normalize(inputs, gain):
@@ -74,20 +79,17 @@
         )
         return (new_high, total, summed)
 
-    def visit(carry, key_block, value_block, key_start):
-        return attend(carry, key_block, value_block, key_start)
-
     def sweep(carry, key_rows, value_rows, key_start):
         count = key_rows.shape[1]
         span = 512
         if span == count:
-            return visit(carry, key_rows, value_rows, key_start)
+            return attend(carry, key_rows, value_rows, key_start)
 
         def advance(index, state):
             offset = (index * span).astype(jnp.int32)
             key_block = lax.dynamic_slice_in_dim(key_rows, offset, span, 1)
             value_block = lax.dynamic_slice_in_dim(value_rows, offset, span, 1)
-            return visit(state, key_block, value_block, key_start + offset)
+            return attend(state, key_block, value_block, key_start + offset)
 
         return lax.fori_loop(0, count // span, advance, carry)
 
@@ -96,7 +98,7 @@
     key_rows = project(piece, full_key).reshape(agents_here, count, HEADS, head_dim)
     value_rows = project(piece, full_value).reshape(agents_here, count, HEADS, head_dim)
     final = sweep(initial, key_rows, value_rows, jnp.int32(0))
-    highest, total, summed = final
+    _, total, summed = final
     denom = jnp.where(row_live[:, None, :], total, 1.0)
     attended = summed / denom[..., None] * row_live[:, None, :, None].astype(jnp.float32)
     attended = (
@@ -110,6 +112,270 @@
     return lax.all_to_all(projected, "tm", split_axis=1, concat_axis=2, tiled=True)
 
 
+def params():
+    return pltpu.CompilerParams(vmem_limit_bytes=24 * 2**20)
+
+
+def cost(flops, transcendentals=0, bytes_accessed=2**20):
+    return pl.CostEstimate(
+        flops=flops, transcendentals=transcendentals, bytes_accessed=bytes_accessed
+    )
+
+
+def norm_kernel(tracks_ref, gain_ref, mine_ref, beside_ref, other_ref, diagonal_ref, *outs):
+    normed_ref, bounds_ref = outs
+    rows_here = mine_ref.shape[1]
+    tm = lax.axis_index("tm")
+    core = tm % 2
+    gain = gain_ref[...]
+    for k, ref in enumerate((mine_ref, beside_ref, other_ref, diagonal_ref)):
+        rows = pl.ds(pl.multiple_of((tm ^ k) * rows_here, rows_here), rows_here)
+        normed_ref[rows, :] = normalize(ref[core], gain)
+    for n in range(2):
+        bounds_ref[n] = jnp.full(bounds_ref.shape[1:], tracks_ref[core, n], jnp.int32)
+
+
+def attend(bounds_ref, queries, keys, values, out_ref, head_dim):
+    span, steps = out_ref.shape
+    block = LANES
+    scale = 1.0 / math.sqrt(head_dim)
+    start, end = bounds_ref[0, :1, :block], bounds_ref[1, :1, :block]
+    lane = lax.broadcasted_iota(jnp.int32, (block, span), 1)
+    for j in range(steps // block):
+        reach = (j + 1) * block
+        key_pos = lax.broadcasted_iota(jnp.int32, (reach, block), 0)
+        query_pos = j * block + lax.broadcasted_iota(jnp.int32, (reach, block), 1)
+        allowed = (key_pos >= start) & (key_pos <= query_pos)
+        column = j * block + lax.broadcasted_iota(jnp.int32, (1, block), 1)
+        live = (column >= start) & (column < end)
+        query_block = queries[pl.ds(j * block, block), :]
+        for h in range(span // head_dim):
+            mine = (lane >= h * head_dim) & (lane < (h + 1) * head_dim)
+            one = jnp.where(mine, query_block, jnp.zeros_like(query_block))
+            scores = lax.dot_general(
+                keys[pl.ds(0, reach), :],
+                one,
+                (((1,), (1,)), ((), ())),
+                preferred_element_type=jnp.float32,
+            )
+            scores = jnp.where(allowed, scores * scale, NEGATIVE)
+            highest = jnp.max(scores, axis=0, keepdims=True)
+            weight = jnp.exp(scores - highest)
+            total = jnp.sum(weight, axis=0, keepdims=True)
+            summed = jnp.dot(
+                values[pl.ds(h * head_dim, head_dim), pl.ds(0, reach)],
+                weight.astype(jnp.bfloat16),
+                preferred_element_type=jnp.float32,
+            )
+            result = jnp.where(live, summed / total, 0.0)
+            out_ref[pl.ds(h * head_dim, head_dim), pl.ds(j * block, block)] = result.astype(
+                jnp.bfloat16
+            )
+
+
+def place(sources, refs, target, begin, columns):
+    depth = refs[0].shape[0]
+    agent = lax.axis_index("agent")
+    core = lax.axis_index("tm") % 2
+
+    def put(ref, index):
+        rows = pl.ds(pl.multiple_of(index * depth, depth), depth)
+        low = min(begin, ref.shape[1] - columns)
+        target[rows, :] = ref[:, low : low + columns]
+
+    put(refs[0], agent)
+    for n, pair in enumerate(sources):
+        for here in (0, 1):
+            for ref, offset in zip(refs[1 + 2 * n : 3 + 2 * n], (pair[here], pair[1 - here])):
+                if offset is not None:
+                    pl.when(core == here)(functools.partial(put, ref, agent ^ offset))
+
+
+def first_kernel(sources, head_dim, bounds_ref, normed_ref, *refs):
+    shards, refs = refs[: 1 + 2 * len(sources)], refs[1 + 2 * len(sources) :]
+    out_ref, late, weights, held = refs[0], refs[1:4], refs[4], refs[5:]
+    _, columns = weights.shape
+    span = columns // 3
+    place(sources, shards, weights, 0, columns)
+    for n in range(3):
+        full = jnp.dot(
+            normed_ref[...], weights[:, n * span : (n + 1) * span], preferred_element_type=jnp.float32
+        )
+        for m, target in enumerate((held[n], late[n])):
+            part = full[:, m * LANES : (m + 1) * LANES]
+            target[...] = (part.T if n == 2 else part).astype(jnp.bfloat16)
+    attend(bounds_ref, *held, out_ref, head_dim)
+
+
+def second_kernel(head_dim, bounds_ref, queries, keys, values, out_ref):
+    attend(bounds_ref, queries, keys, values, out_ref, head_dim)
+
+
+def transposed_dot(weight, value):
+    return lax.dot_general(
+        weight, value, (((0,), (0,)), ((), ())), preferred_element_type=jnp.float32
+    )
+
+
+def partial_kernel(sources, *refs):
+    shards, refs = refs[: 1 + 2 * len(sources)], refs[1 + 2 * len(sources) :]
+    here, kept_ref, given_ref, kept_weights, given_weights, weights = (
+        refs[:3],
+        *refs[3:7],
+        refs[7],
+    )
+    _, columns = weights.shape
+    half = columns // 2
+    core, y = lax.axis_index("tm") % 2, lax.axis_index("tm") // 2
+    place(sources, shards, weights, 3 * columns, columns)
+    for n, (ref, last) in enumerate(((kept_ref, kept_weights), (given_ref, given_weights))):
+        lanes = pl.ds(pl.multiple_of((core ^ n) * half, half), half)
+        total = None
+        for m, value in enumerate(here):
+            first = ((y ^ (m // 2)) * 2 + m % 2) * LANES
+            rows = pl.ds(pl.multiple_of(first, LANES), LANES)
+            term = transposed_dot(weights[rows, lanes], value[...])
+            total = term if total is None else total + term
+        ref[...] = total
+        last[...] = weights[pl.ds(pl.multiple_of(((y ^ 1) * 2 + 1) * LANES, LANES), LANES), lanes]
+
+
+def given_kernel(partial_ref, weights_ref, value_ref, out_ref):
+    out_ref[...] = (partial_ref[...] + transposed_dot(weights_ref[...], value_ref[...])).astype(
+        jnp.bfloat16
+    )
+
+
+def final_kernel(partial_ref, weights_ref, value_ref, received_ref, out_ref):
+    core = lax.axis_index("tm") % 2
+    out_ref[1 - core] = received_ref[...]
+    out_ref[core] = (partial_ref[...] + transposed_dot(weights_ref[...], value_ref[...])).astype(
+        jnp.bfloat16
+    )
+
+
+def fits(n_tm, n_agent, features):
+    agents_here, rows_here, width = features.shape
+    return (
+        n_tm == 4
+        and n_agent >= 4
+        and n_agent & (n_agent - 1) == 0
+        and agents_here == 2
+        and width == 4 * LANES
+        and LANES % (width // HEADS) == 0
+        and rows_here % LANES == 0
+        and width % (16 * n_agent) == 0
+        and n_tm * rows_here * width <= 2**20
+    )
+
+
+def split_heads(n_tm, n_agent, features, norm_gain, w_query, w_key, w_value, w_out, tracks):
+    _, rows_here, width = features.shape
+    head_dim = width // HEADS
+    span = width // 2
+    steps = n_tm * rows_here
+    y = lax.axis_index("tm") // 2
+
+    def across(value):
+        return lax.ppermute(value, "tm", [(i, i ^ 2) for i in range(n_tm)])
+
+    def swap(value):
+        return lax.ppermute(value, "tm", [(i, i ^ 1) for i in range(n_tm)])
+
+    def fetch(value, offsets):
+        pairs = [
+            (t * n_agent + (a ^ offsets[t % 2]), t * n_agent + a)
+            for t in range(n_tm)
+            for a in range(n_agent)
+            if offsets[t % 2] is not None
+        ]
+        return lax.ppermute(value, ("tm", "agent"), pairs)
+
+    def kernel(body, outs, args, scratch=(), smem=0, **estimate):
+        vmem = pl.BlockSpec(memory_space=pltpu.VMEM)
+        out = pl.pallas_call(
+            body,
+            out_shape=[jax.ShapeDtypeStruct(shape, dtype) for shape, dtype in outs],
+            in_specs=[pl.BlockSpec(memory_space=pltpu.SMEM)] * smem + [vmem] * (len(args) - smem),
+            out_specs=[vmem] * len(outs),
+            scratch_shapes=[pltpu.VMEM(shape, dtype) for shape, dtype in scratch],
+            compiler_params=params(),
+            cost_estimate=cost(**estimate),
+        )(*args)
+        return out
+
+    half, full = jnp.bfloat16, jnp.float32
+    pieces = [
+        lax.dynamic_slice_in_dim(w, y * span, span, 1) for w in (w_query, w_key, w_value, w_out)
+    ]
+    packed, projections, outward = jnp.concatenate(pieces, 1), jnp.concatenate(pieces[:3], 1), pieces[3]
+    evens = list(range(n_agent - 2, 0, -2))
+    odds = list(range(n_agent - 1, 0, -2))
+    sources = list(zip(evens + [None], odds))
+    near = len(sources) - 2
+    fetched = [fetch(projections if n < near else packed, pair) for n, pair in enumerate(sources)]
+    fetched_out = [fetch(outward, pair) for pair in sources[:near]]
+    other_rows = across(features)
+    beside = swap(features)
+    diagonal = swap(other_rows)
+    swapped = [swap(value) for value in fetched]
+    swapped_out = [swap(value) for value in fetched_out]
+    normed, bounds = kernel(
+        norm_kernel,
+        [((steps, width), half), ((2, 8, LANES), jnp.int32)],
+        (tracks, norm_gain.reshape(1, width), features, beside, other_rows, diagonal),
+        smem=1,
+        flops=8 * steps * width,
+    )
+    shards = [packed] + [v for pair in zip(fetched, swapped) for v in pair]
+    head_flops = 4 * steps * steps * LANES
+    heads = [((steps, LANES), half)] * 2 + [((LANES, steps), half)]
+    exponentials = steps * steps * LANES // head_dim
+    attended_first, *late = kernel(
+        functools.partial(first_kernel, sources, head_dim),
+        [((LANES, steps), half)] + heads,
+        (bounds, normed, *shards),
+        scratch=[((width, 3 * span), half)] + heads,
+        flops=6 * steps * width * span + head_flops,
+        transcendentals=exponentials,
+    )
+    other_first = across(attended_first)
+    (attended_second,) = kernel(
+        functools.partial(second_kernel, head_dim),
+        [((LANES, steps), half)],
+        (bounds, *late),
+        flops=head_flops,
+        transcendentals=exponentials,
+    )
+    other_second = across(attended_second)
+    out_shards = [packed] + [
+        v
+        for pair in zip(fetched_out + fetched[near:], swapped_out + swapped[near:])
+        for v in pair
+    ]
+    kept, given, kept_weights, given_weights = kernel(
+        functools.partial(partial_kernel, sources),
+        [((span // 2, steps), full)] * 2 + [((LANES, span // 2), half)] * 2,
+        (*out_shards, attended_first, attended_second, other_first),
+        scratch=[((width, span), half)],
+        flops=2 * steps * width * span,
+    )
+    (given,) = kernel(
+        given_kernel,
+        [((span // 2, steps), half)],
+        (given, given_weights, other_second),
+        flops=steps * LANES * span,
+    )
+    received = swap(given)
+    (out,) = kernel(
+        final_kernel,
+        [((2, span // 2, steps), half)],
+        (kept, kept_weights, other_second, received),
+        flops=steps * LANES * span,
+    )
+    return out
+
+
 def solution(mesh):
     in_specs = (
         P("agent", "tm", None),
@@ -121,4 +387,11 @@
         P("agent", None),
     )
     out_specs = P("agent", "tm", None)
-    return jax.shard_map(body, mesh=mesh, in_specs=in_specs, out_specs=out_specs, check_vma=False)
+    n_tm, n_agent = mesh.shape["tm"], mesh.shape["agent"]
+
+    def local(features, *rest):
+        if fits(n_tm, n_agent, features):
+            return split_heads(n_tm, n_agent, features, *rest)
+        return body(features, *rest)
+
+    return jax.shard_map(local, mesh=mesh, in_specs=in_specs, out_specs=out_specs, check_vma=False)

time: 164 us -> 41.5 us (0.25)
  blocking collectives: 137 us -> 0 us
  starting transfers between devices: 0.01 us -> 23.1 us
  between operations: 13.5 us -> 0.15 us
  waiting for transfers between devices: 0.02 us -> 10.9 us
  Pallas kernels: 0 us -> 6.42 us
  matrix products: 6.41 us -> 0 us
  other arithmetic: 4.5 us -> 0.02 us
    all_gather x4 -> x0, blocking collectives: 128 us -> none  [the longest x1 33.5 us: body(): lax.all_gather(w_query, 'agent', axis=0, tiled=True)]
    ppermute x0 -> x18, starting transfers between devices: none -> 23.1 us  [the longest x6 11.3 us: fetch(): return lax.ppermute(value, ('tm', 'agent'), pairs)]
    ppermute x0 -> x18, waiting for transfers between devices: none -> 10.9 us  [the longest x6 5.37 us: fetch(): return lax.ppermute(value, ('tm', 'agent'), pairs)]
    all_to_all x1 -> x0, blocking collectives: 8.54 us -> none  [body(): lax.all_to_all(projected, 'tm', split_axis=1, concat_axis=2, tiled=True)]
    pallas_call x0 -> x6, Pallas kernels: none -> 6.42 us  [kernel(): pl.pallas_call(body, out_shape=[jax.ShapeDtypeStruct(shape, dtype) for sh...]
    dot_general x6 -> x0, matrix products: 6.41 us -> none  [the longest x3 3.98 us: project(): jnp.einsum('asd,de->ase', normed, weight, preferred_element_type=jnp.floa...]
    reduce_sum x2 -> x0, other arithmetic: 2.29 us -> none  [the longest x1 1.17 us: attend(): total = factor * total + jnp.sum(weights, axis=-1)]
    convert_element_type x2 -> x0, other arithmetic: 1.86 us -> none  [the longest x1 1.79 us: normalize(): return (values * lax.rsqrt(meansq + EPSILON) * gain).astype(jnp.bfloat16)]
  transfers between devices with their start and end apart: 1 -> 18, of which waited for: 0 -> 8; matrix products, arithmetic and copies ran while one was open for 2% -> 2% of each run, Pallas kernels for 0% -> 7%
where the time goes in v1:
time: 41.5 us; the launch traced here: 41.4 us
  starting transfers between devices  23.1 us (56%)
  waiting for transfers between devices  10.9 us (26%)
  Pallas kernels  6.42 us (15%)
  local copies, waits for them, and re-layouts  0.82 us (2%)
    ppermute x6, starting transfers between devices, fetch(): return lax.ppermute(value, ('tm', 'agent'), pairs)  11.3 us
    ppermute x9, starting transfers between devices, swap(): return lax.ppermute(value, 'tm', [(i, i ^ 1) for i in range(n_tm)])  7.07 us
    pallas_call x6, Pallas kernels, kernel(): pl.pallas_call(body, out_shape=[jax.ShapeDtypeStruct(shape, dtype) for sh...  6.42 us
    ppermute x6, waiting for transfers between devices, fetch(): return lax.ppermute(value, ('tm', 'agent'), pairs)  5.37 us
    ppermute x3, starting transfers between devices, across(): return lax.ppermute(value, 'tm', [(i, i ^ 2) for i in range(n_tm)])  4.73 us
    ppermute x9, waiting for transfers between devices, swap(): return lax.ppermute(value, 'tm', [(i, i ^ 1) for i in range(n_tm)])  2.89 us
    ppermute x3, waiting for transfers between devices, across(): return lax.ppermute(value, 'tm', [(i, i ^ 2) for i in range(n_tm)])  2.61 us
  transfers between devices with their start and end apart: 18, of which 8 were waited for; matrix products, arithmetic and copies ran while one was open for 2% of the time, Pallas kernels for 7%

profile of v1, /device:TPU:0, one launch (start us, length us, event | category | flops | bytes accessed | tf_op | source)
XLA Modules:
  0.0 41.4 jit_solution(7889554904867581593)
XLA Ops:
  0.0 0.5 %collective-permute-start.8 = (bf16[2,128,512]{2,1,0:T(8,128)(2,1)}, bf16[2,128,512]{2,1,0:T(8,128)(2,1)S(1)}, u32[]{:S(2)}, u32[]{:S(2)}) collective-permute-start(bf16[2,128,512]{2,1,0:T(8,128)(2,1)} %mine_ref.1), channel_id=1, source_target_pairs={{0,8},{8,0},{16,24},{24,16},{1,9},{9,1},{17,25},{25,17},{2,10},{10... | collective-permute-start | bytes 786440 | tf_op jit(solution)/shard_map/ppermute | solution.py:283
  0.5 2.6 %collective-permute-start.9 = (bf16[2,128,512]{2,1,0:T(8,128)(2,1)}, bf16[2,128,512]{2,1,0:T(8,128)(2,1)S(1)}, u32[]{:S(2)}, u32[]{:S(2)}) collective-permute-start(bf16[2,128,512]{2,1,0:T(8,128)(2,1)} %mine_ref.1), channel_id=1, source_target_pairs={{0,16},{8,24},{16,0},{24,8},{1,17},{9,25},{17,1},{25,9},{2,18},{10... | collective-permute-start | bytes 786440 | tf_op jit(solution)/shard_map/ppermute | solution.py:280
  3.1 0.8 %constant_dynamic-slice_fusion.1 = (bf16[64,256]{1,0:T(8,128)(2,1)S(1)}, bf16[64,256]{1,0:T(8,128)(2,1)S(1)}) fusion(bf16[64,512]{1,0:T(8,128)(2,1)} %param.11, s32[]{:T(128)S(6)} %select_n.12, bf16[64,512]{1,0:T(8,128)(2,1)} %param.10), kind=kLoop, calls=%fused_computation.3 | loop fusion | bytes 131076 | tf_op jit(solution)/shard_map/dynamic_slice | solution.py:309
  3.9 3.7 %collective-permute-start.11 = (bf16[64,768]{1,0:T(8,128)(2,1)S(1)}, bf16[64,768]{1,0:T(8,128)(2,1)S(1)}, u32[]{:S(2)}, u32[]{:S(2)}) collective-permute-start(bf16[64,768]{1,0:T(8,128)(2,1)S(1)} %pad_maximum_fusion.1), channel_id=1, source_target_pairs={{6,0},{7,1},{4,2},{5,3},{2,4},{3,5},{0,6},{1,7},{15,8},{14,9},{13,... | collective-permute-start | bytes 294920 | tf_op jit(solution)/shard_map/ppermute | solution.py:292
  7.6 2.6 %collective-permute-done.9.other_ref = bf16[2,128,512]{2,1,0:T(8,128)(2,1)S(1)} collective-permute-done((bf16[2,128,512]{2,1,0:T(8,128)(2,1)}, bf16[2,128,512]{2,1,0:T(8,128)(2,1)S(1)}, u32[]{:S(2)}, u32[]{:S(2)}) %collective-permute-start.9) | collective-permute-done | bytes 262176 | tf_op jit(solution)/shard_map/ppermute | solution.py:280
  10.2 1.9 %collective-permute-start.4 = (bf16[64,1024]{1,0:T(8,128)(2,1)S(1)}, bf16[64,1024]{1,0:T(8,128)(2,1)S(1)}, u32[]{:S(2)}, u32[]{:S(2)}) collective-permute-start(bf16[64,1024]{1,0:T(8,128)(2,1)S(1)} %pad_maximum_fusion.refs_0_), channel_id=1, source_target_pairs={{2,0},{3,1},{0,2},{1,3},{6,4},{7,5},{4,6},{5,7},{11,8},{10,9},{9,1... | collective-permute-start | bytes 393224 | tf_op jit(solution)/shard_map/ppermute | solution.py:292
  12.1 0.7 %collective-permute-start.6 = (bf16[64,1024]{1,0:T(8,128)(2,1)S(1)}, bf16[64,1024]{1,0:T(8,128)(2,1)S(1)}, u32[]{:S(2)}, u32[]{:S(2)}) collective-permute-start(bf16[64,1024]{1,0:T(8,128)(2,1)S(1)} %pad_maximum_fusion.refs_0_), channel_id=1, source_target_pairs={{9,8},{8,9},{11,10},{10,11},{13,12},{12,13},{15,14},{14,15},{25,24... | collective-permute-start | bytes 393224 | tf_op jit(solution)/shard_map/ppermute | solution.py:292
  12.8 2.7 %collective-permute-start.13 = (bf16[64,768]{1,0:T(8,128)(2,1)S(1)}, bf16[64,768]{1,0:T(8,128)(2,1)S(1)}, u32[]{:S(2)}, u32[]{:S(2)}) collective-permute-start(bf16[64,768]{1,0:T(8,128)(2,1)S(1)} %pad_maximum_fusion.1), channel_id=1, source_target_pairs={{4,0},{5,1},{6,2},{7,3},{0,4},{1,5},{2,6},{3,7},{13,8},{12,9},{15,... | collective-permute-start | bytes 294920 | tf_op jit(solution)/shard_map/ppermute | solution.py:292
  15.4 0.6 %collective-permute-done.4.refs_5_ = bf16[64,1024]{1,0:T(8,128)(2,1)S(1)} collective-permute-done((bf16[64,1024]{1,0:T(8,128)(2,1)S(1)}, bf16[64,1024]{1,0:T(8,128)(2,1)S(1)}, u32[]{:S(2)}, u32[]{:S(2)}) %collective-permute-start.4) | collective-permute-done | bytes 131104 | tf_op jit(solution)/shard_map/ppermute | solution.py:292
  16.0 2.7 %collective-permute-start.5 = (bf16[64,1024]{1,0:T(8,128)(2,1)S(1)}, bf16[64,1024]{1,0:T(8,128)(2,1)S(1)}, u32[]{:S(2)}, u32[]{:S(2)}) collective-permute-start(bf16[64,1024]{1,0:T(8,128)(2,1)S(1)} %collective-permute-done.4.refs_5_), channel_id=1, source_target_pairs={{0,8},{8,0},{16,24},{24,16},{1,9},{9,1},{17,25},{25,17},{2,10},{10... | collective-permute-start | bytes 393224 | tf_op jit(solution)/shard_map/ppermute | solution.py:283
  18.9 3.4 %collective-permute-start.12 = (bf16[64,768]{1,0:T(8,128)(2,1)S(1)}, bf16[64,768]{1,0:T(8,128)(2,1)S(1)}, u32[]{:S(2)}, u32[]{:S(2)}) collective-permute-start(bf16[64,768]{1,0:T(8,128)(2,1)S(1)} %collective-permute-done.11.refs_1_), channel_id=1, source_target_pairs={{0,8},{8,0},{16,24},{24,16},{1,9},{9,1},{17,25},{25,17},{2,10},{10... | collective-permute-start | bytes 294920 | tf_op jit(solution)/shard_map/ppermute | solution.py:283
  22.4 0.8 %shard_map.73 = (bf16[512,512]{1,0:T(8,128)(2,1)S(1)}, s32[2,8,128]{2,1,0:T(8,128)S(1)}) custom-call(s32[2,2]{1,0:T(2,128)S(1)} %copy-done.3, f32[1,512]{1,0:T(1,128)S(1)} %bitcast.1, bf16[2,128,512]{2,1,0:T(8,128)(2,1)S(1)} %copy-done.1, bf16[2,128,512]{2,1,0:T(8,128)(2,1)S(1)} %collective-permute-done.8.beside_ref, ...), custom_call_target="tpu_custom_call" | custom-call | flops 2097152 | bytes 1048576 | tf_op jit(solution)/shard_map/pallas_call | solution.py:296
  23.3 0.4 collective-permute-done.14.refs_4_
  23.6 2.4 %shard_map.74 = (bf16[128,512]{1,0:T(8,128)(2,1)S(1)}, bf16[512,128]{1,0:T(8,128)(2,1)S(1)}, bf16[512,128]{1,0:T(8,128)(2,1)S(1)}, bf16[128,512]{1,0:T(8,128)(2,1)S(1)}) custom-call(s32[2,8,128]{2,1,0:T(8,128)S(1)} %get-tuple-element.15.bounds_ref, bf16[512,512]{1,0:T(8,128)(2,1)S(1)} %get-tuple-element.16.normed_ref, ...), custom_call_target="tpu_custom_call" | custom-call | flops 536870912 | bytes 1048576 | tf_op jit(solution)/shard_map/pallas_call | solution.py:296
  26.0 1.6 %collective-permute-start.15 = (bf16[128,512]{1,0:T(8,128)(2,1)S(1)}, bf16[128,512]{1,0:T(8,128)(2,1)S(1)}, u32[]{:S(2)}, u32[]{:S(2)}) collective-permute-start(bf16[128,512]{1,0:T(8,128)(2,1)S(1)} %get-tuple-element.17.refs_9_), channel_id=1, source_target_pairs={{0,16},{8,24},{16,0},{24,8},{1,17},{9,25},{17,1},{25,9},{2,18},{10... | collective-permute-start | bytes 393224 | tf_op jit(solution)/shard_map/ppermute | solution.py:280
  27.6 1.7 %shard_map.75.refs_10_ = bf16[128,512]{1,0:T(8,128)(2,1)S(1)} custom-call(s32[2,8,128]{2,1,0:T(8,128)S(1)} %get-tuple-element.15.bounds_ref, bf16[512,128]{1,0:T(8,128)(2,1)S(1)} %get-tuple-element.18.queries, bf16[512,128]{1,0:T(8,128)(2,1)S(1)} %get-tuple-element.19.keys, bf16[128,512]{1,0:T(8,128)(2,1)S(1)} %get-tuple-element.20.values), custom_call_target="tpu_custom_call" | custom-call | flops 134217728 | bytes 1048576 | tf_op jit(solution)/shard_map/pallas_call | solution.py:296
  29.3 0.6 %collective-permute-start.16 = (bf16[128,512]{1,0:T(8,128)(2,1)S(1)}, bf16[128,512]{1,0:T(8,128)(2,1)S(1)}, u32[]{:S(2)}, u32[]{:S(2)}) collective-permute-start(bf16[128,512]{1,0:T(8,128)(2,1)S(1)} %shard_map.75.refs_10_), channel_id=1, source_target_pairs={{0,16},{8,24},{16,0},{24,8},{1,17},{9,25},{17,1},{25,9},{2,18},{10... | collective-permute-start | bytes 393224 | tf_op jit(solution)/shard_map/ppermute | solution.py:280
  29.9 2.4 %collective-permute-start = (bf16[64,256]{1,0:T(8,128)(2,1)S(1)}, bf16[64,256]{1,0:T(8,128)(2,1)S(1)}, u32[]{:S(2)}, u32[]{:S(2)}) collective-permute-start(bf16[64,256]{1,0:T(8,128)(2,1)S(1)} %constant_dynamic-slice_fusion), channel_id=1, source_target_pairs={{6,0},{7,1},{4,2},{5,3},{2,4},{3,5},{0,6},{1,7},{15,8},{14,9},{13,... | collective-permute-start | bytes 98312 | tf_op jit(solution)/shard_map/ppermute | solution.py:292
  32.3 3.3 %collective-permute-done.refs_1_ = bf16[64,256]{1,0:T(8,128)(2,1)S(1)} collective-permute-done((bf16[64,256]{1,0:T(8,128)(2,1)S(1)}, bf16[64,256]{1,0:T(8,128)(2,1)S(1)}, u32[]{:S(2)}, u32[]{:S(2)}) %collective-permute-start) | collective-permute-done | bytes 32800 | tf_op jit(solution)/shard_map/ppermute | solution.py:292
  35.6 1.5 %collective-permute-done.2.refs_3_ = bf16[64,256]{1,0:T(8,128)(2,1)S(1)} collective-permute-done((bf16[64,256]{1,0:T(8,128)(2,1)S(1)}, bf16[64,256]{1,0:T(8,128)(2,1)S(1)}, u32[]{:S(2)}, u32[]{:S(2)}) %collective-permute-start.2) | collective-permute-done | bytes 32800 | tf_op jit(solution)/shard_map/ppermute | solution.py:292
  37.1 1.2 %collective-permute-done.3.refs_4_ = bf16[64,256]{1,0:T(8,128)(2,1)S(1)} collective-permute-done((bf16[64,256]{1,0:T(8,128)(2,1)S(1)}, bf16[64,256]{1,0:T(8,128)(2,1)S(1)}, u32[]{:S(2)}, u32[]{:S(2)}) %collective-permute-start.3) | collective-permute-done | bytes 32800 | tf_op jit(solution)/shard_map/ppermute | solution.py:283
  38.3 0.5 %shard_map.76 = (f32[128,512]{1,0:T(8,128)S(1)}, f32[128,512]{1,0:T(8,128)S(1)}, bf16[128,128]{1,0:T(8,128)(2,1)S(1)}, bf16[128,128]{1,0:T(8,128)(2,1)S(1)}) custom-call(bf16[64,1024]{1,0:T(8,128)(2,1)S(1)} %pad_maximum_fusion.refs_0_, bf16[64,256]{1,0:T(8,128)(2,1)S(1)} %collective-permute-done.refs_1_, bf16[64,256]{1,0:T(8,128)(2,1)S(1)} %collective-permute-done.1.refs_2_, ...), custom_call_target="tpu_custom_call" | custom-call | flops 134217728 | bytes 1048576 | tf_op jit(solution)/shard_map/pallas_call | solution.py:296
  39.3 1.2 %collective-permute-done.17.received_ref = bf16[128,512]{1,0:T(8,128)(2,1)S(1)} collective-permute-done((bf16[128,512]{1,0:T(8,128)(2,1)S(1)}, bf16[128,512]{1,0:T(8,128)(2,1)S(1)}, u32[]{:S(2)}, u32[]{:S(2)}) %collective-permute-start.17) | collective-permute-done | bytes 131104 | tf_op jit(solution)/shard_map/ppermute | solution.py:283
  40.4 0.9 %shard_map.78 = bf16[2,128,512]{2,1,0:T(8,128)(2,1)} custom-call(f32[128,512]{1,0:T(8,128)S(1)} %get-tuple-element.21.partial_ref, bf16[128,128]{1,0:T(8,128)(2,1)S(1)} %get-tuple-element.22.weights_ref, bf16[128,512]{1,0:T(8,128)(2,1)S(1)} %collective-permute-done.16.value_ref, bf16[128,512]{1,0:T(8,128)(2,1)S(1)} %collective-permute-done.17.received_ref), custom_call_target="tpu_custom_call" | custom-call | flops 16777216 | bytes 1048576 | tf_op jit(solution)/shard_map/pallas_call | solution.py:296
  (33 shorter events, 0.9 us)
Async XLA Ops:
  0.0 3.9 %copy-start = (bf16[64,512]{1,0:T(8,128)(2,1)S(1)}, bf16[64,512]{1,0:T(8,128)(2,1)}, u32[]{:S(2)}) copy-start(bf16[64,512]{1,0:T(8,128)(2,1)} %param.9) | copy-start | bytes 196612
  0.0 22.3 %collective-permute-start.8 = (bf16[2,128,512]{2,1,0:T(8,128)(2,1)}, bf16[2,128,512]{2,1,0:T(8,128)(2,1)S(1)}, u32[]{:S(2)}, u32[]{:S(2)}) collective-permute-start(bf16[2,128,512]{2,1,0:T(8,128)(2,1)} %mine_ref.1), channel_id=1, source_target_pairs={{0,8},{8,0},{16,24},{24,16},{1,9},{9,1},{17,25},{25,17},{2,10},{10... | collective-permute-start | bytes 786440 | tf_op jit(solution)/shard_map/ppermute | solution.py:283
  0.5 9.7 %collective-permute-start.9 = (bf16[2,128,512]{2,1,0:T(8,128)(2,1)}, bf16[2,128,512]{2,1,0:T(8,128)(2,1)S(1)}, u32[]{:S(2)}, u32[]{:S(2)}) collective-permute-start(bf16[2,128,512]{2,1,0:T(8,128)(2,1)} %mine_ref.1), channel_id=1, source_target_pairs={{0,16},{8,24},{16,0},{24,8},{1,17},{9,25},{17,1},{25,9},{2,18},{10... | collective-permute-start | bytes 786440 | tf_op jit(solution)/shard_map/ppermute | solution.py:280
  3.9 3.7 %copy-start.4 = (bf16[64,512]{1,0:T(8,128)(2,1)S(1)}, bf16[64,512]{1,0:T(8,128)(2,1)}, u32[]{:S(2)}) copy-start(bf16[64,512]{1,0:T(8,128)(2,1)} %param.12) | copy-start | bytes 196612
  3.9 18.5 %copy-start.1 = (bf16[2,128,512]{2,1,0:T(8,128)(2,1)S(1)}, bf16[2,128,512]{2,1,0:T(8,128)(2,1)}, u32[]{:S(2)}) copy-start(bf16[2,128,512]{2,1,0:T(8,128)(2,1)} %mine_ref.1) | copy-start | bytes 786436
  3.9 8.8 %collective-permute-start.11 = (bf16[64,768]{1,0:T(8,128)(2,1)S(1)}, bf16[64,768]{1,0:T(8,128)(2,1)S(1)}, u32[]{:S(2)}, u32[]{:S(2)}) collective-permute-start(bf16[64,768]{1,0:T(8,128)(2,1)S(1)} %pad_maximum_fusion.1), channel_id=1, source_target_pairs={{6,0},{7,1},{4,2},{5,3},{2,4},{3,5},{0,6},{1,7},{15,8},{14,9},{13,... | collective-permute-start | bytes 294920 | tf_op jit(solution)/shard_map/ppermute | solution.py:292
  10.2 12.1 %collective-permute-start.10 = (bf16[2,128,512]{2,1,0:T(8,128)(2,1)S(1)}, bf16[2,128,512]{2,1,0:T(8,128)(2,1)S(1)}, u32[]{:S(2)}, u32[]{:S(2)}) collective-permute-start(bf16[2,128,512]{2,1,0:T(8,128)(2,1)S(1)} %collective-permute-done.9.other_ref), channel_id=1, source_target_pairs={{0,8},{8,0},{16,24},{24,16},{1,9},{9,1},{17,25},{25,17},{2,10},{10... | collective-permute-start | bytes 786440 | tf_op jit(solution)/shard_map/ppermute | solution.py:283
  10.2 12.2 %copy-start.2 = (f32[512]{0:T(512)S(1)}, f32[512]{0:T(512)}, u32[]{:S(2)}) copy-start(f32[512]{0:T(512)} %param.8) | copy-start | bytes 6148
  10.2 12.1 %copy-start.3 = (s32[2,2]{1,0:T(2,128)S(1)}, s32[2,2]{1,0:T(2,128)}, u32[]{:S(2)}) copy-start(s32[2,2]{1,0:T(2,128)} %tracks_ref.1) | copy-start | bytes 52
  10.2 5.7 %collective-permute-start.4 = (bf16[64,1024]{1,0:T(8,128)(2,1)S(1)}, bf16[64,1024]{1,0:T(8,128)(2,1)S(1)}, u32[]{:S(2)}, u32[]{:S(2)}) collective-permute-start(bf16[64,1024]{1,0:T(8,128)(2,1)S(1)} %pad_maximum_fusion.refs_0_), channel_id=1, source_target_pairs={{2,0},{3,1},{0,2},{1,3},{6,4},{7,5},{4,6},{5,7},{11,8},{10,9},{9,1... | collective-permute-start | bytes 393224 | tf_op jit(solution)/shard_map/ppermute | solution.py:292
  12.1 6.6 %collective-permute-start.6 = (bf16[64,1024]{1,0:T(8,128)(2,1)S(1)}, bf16[64,1024]{1,0:T(8,128)(2,1)S(1)}, u32[]{:S(2)}, u32[]{:S(2)}) collective-permute-start(bf16[64,1024]{1,0:T(8,128)(2,1)S(1)} %pad_maximum_fusion.refs_0_), channel_id=1, source_target_pairs={{9,8},{8,9},{11,10},{10,11},{13,12},{12,13},{15,14},{14,15},{25,24... | collective-permute-start | bytes 393224 | tf_op jit(solution)/shard_map/ppermute | solution.py:292
  12.8 6.2 %collective-permute-start.13 = (bf16[64,768]{1,0:T(8,128)(2,1)S(1)}, bf16[64,768]{1,0:T(8,128)(2,1)S(1)}, u32[]{:S(2)}, u32[]{:S(2)}) collective-permute-start(bf16[64,768]{1,0:T(8,128)(2,1)S(1)} %pad_maximum_fusion.1), channel_id=1, source_target_pairs={{4,0},{5,1},{6,2},{7,3},{0,4},{1,5},{2,6},{3,7},{13,8},{12,9},{15,... | collective-permute-start | bytes 294920 | tf_op jit(solution)/shard_map/ppermute | solution.py:292
  16.0 7.7 %collective-permute-start.5 = (bf16[64,1024]{1,0:T(8,128)(2,1)S(1)}, bf16[64,1024]{1,0:T(8,128)(2,1)S(1)}, u32[]{:S(2)}, u32[]{:S(2)}) collective-permute-start(bf16[64,1024]{1,0:T(8,128)(2,1)S(1)} %collective-permute-done.4.refs_5_), channel_id=1, source_target_pairs={{0,8},{8,0},{16,24},{24,16},{1,9},{9,1},{17,25},{25,17},{2,10},{10... | collective-permute-start | bytes 393224 | tf_op jit(solution)/shard_map/ppermute | solution.py:283
  18.7 4.9 %collective-permute-start.7 = (bf16[64,1024]{1,0:T(8,128)(2,1)S(1)}, bf16[64,1024]{1,0:T(8,128)(2,1)S(1)}, u32[]{:S(2)}, u32[]{:S(2)}) collective-permute-start(bf16[64,1024]{1,0:T(8,128)(2,1)S(1)} %collective-permute-done.6.refs_7_), channel_id=1, source_target_pairs={{0,8},{8,0},{16,24},{24,16},{1,9},{9,1},{17,25},{25,17},{2,10},{10... | collective-permute-start | bytes 393224 | tf_op jit(solution)/shard_map/ppermute | solution.py:283
  18.9 4.3 %collective-permute-start.12 = (bf16[64,768]{1,0:T(8,128)(2,1)S(1)}, bf16[64,768]{1,0:T(8,128)(2,1)S(1)}, u32[]{:S(2)}, u32[]{:S(2)}) collective-permute-start(bf16[64,768]{1,0:T(8,128)(2,1)S(1)} %collective-permute-done.11.refs_1_), channel_id=1, source_target_pairs={{0,8},{8,0},{16,24},{24,16},{1,9},{9,1},{17,25},{25,17},{2,10},{10... | collective-permute-start | bytes 294920 | tf_op jit(solution)/shard_map/ppermute | solution.py:283
  22.3 1.3 %collective-permute-start.14 = (bf16[64,768]{1,0:T(8,128)(2,1)S(1)}, bf16[64,768]{1,0:T(8,128)(2,1)S(1)}, u32[]{:S(2)}, u32[]{:S(2)}) collective-permute-start(bf16[64,768]{1,0:T(8,128)(2,1)S(1)} %collective-permute-done.13.refs_3_), channel_id=1, source_target_pairs={{0,8},{8,0},{16,24},{24,16},{1,9},{9,1},{17,25},{25,17},{2,10},{10... | collective-permute-start | bytes 294920 | tf_op jit(solution)/shard_map/ppermute | solution.py:283
  26.0 12.4 %collective-permute-start.15 = (bf16[128,512]{1,0:T(8,128)(2,1)S(1)}, bf16[128,512]{1,0:T(8,128)(2,1)S(1)}, u32[]{:S(2)}, u32[]{:S(2)}) collective-permute-start(bf16[128,512]{1,0:T(8,128)(2,1)S(1)} %get-tuple-element.17.refs_9_), channel_id=1, source_target_pairs={{0,16},{8,24},{16,0},{24,8},{1,17},{9,25},{17,1},{25,9},{2,18},{10... | collective-permute-start | bytes 393224 | tf_op jit(solution)/shard_map/ppermute | solution.py:280
  29.3 9.5 %collective-permute-start.16 = (bf16[128,512]{1,0:T(8,128)(2,1)S(1)}, bf16[128,512]{1,0:T(8,128)(2,1)S(1)}, u32[]{:S(2)}, u32[]{:S(2)}) collective-permute-start(bf16[128,512]{1,0:T(8,128)(2,1)S(1)} %shard_map.75.refs_10_), channel_id=1, source_target_pairs={{0,16},{8,24},{16,0},{24,8},{1,17},{9,25},{17,1},{25,9},{2,18},{10... | collective-permute-start | bytes 393224 | tf_op jit(solution)/shard_map/ppermute | solution.py:280
  29.9 5.7 %collective-permute-start = (bf16[64,256]{1,0:T(8,128)(2,1)S(1)}, bf16[64,256]{1,0:T(8,128)(2,1)S(1)}, u32[]{:S(2)}, u32[]{:S(2)}) collective-permute-start(bf16[64,256]{1,0:T(8,128)(2,1)S(1)} %constant_dynamic-slice_fusion), channel_id=1, source_target_pairs={{6,0},{7,1},{4,2},{5,3},{2,4},{3,5},{0,6},{1,7},{15,8},{14,9},{13,... | collective-permute-start | bytes 98312 | tf_op jit(solution)/shard_map/ppermute | solution.py:292
  32.3 4.8 %collective-permute-start.2 = (bf16[64,256]{1,0:T(8,128)(2,1)S(1)}, bf16[64,256]{1,0:T(8,128)(2,1)S(1)}, u32[]{:S(2)}, u32[]{:S(2)}) collective-permute-start(bf16[64,256]{1,0:T(8,128)(2,1)S(1)} %constant_dynamic-slice_fusion), channel_id=1, source_target_pairs={{4,0},{5,1},{6,2},{7,3},{0,4},{1,5},{2,6},{3,7},{13,8},{12,9},{15,... | collective-permute-start | bytes 98312 | tf_op jit(solution)/shard_map/ppermute | solution.py:292
  35.6 1.6 %collective-permute-start.1 = (bf16[64,256]{1,0:T(8,128)(2,1)S(1)}, bf16[64,256]{1,0:T(8,128)(2,1)S(1)}, u32[]{:S(2)}, u32[]{:S(2)}) collective-permute-start(bf16[64,256]{1,0:T(8,128)(2,1)S(1)} %collective-permute-done.refs_1_), channel_id=1, source_target_pairs={{0,8},{8,0},{16,24},{24,16},{1,9},{9,1},{17,25},{25,17},{2,10},{10... | collective-permute-start | bytes 98312 | tf_op jit(solution)/shard_map/ppermute | solution.py:283
  37.1 1.2 %collective-permute-start.3 = (bf16[64,256]{1,0:T(8,128)(2,1)S(1)}, bf16[64,256]{1,0:T(8,128)(2,1)S(1)}, u32[]{:S(2)}, u32[]{:S(2)}) collective-permute-start(bf16[64,256]{1,0:T(8,128)(2,1)S(1)} %collective-permute-done.2.refs_3_), channel_id=1, source_target_pairs={{0,8},{8,0},{16,24},{24,16},{1,9},{9,1},{17,25},{25,17},{2,10},{10... | collective-permute-start | bytes 98312 | tf_op jit(solution)/shard_map/ppermute | solution.py:283
  39.0 1.4 %collective-permute-start.17 = (bf16[128,512]{1,0:T(8,128)(2,1)S(1)}, bf16[128,512]{1,0:T(8,128)(2,1)S(1)}, u32[]{:S(2)}, u32[]{:S(2)}) collective-permute-start(bf16[128,512]{1,0:T(8,128)(2,1)S(1)} %shard_map.77), channel_id=1, source_target_pairs={{0,8},{8,0},{16,24},{24,16},{1,9},{9,1},{17,25},{25,17},{2,10},{10... | collective-permute-start | bytes 393224 | tf_op jit(solution)/shard_map/ppermute | solution.py:283

commit v2 on v1

--- a/solution.py
+++ b/solution.py
@@ -146,31 +146,31 @@
         key_pos = lax.broadcasted_iota(jnp.int32, (reach, block), 0)
         query_pos = j * block + lax.broadcasted_iota(jnp.int32, (reach, block), 1)
         allowed = (key_pos >= start) & (key_pos <= query_pos)
+        allowed = jnp.concatenate([allowed] * (span // head_dim), axis=1)
         column = j * block + lax.broadcasted_iota(jnp.int32, (1, block), 1)
         live = (column >= start) & (column < end)
         query_block = queries[pl.ds(j * block, block), :]
+        one = [
+            jnp.where((lane >= low) & (lane < low + head_dim), query_block, jnp.zeros_like(query_block))
+            for low in range(0, span, head_dim)
+        ]
+        scores = lax.dot_general(
+            keys[pl.ds(0, reach), :],
+            jnp.concatenate(one, axis=0),
+            (((1,), (1,)), ((), ())),
+            preferred_element_type=jnp.float32,
+        )
+        scores = jnp.where(allowed, scores * scale, NEGATIVE)
+        highest = jnp.max(scores, axis=0, keepdims=True)
+        weight = jnp.exp(scores - highest)
+        total = jnp.sum(weight, axis=0, keepdims=True)
+        summed = jnp.dot(
+            values[:, pl.ds(0, reach)], weight.astype(jnp.bfloat16), preferred_element_type=jnp.float32
+        )
         for h in range(span // head_dim):
-            mine = (lane >= h * head_dim) & (lane < (h + 1) * head_dim)
-            one = jnp.where(mine, query_block, jnp.zeros_like(query_block))
-            scores = lax.dot_general(
-                keys[pl.ds(0, reach), :],
-                one,
-                (((1,), (1,)), ((), ())),
-                preferred_element_type=jnp.float32,
-            )
-            scores = jnp.where(allowed, scores * scale, NEGATIVE)
-            highest = jnp.max(scores, axis=0, keepdims=True)
-            weight = jnp.exp(scores - highest)
-            total = jnp.sum(weight, axis=0, keepdims=True)
-            summed = jnp.dot(
-                values[pl.ds(h * head_dim, head_dim), pl.ds(0, reach)],
-                weight.astype(jnp.bfloat16),
-                preferred_element_type=jnp.float32,
-            )
-            result = jnp.where(live, summed / total, 0.0)
-            out_ref[pl.ds(h * head_dim, head_dim), pl.ds(j * block, block)] = result.astype(
-                jnp.bfloat16
-            )
+            rows, lanes = slice(h * head_dim, (h + 1) * head_dim), slice(h * block, (h + 1) * block)
+            result = jnp.where(live, summed[rows, lanes] / total[:, lanes], 0.0)
+            out_ref[rows, pl.ds(j * block, block)] = result.astype(jnp.bfloat16)
 
 
 def place(sources, refs, target, begin, columns):

time: 41.5 us -> 40.5 us (0.976)
  Pallas kernels: 6.42 us -> 5.37 us
    pallas_call x6, Pallas kernels: 6.42 us -> 5.37 us  [kernel(): pl.pallas_call(body, out_shape=[jax.ShapeDtypeStruct(shape, dtype) for sh...]
  transfers between devices with their start and end apart: 18 -> 18, of which waited for: 8 -> 8; matrix products, arithmetic and copies ran while one was open for 2% -> 2% of each run, Pallas kernels for 7% -> 6%
where the time goes in v2:
time: 40.5 us; the launch traced here: 40.3 us
  starting transfers between devices  23.1 us (57%)
  waiting for transfers between devices  10.9 us (27%)
  Pallas kernels  5.37 us (13%)
  local copies, waits for them, and re-layouts  0.82 us (2%)
    ppermute x6, starting transfers between devices, fetch(): return lax.ppermute(value, ('tm', 'agent'), pairs)  11.3 us
    ppermute x9, starting transfers between devices, swap(): return lax.ppermute(value, 'tm', [(i, i ^ 1) for i in range(n_tm)])  7.09 us
    ppermute x6, waiting for transfers between devices, fetch(): return lax.ppermute(value, ('tm', 'agent'), pairs)  5.37 us
    pallas_call x6, Pallas kernels, kernel(): pl.pallas_call(body, out_shape=[jax.ShapeDtypeStruct(shape, dtype) for sh...  5.37 us
    ppermute x3, starting transfers between devices, across(): return lax.ppermute(value, 'tm', [(i, i ^ 2) for i in range(n_tm)])  4.74 us
    ppermute x9, waiting for transfers between devices, swap(): return lax.ppermute(value, 'tm', [(i, i ^ 1) for i in range(n_tm)])  2.87 us
    ppermute x3, waiting for transfers between devices, across(): return lax.ppermute(value, 'tm', [(i, i ^ 2) for i in range(n_tm)])  2.61 us
  transfers between devices with their start and end apart: 18, of which 8 were waited for; matrix products, arithmetic and copies ran while one was open for 2% of the time, Pallas kernels for 6%

profile of v2, /device:TPU:0, one launch (start us, length us, event | category | flops | bytes accessed | tf_op | source)
XLA Modules:
  0.0 40.3 jit_solution(6507124251258895829)
XLA Ops:
  0.0 0.5 %collective-permute-start.8 = (bf16[2,128,512]{2,1,0:T(8,128)(2,1)}, bf16[2,128,512]{2,1,0:T(8,128)(2,1)S(1)}, u32[]{:S(2)}, u32[]{:S(2)}) collective-permute-start(bf16[2,128,512]{2,1,0:T(8,128)(2,1)} %mine_ref.1), channel_id=1, source_target_pairs={{0,8},{8,0},{16,24},{24,16},{1,9},{9,1},{17,25},{25,17},{2,10},{10... | collective-permute-start | bytes 786440 | tf_op jit(solution)/shard_map/ppermute | solution.py:283
  0.5 2.6 %collective-permute-start.9 = (bf16[2,128,512]{2,1,0:T(8,128)(2,1)}, bf16[2,128,512]{2,1,0:T(8,128)(2,1)S(1)}, u32[]{:S(2)}, u32[]{:S(2)}) collective-permute-start(bf16[2,128,512]{2,1,0:T(8,128)(2,1)} %mine_ref.1), channel_id=1, source_target_pairs={{0,16},{8,24},{16,0},{24,8},{1,17},{9,25},{17,1},{25,9},{2,18},{10... | collective-permute-start | bytes 786440 | tf_op jit(solution)/shard_map/ppermute | solution.py:280
  3.1 0.8 %constant_dynamic-slice_fusion.1 = (bf16[64,256]{1,0:T(8,128)(2,1)S(1)}, bf16[64,256]{1,0:T(8,128)(2,1)S(1)}) fusion(bf16[64,512]{1,0:T(8,128)(2,1)} %param.11, s32[]{:T(128)S(6)} %select_n.12, bf16[64,512]{1,0:T(8,128)(2,1)} %param.10), kind=kLoop, calls=%fused_computation.3 | loop fusion | bytes 131076 | tf_op jit(solution)/shard_map/dynamic_slice | solution.py:309
  3.9 3.7 %collective-permute-start.11 = (bf16[64,768]{1,0:T(8,128)(2,1)S(1)}, bf16[64,768]{1,0:T(8,128)(2,1)S(1)}, u32[]{:S(2)}, u32[]{:S(2)}) collective-permute-start(bf16[64,768]{1,0:T(8,128)(2,1)S(1)} %pad_maximum_fusion.1), channel_id=1, source_target_pairs={{6,0},{7,1},{4,2},{5,3},{2,4},{3,5},{0,6},{1,7},{15,8},{14,9},{13,... | collective-permute-start | bytes 294920 | tf_op jit(solution)/shard_map/ppermute | solution.py:292
  7.6 2.6 %collective-permute-done.9.other_ref = bf16[2,128,512]{2,1,0:T(8,128)(2,1)S(1)} collective-permute-done((bf16[2,128,512]{2,1,0:T(8,128)(2,1)}, bf16[2,128,512]{2,1,0:T(8,128)(2,1)S(1)}, u32[]{:S(2)}, u32[]{:S(2)}) %collective-permute-start.9) | collective-permute-done | bytes 262176 | tf_op jit(solution)/shard_map/ppermute | solution.py:280
  10.2 1.9 %collective-permute-start.4 = (bf16[64,1024]{1,0:T(8,128)(2,1)S(1)}, bf16[64,1024]{1,0:T(8,128)(2,1)S(1)}, u32[]{:S(2)}, u32[]{:S(2)}) collective-permute-start(bf16[64,1024]{1,0:T(8,128)(2,1)S(1)} %pad_maximum_fusion.refs_0_), channel_id=1, source_target_pairs={{2,0},{3,1},{0,2},{1,3},{6,4},{7,5},{4,6},{5,7},{11,8},{10,9},{9,1... | collective-permute-start | bytes 393224 | tf_op jit(solution)/shard_map/ppermute | solution.py:292
  12.1 0.7 %collective-permute-start.6 = (bf16[64,1024]{1,0:T(8,128)(2,1)S(1)}, bf16[64,1024]{1,0:T(8,128)(2,1)S(1)}, u32[]{:S(2)}, u32[]{:S(2)}) collective-permute-start(bf16[64,1024]{1,0:T(8,128)(2,1)S(1)} %pad_maximum_fusion.refs_0_), channel_id=1, source_target_pairs={{9,8},{8,9},{11,10},{10,11},{13,12},{12,13},{15,14},{14,15},{25,24... | collective-permute-start | bytes 393224 | tf_op jit(solution)/shard_map/ppermute | solution.py:292
  12.8 2.7 %collective-permute-start.13 = (bf16[64,768]{1,0:T(8,128)(2,1)S(1)}, bf16[64,768]{1,0:T(8,128)(2,1)S(1)}, u32[]{:S(2)}, u32[]{:S(2)}) collective-permute-start(bf16[64,768]{1,0:T(8,128)(2,1)S(1)} %pad_maximum_fusion.1), channel_id=1, source_target_pairs={{4,0},{5,1},{6,2},{7,3},{0,4},{1,5},{2,6},{3,7},{13,8},{12,9},{15,... | collective-permute-start | bytes 294920 | tf_op jit(solution)/shard_map/ppermute | solution.py:292
  15.4 0.6 %collective-permute-done.4.refs_5_ = bf16[64,1024]{1,0:T(8,128)(2,1)S(1)} collective-permute-done((bf16[64,1024]{1,0:T(8,128)(2,1)S(1)}, bf16[64,1024]{1,0:T(8,128)(2,1)S(1)}, u32[]{:S(2)}, u32[]{:S(2)}) %collective-permute-start.4) | collective-permute-done | bytes 131104 | tf_op jit(solution)/shard_map/ppermute | solution.py:292
  16.0 2.7 %collective-permute-start.5 = (bf16[64,1024]{1,0:T(8,128)(2,1)S(1)}, bf16[64,1024]{1,0:T(8,128)(2,1)S(1)}, u32[]{:S(2)}, u32[]{:S(2)}) collective-permute-start(bf16[64,1024]{1,0:T(8,128)(2,1)S(1)} %collective-permute-done.4.refs_5_), channel_id=1, source_target_pairs={{0,8},{8,0},{16,24},{24,16},{1,9},{9,1},{17,25},{25,17},{2,10},{10... | collective-permute-start | bytes 393224 | tf_op jit(solution)/shard_map/ppermute | solution.py:283
  18.9 3.4 %collective-permute-start.12 = (bf16[64,768]{1,0:T(8,128)(2,1)S(1)}, bf16[64,768]{1,0:T(8,128)(2,1)S(1)}, u32[]{:S(2)}, u32[]{:S(2)}) collective-permute-start(bf16[64,768]{1,0:T(8,128)(2,1)S(1)} %collective-permute-done.11.refs_1_), channel_id=1, source_target_pairs={{0,8},{8,0},{16,24},{24,16},{1,9},{9,1},{17,25},{25,17},{2,10},{10... | collective-permute-start | bytes 294920 | tf_op jit(solution)/shard_map/ppermute | solution.py:283
  22.4 0.8 %shard_map.73 = (bf16[512,512]{1,0:T(8,128)(2,1)S(1)}, s32[2,8,128]{2,1,0:T(8,128)S(1)}) custom-call(s32[2,2]{1,0:T(2,128)S(1)} %copy-done.3, f32[1,512]{1,0:T(1,128)S(1)} %bitcast.1, bf16[2,128,512]{2,1,0:T(8,128)(2,1)S(1)} %copy-done.1, bf16[2,128,512]{2,1,0:T(8,128)(2,1)S(1)} %collective-permute-done.8.beside_ref, ...), custom_call_target="tpu_custom_call" | custom-call | flops 2097152 | bytes 1048576 | tf_op jit(solution)/shard_map/pallas_call | solution.py:296
  23.3 0.4 collective-permute-done.14.refs_4_
  23.6 1.8 %shard_map.74 = (bf16[128,512]{1,0:T(8,128)(2,1)S(1)}, bf16[512,128]{1,0:T(8,128)(2,1)S(1)}, bf16[512,128]{1,0:T(8,128)(2,1)S(1)}, bf16[128,512]{1,0:T(8,128)(2,1)S(1)}) custom-call(s32[2,8,128]{2,1,0:T(8,128)S(1)} %get-tuple-element.15.bounds_ref, bf16[512,512]{1,0:T(8,128)(2,1)S(1)} %get-tuple-element.16.normed_ref, ...), custom_call_target="tpu_custom_call" | custom-call | flops 536870912 | bytes 1048576 | tf_op jit(solution)/shard_map/pallas_call | solution.py:296
  25.4 1.6 %collective-permute-start.15 = (bf16[128,512]{1,0:T(8,128)(2,1)S(1)}, bf16[128,512]{1,0:T(8,128)(2,1)S(1)}, u32[]{:S(2)}, u32[]{:S(2)}) collective-permute-start(bf16[128,512]{1,0:T(8,128)(2,1)S(1)} %get-tuple-element.17.refs_9_), channel_id=1, source_target_pairs={{0,16},{8,24},{16,0},{24,8},{1,17},{9,25},{17,1},{25,9},{2,18},{10... | collective-permute-start | bytes 393224 | tf_op jit(solution)/shard_map/ppermute | solution.py:280
  27.0 1.3 %shard_map.75.refs_10_ = bf16[128,512]{1,0:T(8,128)(2,1)S(1)} custom-call(s32[2,8,128]{2,1,0:T(8,128)S(1)} %get-tuple-element.15.bounds_ref, bf16[512,128]{1,0:T(8,128)(2,1)S(1)} %get-tuple-element.18.queries, bf16[512,128]{1,0:T(8,128)(2,1)S(1)} %get-tuple-element.19.keys, bf16[128,512]{1,0:T(8,128)(2,1)S(1)} %get-tuple-element.20.values), custom_call_target="tpu_custom_call" | custom-call | flops 134217728 | bytes 1048576 | tf_op jit(solution)/shard_map/pallas_call | solution.py:296
  28.3 0.6 %collective-permute-start.16 = (bf16[128,512]{1,0:T(8,128)(2,1)S(1)}, bf16[128,512]{1,0:T(8,128)(2,1)S(1)}, u32[]{:S(2)}, u32[]{:S(2)}) collective-permute-start(bf16[128,512]{1,0:T(8,128)(2,1)S(1)} %shard_map.75.refs_10_), channel_id=1, source_target_pairs={{0,16},{8,24},{16,0},{24,8},{1,17},{9,25},{17,1},{25,9},{2,18},{10... | collective-permute-start | bytes 393224 | tf_op jit(solution)/shard_map/ppermute | solution.py:280
  28.8 2.4 %collective-permute-start = (bf16[64,256]{1,0:T(8,128)(2,1)S(1)}, bf16[64,256]{1,0:T(8,128)(2,1)S(1)}, u32[]{:S(2)}, u32[]{:S(2)}) collective-permute-start(bf16[64,256]{1,0:T(8,128)(2,1)S(1)} %constant_dynamic-slice_fusion), channel_id=1, source_target_pairs={{6,0},{7,1},{4,2},{5,3},{2,4},{3,5},{0,6},{1,7},{15,8},{14,9},{13,... | collective-permute-start | bytes 98312 | tf_op jit(solution)/shard_map/ppermute | solution.py:292
  31.3 3.3 %collective-permute-done.refs_1_ = bf16[64,256]{1,0:T(8,128)(2,1)S(1)} collective-permute-done((bf16[64,256]{1,0:T(8,128)(2,1)S(1)}, bf16[64,256]{1,0:T(8,128)(2,1)S(1)}, u32[]{:S(2)}, u32[]{:S(2)}) %collective-permute-start) | collective-permute-done | bytes 32800 | tf_op jit(solution)/shard_map/ppermute | solution.py:292
  34.6 1.5 %collective-permute-done.2.refs_3_ = bf16[64,256]{1,0:T(8,128)(2,1)S(1)} collective-permute-done((bf16[64,256]{1,0:T(8,128)(2,1)S(1)}, bf16[64,256]{1,0:T(8,128)(2,1)S(1)}, u32[]{:S(2)}, u32[]{:S(2)}) %collective-permute-start.2) | collective-permute-done | bytes 32800 | tf_op jit(solution)/shard_map/ppermute | solution.py:292
  36.1 1.2 %collective-permute-done.3.refs_4_ = bf16[64,256]{1,0:T(8,128)(2,1)S(1)} collective-permute-done((bf16[64,256]{1,0:T(8,128)(2,1)S(1)}, bf16[64,256]{1,0:T(8,128)(2,1)S(1)}, u32[]{:S(2)}, u32[]{:S(2)}) %collective-permute-start.3) | collective-permute-done | bytes 32800 | tf_op jit(solution)/shard_map/ppermute | solution.py:283
  37.3 0.4 %shard_map.76 = (f32[128,512]{1,0:T(8,128)S(1)}, f32[128,512]{1,0:T(8,128)S(1)}, bf16[128,128]{1,0:T(8,128)(2,1)S(1)}, bf16[128,128]{1,0:T(8,128)(2,1)S(1)}) custom-call(bf16[64,1024]{1,0:T(8,128)(2,1)S(1)} %pad_maximum_fusion.refs_0_, bf16[64,256]{1,0:T(8,128)(2,1)S(1)} %collective-permute-done.refs_1_, bf16[64,256]{1,0:T(8,128)(2,1)S(1)} %collective-permute-done.1.refs_2_, ...), custom_call_target="tpu_custom_call" | custom-call | flops 134217728 | bytes 1048576 | tf_op jit(solution)/shard_map/pallas_call | solution.py:296
  38.2 1.2 %collective-permute-done.17.received_ref = bf16[128,512]{1,0:T(8,128)(2,1)S(1)} collective-permute-done((bf16[128,512]{1,0:T(8,128)(2,1)S(1)}, bf16[128,512]{1,0:T(8,128)(2,1)S(1)}, u32[]{:S(2)}, u32[]{:S(2)}) %collective-permute-start.17) | collective-permute-done | bytes 131104 | tf_op jit(solution)/shard_map/ppermute | solution.py:283
  39.4 0.9 %shard_map.78 = bf16[2,128,512]{2,1,0:T(8,128)(2,1)} custom-call(f32[128,512]{1,0:T(8,128)S(1)} %get-tuple-element.21.partial_ref, bf16[128,128]{1,0:T(8,128)(2,1)S(1)} %get-tuple-element.22.weights_ref, bf16[128,512]{1,0:T(8,128)(2,1)S(1)} %collective-permute-done.16.value_ref, bf16[128,512]{1,0:T(8,128)(2,1)S(1)} %collective-permute-done.17.received_ref), custom_call_target="tpu_custom_call" | custom-call | flops 16777216 | bytes 1048576 | tf_op jit(solution)/shard_map/pallas_call | solution.py:296
  (33 shorter events, 0.9 us)
Async XLA Ops:
  0.0 3.9 %copy-start = (bf16[64,512]{1,0:T(8,128)(2,1)S(1)}, bf16[64,512]{1,0:T(8,128)(2,1)}, u32[]{:S(2)}) copy-start(bf16[64,512]{1,0:T(8,128)(2,1)} %param.9) | copy-start | bytes 196612
  0.0 22.3 %collective-permute-start.8 = (bf16[2,128,512]{2,1,0:T(8,128)(2,1)}, bf16[2,128,512]{2,1,0:T(8,128)(2,1)S(1)}, u32[]{:S(2)}, u32[]{:S(2)}) collective-permute-start(bf16[2,128,512]{2,1,0:T(8,128)(2,1)} %mine_ref.1), channel_id=1, source_target_pairs={{0,8},{8,0},{16,24},{24,16},{1,9},{9,1},{17,25},{25,17},{2,10},{10... | collective-permute-start | bytes 786440 | tf_op jit(solution)/shard_map/ppermute | solution.py:283
  0.5 9.7 %collective-permute-start.9 = (bf16[2,128,512]{2,1,0:T(8,128)(2,1)}, bf16[2,128,512]{2,1,0:T(8,128)(2,1)S(1)}, u32[]{:S(2)}, u32[]{:S(2)}) collective-permute-start(bf16[2,128,512]{2,1,0:T(8,128)(2,1)} %mine_ref.1), channel_id=1, source_target_pairs={{0,16},{8,24},{16,0},{24,8},{1,17},{9,25},{17,1},{25,9},{2,18},{10... | collective-permute-start | bytes 786440 | tf_op jit(solution)/shard_map/ppermute | solution.py:280
  3.9 3.7 %copy-start.4 = (bf16[64,512]{1,0:T(8,128)(2,1)S(1)}, bf16[64,512]{1,0:T(8,128)(2,1)}, u32[]{:S(2)}) copy-start(bf16[64,512]{1,0:T(8,128)(2,1)} %param.12) | copy-start | bytes 196612
  3.9 18.5 %copy-start.1 = (bf16[2,128,512]{2,1,0:T(8,128)(2,1)S(1)}, bf16[2,128,512]{2,1,0:T(8,128)(2,1)}, u32[]{:S(2)}) copy-start(bf16[2,128,512]{2,1,0:T(8,128)(2,1)} %mine_ref.1) | copy-start | bytes 786436
  3.9 8.8 %collective-permute-start.11 = (bf16[64,768]{1,0:T(8,128)(2,1)S(1)}, bf16[64,768]{1,0:T(8,128)(2,1)S(1)}, u32[]{:S(2)}, u32[]{:S(2)}) collective-permute-start(bf16[64,768]{1,0:T(8,128)(2,1)S(1)} %pad_maximum_fusion.1), channel_id=1, source_target_pairs={{6,0},{7,1},{4,2},{5,3},{2,4},{3,5},{0,6},{1,7},{15,8},{14,9},{13,... | collective-permute-start | bytes 294920 | tf_op jit(solution)/shard_map/ppermute | solution.py:292
  10.2 12.1 %collective-permute-start.10 = (bf16[2,128,512]{2,1,0:T(8,128)(2,1)S(1)}, bf16[2,128,512]{2,1,0:T(8,128)(2,1)S(1)}, u32[]{:S(2)}, u32[]{:S(2)}) collective-permute-start(bf16[2,128,512]{2,1,0:T(8,128)(2,1)S(1)} %collective-permute-done.9.other_ref), channel_id=1, source_target_pairs={{0,8},{8,0},{16,24},{24,16},{1,9},{9,1},{17,25},{25,17},{2,10},{10... | collective-permute-start | bytes 786440 | tf_op jit(solution)/shard_map/ppermute | solution.py:283
  10.2 12.2 %copy-start.2 = (f32[512]{0:T(512)S(1)}, f32[512]{0:T(512)}, u32[]{:S(2)}) copy-start(f32[512]{0:T(512)} %param.8) | copy-start | bytes 6148
  10.2 12.1 %copy-start.3 = (s32[2,2]{1,0:T(2,128)S(1)}, s32[2,2]{1,0:T(2,128)}, u32[]{:S(2)}) copy-start(s32[2,2]{1,0:T(2,128)} %tracks_ref.1) | copy-start | bytes 52
  10.2 5.7 %collective-permute-start.4 = (bf16[64,1024]{1,0:T(8,128)(2,1)S(1)}, bf16[64,1024]{1,0:T(8,128)(2,1)S(1)}, u32[]{:S(2)}, u32[]{:S(2)}) collective-permute-start(bf16[64,1024]{1,0:T(8,128)(2,1)S(1)} %pad_maximum_fusion.refs_0_), channel_id=1, source_target_pairs={{2,0},{3,1},{0,2},{1,3},{6,4},{7,5},{4,6},{5,7},{11,8},{10,9},{9,1... | collective-permute-start | bytes 393224 | tf_op jit(solution)/shard_map/ppermute | solution.py:292
  12.1 6.6 %collective-permute-start.6 = (bf16[64,1024]{1,0:T(8,128)(2,1)S(1)}, bf16[64,1024]{1,0:T(8,128)(2,1)S(1)}, u32[]{:S(2)}, u32[]{:S(2)}) collective-permute-start(bf16[64,1024]{1,0:T(8,128)(2,1)S(1)} %pad_maximum_fusion.refs_0_), channel_id=1, source_target_pairs={{9,8},{8,9},{11,10},{10,11},{13,12},{12,13},{15,14},{14,15},{25,24... | collective-permute-start | bytes 393224 | tf_op jit(solution)/shard_map/ppermute | solution.py:292
  12.8 6.2 %collective-permute-start.13 = (bf16[64,768]{1,0:T(8,128)(2,1)S(1)}, bf16[64,768]{1,0:T(8,128)(2,1)S(1)}, u32[]{:S(2)}, u32[]{:S(2)}) collective-permute-start(bf16[64,768]{1,0:T(8,128)(2,1)S(1)} %pad_maximum_fusion.1), channel_id=1, source_target_pairs={{4,0},{5,1},{6,2},{7,3},{0,4},{1,5},{2,6},{3,7},{13,8},{12,9},{15,... | collective-permute-start | bytes 294920 | tf_op jit(solution)/shard_map/ppermute | solution.py:292
  16.0 7.7 %collective-permute-start.5 = (bf16[64,1024]{1,0:T(8,128)(2,1)S(1)}, bf16[64,1024]{1,0:T(8,128)(2,1)S(1)}, u32[]{:S(2)}, u32[]{:S(2)}) collective-permute-start(bf16[64,1024]{1,0:T(8,128)(2,1)S(1)} %collective-permute-done.4.refs_5_), channel_id=1, source_target_pairs={{0,8},{8,0},{16,24},{24,16},{1,9},{9,1},{17,25},{25,17},{2,10},{10... | collective-permute-start | bytes 393224 | tf_op jit(solution)/shard_map/ppermute | solution.py:283
  18.7 4.9 %collective-permute-start.7 = (bf16[64,1024]{1,0:T(8,128)(2,1)S(1)}, bf16[64,1024]{1,0:T(8,128)(2,1)S(1)}, u32[]{:S(2)}, u32[]{:S(2)}) collective-permute-start(bf16[64,1024]{1,0:T(8,128)(2,1)S(1)} %collective-permute-done.6.refs_7_), channel_id=1, source_target_pairs={{0,8},{8,0},{16,24},{24,16},{1,9},{9,1},{17,25},{25,17},{2,10},{10... | collective-permute-start | bytes 393224 | tf_op jit(solution)/shard_map/ppermute | solution.py:283
  18.9 4.3 %collective-permute-start.12 = (bf16[64,768]{1,0:T(8,128)(2,1)S(1)}, bf16[64,768]{1,0:T(8,128)(2,1)S(1)}, u32[]{:S(2)}, u32[]{:S(2)}) collective-permute-start(bf16[64,768]{1,0:T(8,128)(2,1)S(1)} %collective-permute-done.11.refs_1_), channel_id=1, source_target_pairs={{0,8},{8,0},{16,24},{24,16},{1,9},{9,1},{17,25},{25,17},{2,10},{10... | collective-permute-start | bytes 294920 | tf_op jit(solution)/shard_map/ppermute | solution.py:283
  22.3 1.3 %collective-permute-start.14 = (bf16[64,768]{1,0:T(8,128)(2,1)S(1)}, bf16[64,768]{1,0:T(8,128)(2,1)S(1)}, u32[]{:S(2)}, u32[]{:S(2)}) collective-permute-start(bf16[64,768]{1,0:T(8,128)(2,1)S(1)} %collective-permute-done.13.refs_3_), channel_id=1, source_target_pairs={{0,8},{8,0},{16,24},{24,16},{1,9},{9,1},{17,25},{25,17},{2,10},{10... | collective-permute-start | bytes 294920 | tf_op jit(solution)/shard_map/ppermute | solution.py:283
  25.4 11.9 %collective-permute-start.15 = (bf16[128,512]{1,0:T(8,128)(2,1)S(1)}, bf16[128,512]{1,0:T(8,128)(2,1)S(1)}, u32[]{:S(2)}, u32[]{:S(2)}) collective-permute-start(bf16[128,512]{1,0:T(8,128)(2,1)S(1)} %get-tuple-element.17.refs_9_), channel_id=1, source_target_pairs={{0,16},{8,24},{16,0},{24,8},{1,17},{9,25},{17,1},{25,9},{2,18},{10... | collective-permute-start | bytes 393224 | tf_op jit(solution)/shard_map/ppermute | solution.py:280
  28.3 9.5 %collective-permute-start.16 = (bf16[128,512]{1,0:T(8,128)(2,1)S(1)}, bf16[128,512]{1,0:T(8,128)(2,1)S(1)}, u32[]{:S(2)}, u32[]{:S(2)}) collective-permute-start(bf16[128,512]{1,0:T(8,128)(2,1)S(1)} %shard_map.75.refs_10_), channel_id=1, source_target_pairs={{0,16},{8,24},{16,0},{24,8},{1,17},{9,25},{17,1},{25,9},{2,18},{10... | collective-permute-start | bytes 393224 | tf_op jit(solution)/shard_map/ppermute | solution.py:280
  28.8 5.7 %collective-permute-start = (bf16[64,256]{1,0:T(8,128)(2,1)S(1)}, bf16[64,256]{1,0:T(8,128)(2,1)S(1)}, u32[]{:S(2)}, u32[]{:S(2)}) collective-permute-start(bf16[64,256]{1,0:T(8,128)(2,1)S(1)} %constant_dynamic-slice_fusion), channel_id=1, source_target_pairs={{6,0},{7,1},{4,2},{5,3},{2,4},{3,5},{0,6},{1,7},{15,8},{14,9},{13,... | collective-permute-start | bytes 98312 | tf_op jit(solution)/shard_map/ppermute | solution.py:292
  31.3 4.8 %collective-permute-start.2 = (bf16[64,256]{1,0:T(8,128)(2,1)S(1)}, bf16[64,256]{1,0:T(8,128)(2,1)S(1)}, u32[]{:S(2)}, u32[]{:S(2)}) collective-permute-start(bf16[64,256]{1,0:T(8,128)(2,1)S(1)} %constant_dynamic-slice_fusion), channel_id=1, source_target_pairs={{4,0},{5,1},{6,2},{7,3},{0,4},{1,5},{2,6},{3,7},{13,8},{12,9},{15,... | collective-permute-start | bytes 98312 | tf_op jit(solution)/shard_map/ppermute | solution.py:292
  34.6 1.6 %collective-permute-start.1 = (bf16[64,256]{1,0:T(8,128)(2,1)S(1)}, bf16[64,256]{1,0:T(8,128)(2,1)S(1)}, u32[]{:S(2)}, u32[]{:S(2)}) collective-permute-start(bf16[64,256]{1,0:T(8,128)(2,1)S(1)} %collective-permute-done.refs_1_), channel_id=1, source_target_pairs={{0,8},{8,0},{16,24},{24,16},{1,9},{9,1},{17,25},{25,17},{2,10},{10... | collective-permute-start | bytes 98312 | tf_op jit(solution)/shard_map/ppermute | solution.py:283
  36.1 1.2 %collective-permute-start.3 = (bf16[64,256]{1,0:T(8,128)(2,1)S(1)}, bf16[64,256]{1,0:T(8,128)(2,1)S(1)}, u32[]{:S(2)}, u32[]{:S(2)}) collective-permute-start(bf16[64,256]{1,0:T(8,128)(2,1)S(1)} %collective-permute-done.2.refs_3_), channel_id=1, source_target_pairs={{0,8},{8,0},{16,24},{24,16},{1,9},{9,1},{17,25},{25,17},{2,10},{10... | collective-permute-start | bytes 98312 | tf_op jit(solution)/shard_map/ppermute | solution.py:283
  38.0 1.4 %collective-permute-start.17 = (bf16[128,512]{1,0:T(8,128)(2,1)S(1)}, bf16[128,512]{1,0:T(8,128)(2,1)S(1)}, u32[]{:S(2)}, u32[]{:S(2)}) collective-permute-start(bf16[128,512]{1,0:T(8,128)(2,1)S(1)} %shard_map.77), channel_id=1, source_target_pairs={{0,8},{8,0},{16,24},{24,16},{1,9},{9,1},{17,25},{25,17},{2,10},{10... | collective-permute-start | bytes 393224 | tf_op jit(solution)/shard_map/ppermute | solution.py:283

commit v3 on v2

--- a/solution.py
+++ b/solution.py
@@ -123,7 +123,7 @@
 
 
 def norm_kernel(tracks_ref, gain_ref, mine_ref, beside_ref, other_ref, diagonal_ref, *outs):
-    normed_ref, bounds_ref = outs
+    normed_ref, below_ref, within_ref, live_ref = outs
     rows_here = mine_ref.shape[1]
     tm = lax.axis_index("tm")
     core = tm % 2
@@ -131,46 +131,60 @@
     for k, ref in enumerate((mine_ref, beside_ref, other_ref, diagonal_ref)):
         rows = pl.ds(pl.multiple_of((tm ^ k) * rows_here, rows_here), rows_here)
         normed_ref[rows, :] = normalize(ref[core], gain)
-    for n in range(2):
-        bounds_ref[n] = jnp.full(bounds_ref.shape[1:], tracks_ref[core, n], jnp.int32)
-
-
-def attend(bounds_ref, queries, keys, values, out_ref, head_dim):
-    span, steps = out_ref.shape
-    block = LANES
-    scale = 1.0 / math.sqrt(head_dim)
-    start, end = bounds_ref[0, :1, :block], bounds_ref[1, :1, :block]
+    start, end = tracks_ref[core, 0], tracks_ref[core, 1]
+    steps, block = below_ref.shape
+    key_pos = lax.broadcasted_iota(jnp.int32, (steps, block), 0)
+    column = lax.broadcasted_iota(jnp.int32, (steps, block), 1)
+    early = key_pos < start
+    barred = early | (lax.rem(key_pos, block) > column)
+    below_ref[...] = jnp.where(early, NEGATIVE, 0.0).astype(below_ref.dtype)
+    within_ref[...] = jnp.where(barred, NEGATIVE, 0.0).astype(within_ref.dtype)
+    position = lax.broadcasted_iota(jnp.int32, live_ref.shape, 1)
+    live_ref[...] = ((position >= start) & (position < end)).astype(jnp.float32)
+
+
+def attend(below_ref, within_ref, live_ref, queries, keys, values, out_ref, first, head_dim):
+    steps = out_ref.shape[1]
+    block = span = LANES
+    group = pl.ds(first, span)
+    ratio = math.log2(math.e) / math.sqrt(head_dim)
     lane = lax.broadcasted_iota(jnp.int32, (block, span), 1)
+    diagonal = lane == lax.broadcasted_iota(jnp.int32, (block, span), 0)
+    diagonal = diagonal.astype(jnp.float32).astype(jnp.bfloat16)
     for j in range(steps // block):
-        reach = (j + 1) * block
-        key_pos = lax.broadcasted_iota(jnp.int32, (reach, block), 0)
-        query_pos = j * block + lax.broadcasted_iota(jnp.int32, (reach, block), 1)
-        allowed = (key_pos >= start) & (key_pos <= query_pos)
-        allowed = jnp.concatenate([allowed] * (span // head_dim), axis=1)
-        column = j * block + lax.broadcasted_iota(jnp.int32, (1, block), 1)
-        live = (column >= start) & (column < end)
-        query_block = queries[pl.ds(j * block, block), :]
+        here = pl.ds(j * block, block)
+        query_block = queries[here, group]
         one = [
             jnp.where((lane >= low) & (lane < low + head_dim), query_block, jnp.zeros_like(query_block))
             for low in range(0, span, head_dim)
         ]
-        scores = lax.dot_general(
-            keys[pl.ds(0, reach), :],
-            jnp.concatenate(one, axis=0),
-            (((1,), (1,)), ((), ())),
-            preferred_element_type=jnp.float32,
-        )
-        scores = jnp.where(allowed, scores * scale, NEGATIVE)
-        highest = jnp.max(scores, axis=0, keepdims=True)
-        weight = jnp.exp(scores - highest)
-        total = jnp.sum(weight, axis=0, keepdims=True)
+        one = jnp.concatenate([jnp.concatenate([o, diagonal], axis=1) for o in one], axis=0)
+        scores = []
+        for begin, count, mask in ((0, j * block, below_ref), (j * block, block, within_ref)):
+            if count:
+                rows = pl.ds(begin, count)
+                scores.append(
+                    lax.dot_general(
+                        jnp.concatenate([keys[rows, group], mask[rows, :]], axis=1),
+                        one,
+                        (((1,), (1,)), ((), ())),
+                        preferred_element_type=jnp.float32,
+                    )
+                )
+        highest = functools.reduce(
+            jnp.maximum, [jnp.max(score, axis=0, keepdims=True) for score in scores]
+        )
+        weight = [jnp.exp2((score - highest) * ratio) for score in scores]
+        total = sum(jnp.sum(w, axis=0, keepdims=True) for w in weight)
+        weight = jnp.concatenate([w.astype(jnp.bfloat16) for w in weight], axis=0)
         summed = jnp.dot(
-            values[:, pl.ds(0, reach)], weight.astype(jnp.bfloat16), preferred_element_type=jnp.float32
-        )
+            values[group, pl.ds(0, (j + 1) * block)], weight, preferred_element_type=jnp.float32
+        )
+        live = live_ref[:1, here] > 0.0
         for h in range(span // head_dim):
             rows, lanes = slice(h * head_dim, (h + 1) * head_dim), slice(h * block, (h + 1) * block)
             result = jnp.where(live, summed[rows, lanes] / total[:, lanes], 0.0)
-            out_ref[rows, pl.ds(j * block, block)] = result.astype(jnp.bfloat16)
+            out_ref[pl.ds(first + h * head_dim, head_dim), here] = result.astype(jnp.bfloat16)
 
 
 def place(sources, refs, target, begin, columns):
@@ -191,24 +205,19 @@
                     pl.when(core == here)(functools.partial(put, ref, agent ^ offset))
 
 
-def first_kernel(sources, head_dim, bounds_ref, normed_ref, *refs):
-    shards, refs = refs[: 1 + 2 * len(sources)], refs[1 + 2 * len(sources) :]
-    out_ref, late, weights, held = refs[0], refs[1:4], refs[4], refs[5:]
+def attention_kernel(sources, head_dim, normed_ref, below_ref, within_ref, live_ref, *refs):
+    shards = refs[: 1 + 2 * len(sources)]
+    out_ref, weights, queries, keys, values = refs[1 + 2 * len(sources) :]
     _, columns = weights.shape
     span = columns // 3
     place(sources, shards, weights, 0, columns)
-    for n in range(3):
+    for n, target in enumerate((queries, keys, values)):
         full = jnp.dot(
             normed_ref[...], weights[:, n * span : (n + 1) * span], preferred_element_type=jnp.float32
         )
-        for m, target in enumerate((held[n], late[n])):
-            part = full[:, m * LANES : (m + 1) * LANES]
-            target[...] = (part.T if n == 2 else part).astype(jnp.bfloat16)
-    attend(bounds_ref, *held, out_ref, head_dim)
-
-
-def second_kernel(head_dim, bounds_ref, queries, keys, values, out_ref):
-    attend(bounds_ref, queries, keys, values, out_ref, head_dim)
+        target[...] = (full.T if n == 2 else full).astype(jnp.bfloat16)
+    for first in range(0, span, LANES):
+        attend(below_ref, within_ref, live_ref, queries, keys, values, out_ref, first, head_dim)
 
 
 def transposed_dot(weight, value):
@@ -219,25 +228,17 @@
 
 def partial_kernel(sources, *refs):
     shards, refs = refs[: 1 + 2 * len(sources)], refs[1 + 2 * len(sources) :]
-    here, kept_ref, given_ref, kept_weights, given_weights, weights = (
-        refs[:3],
-        *refs[3:7],
-        refs[7],
-    )
+    value_ref, kept_ref, given_ref, kept_weights, given_weights, weights = refs
     _, columns = weights.shape
     half = columns // 2
     core, y = lax.axis_index("tm") % 2, lax.axis_index("tm") // 2
     place(sources, shards, weights, 3 * columns, columns)
+    mine = pl.ds(pl.multiple_of(y * columns, columns), columns)
+    other = pl.ds(pl.multiple_of((y ^ 1) * columns, columns), columns)
     for n, (ref, last) in enumerate(((kept_ref, kept_weights), (given_ref, given_weights))):
         lanes = pl.ds(pl.multiple_of((core ^ n) * half, half), half)
-        total = None
-        for m, value in enumerate(here):
-            first = ((y ^ (m // 2)) * 2 + m % 2) * LANES
-            rows = pl.ds(pl.multiple_of(first, LANES), LANES)
-            term = transposed_dot(weights[rows, lanes], value[...])
-            total = term if total is None else total + term
-        ref[...] = total
-        last[...] = weights[pl.ds(pl.multiple_of(((y ^ 1) * 2 + 1) * LANES, LANES), LANES), lanes]
+        ref[...] = transposed_dot(weights[mine, lanes], value_ref[...])
+        last[...] = weights[other, lanes]
 
 
 def given_kernel(partial_ref, weights_ref, value_ref, out_ref):
@@ -246,12 +247,13 @@
     )
 
 
-def final_kernel(partial_ref, weights_ref, value_ref, received_ref, out_ref):
-    core = lax.axis_index("tm") % 2
-    out_ref[1 - core] = received_ref[...]
-    out_ref[core] = (partial_ref[...] + transposed_dot(weights_ref[...], value_ref[...])).astype(
-        jnp.bfloat16
-    )
+def kept_kernel(partial_ref, weights_ref, value_ref, out_ref, held):
+    given_kernel(partial_ref, weights_ref, value_ref, held)
+    pltpu.sync_copy(held, out_ref.at[lax.axis_index("tm") % 2])
+
+
+def final_kernel(received_ref, started_ref, out_ref):
+    pltpu.sync_copy(received_ref, out_ref.at[1 - lax.axis_index("tm") % 2])
 
 
 def fits(n_tm, n_agent, features):
@@ -291,18 +293,21 @@
         ]
         return lax.ppermute(value, ("tm", "agent"), pairs)
 
-    def kernel(body, outs, args, scratch=(), smem=0, **estimate):
-        vmem = pl.BlockSpec(memory_space=pltpu.VMEM)
-        out = pl.pallas_call(
+    vmem = pl.BlockSpec(memory_space=pltpu.VMEM)
+    smem = pl.BlockSpec(memory_space=pltpu.SMEM)
+    anywhere = pl.BlockSpec(memory_space=pl.ANY)
+
+    def kernel(body, outs, args, scratch=(), specs=None, out_spec=vmem, aliases={}, **estimate):
+        return pl.pallas_call(
             body,
             out_shape=[jax.ShapeDtypeStruct(shape, dtype) for shape, dtype in outs],
-            in_specs=[pl.BlockSpec(memory_space=pltpu.SMEM)] * smem + [vmem] * (len(args) - smem),
-            out_specs=[vmem] * len(outs),
+            in_specs=specs or [vmem] * len(args),
+            out_specs=[out_spec] * len(outs),
             scratch_shapes=[pltpu.VMEM(shape, dtype) for shape, dtype in scratch],
+            input_output_aliases=aliases,
             compiler_params=params(),
             cost_estimate=cost(**estimate),
         )(*args)
-        return out
 
     half, full = jnp.bfloat16, jnp.float32
     pieces = [
@@ -320,34 +325,23 @@
     diagonal = swap(other_rows)
     swapped = [swap(value) for value in fetched]
     swapped_out = [swap(value) for value in fetched_out]
-    normed, bounds = kernel(
+    masks = kernel(
         norm_kernel,
-        [((steps, width), half), ((2, 8, LANES), jnp.int32)],
+        [((steps, width), half)] + [((steps, LANES), half)] * 2 + [((8, steps), full)],
         (tracks, norm_gain.reshape(1, width), features, beside, other_rows, diagonal),
-        smem=1,
+        specs=[smem] + [vmem] * 5,
         flops=8 * steps * width,
     )
     shards = [packed] + [v for pair in zip(fetched, swapped) for v in pair]
-    head_flops = 4 * steps * steps * LANES
-    heads = [((steps, LANES), half)] * 2 + [((LANES, steps), half)]
-    exponentials = steps * steps * LANES // head_dim
-    attended_first, *late = kernel(
-        functools.partial(first_kernel, sources, head_dim),
-        [((LANES, steps), half)] + heads,
-        (bounds, normed, *shards),
-        scratch=[((width, 3 * span), half)] + heads,
-        flops=6 * steps * width * span + head_flops,
-        transcendentals=exponentials,
-    )
-    other_first = across(attended_first)
-    (attended_second,) = kernel(
-        functools.partial(second_kernel, head_dim),
-        [((LANES, steps), half)],
-        (bounds, *late),
-        flops=head_flops,
-        transcendentals=exponentials,
-    )
-    other_second = across(attended_second)
+    (attended,) = kernel(
+        functools.partial(attention_kernel, sources, head_dim),
+        [((span, steps), half)],
+        (*masks, *shards),
+        scratch=[((width, 3 * span), half)] + [((steps, span), half)] * 2 + [((span, steps), half)],
+        flops=6 * steps * width * span + 4 * steps * steps * span,
+        transcendentals=steps * steps * span // head_dim,
+    )
+    other = across(attended)
     out_shards = [packed] + [
         v
         for pair in zip(fetched_out + fetched[near:], swapped_out + swapped[near:])
@@ -355,23 +349,34 @@
     ]
     kept, given, kept_weights, given_weights = kernel(
         functools.partial(partial_kernel, sources),
-        [((span // 2, steps), full)] * 2 + [((LANES, span // 2), half)] * 2,
-        (*out_shards, attended_first, attended_second, other_first),
+        [((span // 2, steps), full)] * 2 + [((span, span // 2), half)] * 2,
+        (*out_shards, attended),
         scratch=[((width, span), half)],
-        flops=2 * steps * width * span,
+        flops=2 * steps * span * span,
     )
     (given,) = kernel(
         given_kernel,
         [((span // 2, steps), half)],
-        (given, given_weights, other_second),
-        flops=steps * LANES * span,
+        (given, given_weights, other),
+        flops=steps * span * span,
     )
     received = swap(given)
+    (started,) = kernel(
+        kept_kernel,
+        [((2, span // 2, steps), half)],
+        (kept, kept_weights, other),
+        scratch=[((span // 2, steps), half)],
+        out_spec=anywhere,
+        flops=steps * span * span,
+    )
     (out,) = kernel(
         final_kernel,
         [((2, span // 2, steps), half)],
-        (kept, kept_weights, other_second, received),
-        flops=steps * LANES * span,
+        (received, started),
+        specs=[vmem, anywhere],
+        out_spec=anywhere,
+        aliases={1: 0},
+        flops=0,
     )
     return out
 

time: 40.5 us -> 39.5 us (0.975)
  waiting for transfers between devices: 10.9 us -> 9.78 us
  Pallas kernels: 5.37 us -> 5.98 us
  starting transfers between devices: 23.1 us -> 22.6 us
    ppermute x9, waiting for transfers between devices: 2.87 us -> 1.8 us  [swap(): return lax.ppermute(value, 'tm', [(i, i ^ 1) for i in range(n_tm)])]
    pallas_call x6, Pallas kernels: 5.37 us -> 5.98 us  [kernel(): pl.pallas_call(body, out_shape=[jax.ShapeDtypeStruct(shape, dtype) for sh...]
    ppermute x3 -> x2, starting transfers between devices: 4.74 us -> 4.16 us  [across(): return lax.ppermute(value, 'tm', [(i, i ^ 2) for i in range(n_tm)])]
    ppermute x3 -> x2, waiting for transfers between devices: 2.61 us -> 2.61 us  [across(): return lax.ppermute(value, 'tm', [(i, i ^ 2) for i in range(n_tm)])]
  transfers between devices with their start and end apart: 18 -> 17, of which waited for: 8 -> 7; matrix products, arithmetic and copies ran while one was open for 2% -> 2% of each run, Pallas kernels for 6% -> 5%
where the time goes in v3:
time: 39.5 us; the launch traced here: 39.3 us
  starting transfers between devices  22.6 us (57%)
  waiting for transfers between devices  9.78 us (25%)
  Pallas kernels  5.98 us (15%)
  local copies, waits for them, and re-layouts  0.82 us (2%)
    ppermute x6, starting transfers between devices, fetch(): return lax.ppermute(value, ('tm', 'agent'), pairs)  11.3 us
    ppermute x9, starting transfers between devices, swap(): return lax.ppermute(value, 'tm', [(i, i ^ 1) for i in range(n_tm)])  7.17 us
    pallas_call x6, Pallas kernels, kernel(): pl.pallas_call(body, out_shape=[jax.ShapeDtypeStruct(shape, dtype) for sh...  5.98 us
    ppermute x6, waiting for transfers between devices, fetch(): return lax.ppermute(value, ('tm', 'agent'), pairs)  5.37 us
    ppermute x2, starting transfers between devices, across(): return lax.ppermute(value, 'tm', [(i, i ^ 2) for i in range(n_tm)])  4.16 us
    ppermute x2, waiting for transfers between devices, across(): return lax.ppermute(value, 'tm', [(i, i ^ 2) for i in range(n_tm)])  2.61 us
    ppermute x9, waiting for transfers between devices, swap(): return lax.ppermute(value, 'tm', [(i, i ^ 1) for i in range(n_tm)])  1.8 us
    dynamic_slice x3, local copies, waits for them, and re-layouts, split_heads(): lax.dynamic_slice_in_dim(w, y * span, span, 1)  0.79 us
  transfers between devices with their start and end apart: 17, of which 7 were waited for; matrix products, arithmetic and copies ran while one was open for 2% of the time, Pallas kernels for 5%

profile of v3, /device:TPU:0, one launch (start us, length us, event | category | flops | bytes accessed | tf_op | source)
XLA Modules:
  0.0 39.3 jit_solution(9254521449783088944)
XLA Ops:
  0.0 0.5 %collective-permute-start.8 = (bf16[2,128,512]{2,1,0:T(8,128)(2,1)}, bf16[2,128,512]{2,1,0:T(8,128)(2,1)S(1)}, u32[]{:S(2)}, u32[]{:S(2)}) collective-permute-start(bf16[2,128,512]{2,1,0:T(8,128)(2,1)} %mine_ref.1), channel_id=1, source_target_pairs={{0,8},{8,0},{16,24},{24,16},{1,9},{9,1},{17,25},{25,17},{2,10},{10... | collective-permute-start | bytes 786440 | tf_op jit(solution)/shard_map/ppermute | solution.py:285
  0.5 2.6 %collective-permute-start.9 = (bf16[2,128,512]{2,1,0:T(8,128)(2,1)}, bf16[2,128,512]{2,1,0:T(8,128)(2,1)S(1)}, u32[]{:S(2)}, u32[]{:S(2)}) collective-permute-start(bf16[2,128,512]{2,1,0:T(8,128)(2,1)} %mine_ref.1), channel_id=1, source_target_pairs={{0,16},{8,24},{16,0},{24,8},{1,17},{9,25},{17,1},{25,9},{2,18},{10... | collective-permute-start | bytes 786440 | tf_op jit(solution)/shard_map/ppermute | solution.py:282
  3.1 0.8 %constant_dynamic-slice_fusion.1 = (bf16[64,256]{1,0:T(8,128)(2,1)S(1)}, bf16[64,256]{1,0:T(8,128)(2,1)S(1)}) fusion(bf16[64,512]{1,0:T(8,128)(2,1)} %param.11, s32[]{:T(128)S(6)} %select_n.12, bf16[64,512]{1,0:T(8,128)(2,1)} %param.10), kind=kLoop, calls=%fused_computation.3 | loop fusion | bytes 131076 | tf_op jit(solution)/shard_map/dynamic_slice | solution.py:314
  3.9 3.7 %collective-permute-start.11 = (bf16[64,768]{1,0:T(8,128)(2,1)S(1)}, bf16[64,768]{1,0:T(8,128)(2,1)S(1)}, u32[]{:S(2)}, u32[]{:S(2)}) collective-permute-start(bf16[64,768]{1,0:T(8,128)(2,1)S(1)} %pad_maximum_fusion.1), channel_id=1, source_target_pairs={{6,0},{7,1},{4,2},{5,3},{2,4},{3,5},{0,6},{1,7},{15,8},{14,9},{13,... | collective-permute-start | bytes 294920 | tf_op jit(solution)/shard_map/ppermute | solution.py:294
  7.6 2.6 %collective-permute-done.9.other_ref = bf16[2,128,512]{2,1,0:T(8,128)(2,1)S(1)} collective-permute-done((bf16[2,128,512]{2,1,0:T(8,128)(2,1)}, bf16[2,128,512]{2,1,0:T(8,128)(2,1)S(1)}, u32[]{:S(2)}, u32[]{:S(2)}) %collective-permute-start.9) | collective-permute-done | bytes 262176 | tf_op jit(solution)/shard_map/ppermute | solution.py:282
  10.2 1.9 %collective-permute-start.4 = (bf16[64,1024]{1,0:T(8,128)(2,1)S(1)}, bf16[64,1024]{1,0:T(8,128)(2,1)S(1)}, u32[]{:S(2)}, u32[]{:S(2)}) collective-permute-start(bf16[64,1024]{1,0:T(8,128)(2,1)S(1)} %pad_maximum_fusion.refs_0_), channel_id=1, source_target_pairs={{2,0},{3,1},{0,2},{1,3},{6,4},{7,5},{4,6},{5,7},{11,8},{10,9},{9,1... | collective-permute-start | bytes 393224 | tf_op jit(solution)/shard_map/ppermute | solution.py:294
  12.1 0.7 %collective-permute-start.6 = (bf16[64,1024]{1,0:T(8,128)(2,1)S(1)}, bf16[64,1024]{1,0:T(8,128)(2,1)S(1)}, u32[]{:S(2)}, u32[]{:S(2)}) collective-permute-start(bf16[64,1024]{1,0:T(8,128)(2,1)S(1)} %pad_maximum_fusion.refs_0_), channel_id=1, source_target_pairs={{9,8},{8,9},{11,10},{10,11},{13,12},{12,13},{15,14},{14,15},{25,24... | collective-permute-start | bytes 393224 | tf_op jit(solution)/shard_map/ppermute | solution.py:294
  12.8 2.7 %collective-permute-start.13 = (bf16[64,768]{1,0:T(8,128)(2,1)S(1)}, bf16[64,768]{1,0:T(8,128)(2,1)S(1)}, u32[]{:S(2)}, u32[]{:S(2)}) collective-permute-start(bf16[64,768]{1,0:T(8,128)(2,1)S(1)} %pad_maximum_fusion.1), channel_id=1, source_target_pairs={{4,0},{5,1},{6,2},{7,3},{0,4},{1,5},{2,6},{3,7},{13,8},{12,9},{15,... | collective-permute-start | bytes 294920 | tf_op jit(solution)/shard_map/ppermute | solution.py:294
  15.4 0.6 %collective-permute-done.4.refs_5_ = bf16[64,1024]{1,0:T(8,128)(2,1)S(1)} collective-permute-done((bf16[64,1024]{1,0:T(8,128)(2,1)S(1)}, bf16[64,1024]{1,0:T(8,128)(2,1)S(1)}, u32[]{:S(2)}, u32[]{:S(2)}) %collective-permute-start.4) | collective-permute-done | bytes 131104 | tf_op jit(solution)/shard_map/ppermute | solution.py:294
  16.0 2.7 %collective-permute-start.5 = (bf16[64,1024]{1,0:T(8,128)(2,1)S(1)}, bf16[64,1024]{1,0:T(8,128)(2,1)S(1)}, u32[]{:S(2)}, u32[]{:S(2)}) collective-permute-start(bf16[64,1024]{1,0:T(8,128)(2,1)S(1)} %collective-permute-done.4.refs_5_), channel_id=1, source_target_pairs={{0,8},{8,0},{16,24},{24,16},{1,9},{9,1},{17,25},{25,17},{2,10},{10... | collective-permute-start | bytes 393224 | tf_op jit(solution)/shard_map/ppermute | solution.py:285
  18.9 3.4 %collective-permute-start.12 = (bf16[64,768]{1,0:T(8,128)(2,1)S(1)}, bf16[64,768]{1,0:T(8,128)(2,1)S(1)}, u32[]{:S(2)}, u32[]{:S(2)}) collective-permute-start(bf16[64,768]{1,0:T(8,128)(2,1)S(1)} %collective-permute-done.11.refs_1_), channel_id=1, source_target_pairs={{0,8},{8,0},{16,24},{24,16},{1,9},{9,1},{17,25},{25,17},{2,10},{10... | collective-permute-start | bytes 294920 | tf_op jit(solution)/shard_map/ppermute | solution.py:285
  22.4 0.9 %shard_map.73 = (bf16[512,512]{1,0:T(8,128)(2,1)S(1)}, bf16[512,128]{1,0:T(8,128)(2,1)S(1)}, bf16[512,128]{1,0:T(8,128)(2,1)S(1)}, f32[8,512]{1,0:T(8,128)S(1)}) custom-call(s32[2,2]{1,0:T(2,128)S(1)} %copy-done.3, f32[1,512]{1,0:T(1,128)S(1)} %bitcast.1, bf16[2,128,512]{2,1,0:T(8,128)(2,1)S(1)} %copy-done.1, ...), custom_call_target="tpu_custom_call" | custom-call | flops 2097152 | bytes 1048576 | tf_op jit(solution)/shard_map/pallas_call | solution.py:301
  23.3 0.4 collective-permute-done.14.refs_4_
  23.6 3.0 %shard_map.74.refs_9_ = bf16[256,512]{1,0:T(8,128)(2,1)S(1)} custom-call(bf16[512,512]{1,0:T(8,128)(2,1)S(1)} %get-tuple-element.13.normed_ref, bf16[512,128]{1,0:T(8,128)(2,1)S(1)} %get-tuple-element.14.below_ref, bf16[512,128]{1,0:T(8,128)(2,1)S(1)} %get-tuple-element.15.within_ref, f32[8,512]{1,0:T(8,128)S(1)} %get-tuple-element.16.live_ref, ...), custom_call_target="tpu_custom_call" | custom-call | flops 671088640 | bytes 1048576 | tf_op jit(solution)/shard_map/pallas_call | solution.py:301
  26.7 1.6 %collective-permute-start.15 = (bf16[256,512]{1,0:T(8,128)(2,1)S(1)}, bf16[256,512]{1,0:T(8,128)(2,1)S(1)}, u32[]{:S(2)}, u32[]{:S(2)}) collective-permute-start(bf16[256,512]{1,0:T(8,128)(2,1)S(1)} %shard_map.74.refs_9_), channel_id=1, source_target_pairs={{0,16},{8,24},{16,0},{24,8},{1,17},{9,25},{17,1},{25,9},{2,18},{10... | collective-permute-start | bytes 786440 | tf_op jit(solution)/shard_map/ppermute | solution.py:282
  28.3 2.5 %collective-permute-start = (bf16[64,256]{1,0:T(8,128)(2,1)S(1)}, bf16[64,256]{1,0:T(8,128)(2,1)S(1)}, u32[]{:S(2)}, u32[]{:S(2)}) collective-permute-start(bf16[64,256]{1,0:T(8,128)(2,1)S(1)} %constant_dynamic-slice_fusion), channel_id=1, source_target_pairs={{6,0},{7,1},{4,2},{5,3},{2,4},{3,5},{0,6},{1,7},{15,8},{14,9},{13,... | collective-permute-start | bytes 98312 | tf_op jit(solution)/shard_map/ppermute | solution.py:294
  30.7 3.4 %collective-permute-done.refs_1_ = bf16[64,256]{1,0:T(8,128)(2,1)S(1)} collective-permute-done((bf16[64,256]{1,0:T(8,128)(2,1)S(1)}, bf16[64,256]{1,0:T(8,128)(2,1)S(1)}, u32[]{:S(2)}, u32[]{:S(2)}) %collective-permute-start) | collective-permute-done | bytes 32800 | tf_op jit(solution)/shard_map/ppermute | solution.py:294
  34.1 1.4 %collective-permute-done.2.refs_3_ = bf16[64,256]{1,0:T(8,128)(2,1)S(1)} collective-permute-done((bf16[64,256]{1,0:T(8,128)(2,1)S(1)}, bf16[64,256]{1,0:T(8,128)(2,1)S(1)}, u32[]{:S(2)}, u32[]{:S(2)}) %collective-permute-start.2) | collective-permute-done | bytes 32800 | tf_op jit(solution)/shard_map/ppermute | solution.py:294
  35.6 1.1 %collective-permute-done.3.refs_4_ = bf16[64,256]{1,0:T(8,128)(2,1)S(1)} collective-permute-done((bf16[64,256]{1,0:T(8,128)(2,1)S(1)}, bf16[64,256]{1,0:T(8,128)(2,1)S(1)}, u32[]{:S(2)}, u32[]{:S(2)}) %collective-permute-start.3) | collective-permute-done | bytes 32800 | tf_op jit(solution)/shard_map/ppermute | solution.py:285
  36.7 0.3 shard_map.75
  37.3 0.2 collective-permute-start.16
  37.5 0.9 %shard_map.77.started_ref = bf16[2,128,512]{2,1,0:T(8,128)(2,1)} custom-call(f32[128,512]{1,0:T(8,128)S(1)} %get-tuple-element.19.partial_ref, bf16[256,128]{1,0:T(8,128)(2,1)S(1)} %get-tuple-element.20.weights_ref, bf16[256,512]{1,0:T(8,128)(2,1)S(1)} %collective-permute-done.15.value_ref), custom_call_target="tpu_custom_call" | custom-call | flops 33554432 | bytes 1048576 | tf_op jit(solution)/shard_map/pallas_call | solution.py:301
  38.4 0.3 collective-permute-done.16.received_ref
  38.7 0.7 %shard_map.78 = bf16[2,128,512]{2,1,0:T(8,128)(2,1)} custom-call(bf16[128,512]{1,0:T(8,128)(2,1)S(1)} %collective-permute-done.16.received_ref, bf16[2,128,512]{2,1,0:T(8,128)(2,1)} %shard_map.77.started_ref), custom_call_target="tpu_custom_call", output_to_operand_aliasing={{}: (1, {})} | custom-call | bytes 1048576 | tf_op jit(solution)/shard_map/pallas_call | solution.py:301
  (31 shorter events, 0.6 us)
Async XLA Ops:
  0.0 3.9 %copy-start = (bf16[64,512]{1,0:T(8,128)(2,1)S(1)}, bf16[64,512]{1,0:T(8,128)(2,1)}, u32[]{:S(2)}) copy-start(bf16[64,512]{1,0:T(8,128)(2,1)} %param.9) | copy-start | bytes 196612
  0.0 22.3 %collective-permute-start.8 = (bf16[2,128,512]{2,1,0:T(8,128)(2,1)}, bf16[2,128,512]{2,1,0:T(8,128)(2,1)S(1)}, u32[]{:S(2)}, u32[]{:S(2)}) collective-permute-start(bf16[2,128,512]{2,1,0:T(8,128)(2,1)} %mine_ref.1), channel_id=1, source_target_pairs={{0,8},{8,0},{16,24},{24,16},{1,9},{9,1},{17,25},{25,17},{2,10},{10... | collective-permute-start | bytes 786440 | tf_op jit(solution)/shard_map/ppermute | solution.py:285
  0.5 9.7 %collective-permute-start.9 = (bf16[2,128,512]{2,1,0:T(8,128)(2,1)}, bf16[2,128,512]{2,1,0:T(8,128)(2,1)S(1)}, u32[]{:S(2)}, u32[]{:S(2)}) collective-permute-start(bf16[2,128,512]{2,1,0:T(8,128)(2,1)} %mine_ref.1), channel_id=1, source_target_pairs={{0,16},{8,24},{16,0},{24,8},{1,17},{9,25},{17,1},{25,9},{2,18},{10... | collective-permute-start | bytes 786440 | tf_op jit(solution)/shard_map/ppermute | solution.py:282
  3.9 3.7 %copy-start.4 = (bf16[64,512]{1,0:T(8,128)(2,1)S(1)}, bf16[64,512]{1,0:T(8,128)(2,1)}, u32[]{:S(2)}) copy-start(bf16[64,512]{1,0:T(8,128)(2,1)} %param.12) | copy-start | bytes 196612
  3.9 18.5 %copy-start.1 = (bf16[2,128,512]{2,1,0:T(8,128)(2,1)S(1)}, bf16[2,128,512]{2,1,0:T(8,128)(2,1)}, u32[]{:S(2)}) copy-start(bf16[2,128,512]{2,1,0:T(8,128)(2,1)} %mine_ref.1) | copy-start | bytes 786436
  3.9 8.8 %collective-permute-start.11 = (bf16[64,768]{1,0:T(8,128)(2,1)S(1)}, bf16[64,768]{1,0:T(8,128)(2,1)S(1)}, u32[]{:S(2)}, u32[]{:S(2)}) collective-permute-start(bf16[64,768]{1,0:T(8,128)(2,1)S(1)} %pad_maximum_fusion.1), channel_id=1, source_target_pairs={{6,0},{7,1},{4,2},{5,3},{2,4},{3,5},{0,6},{1,7},{15,8},{14,9},{13,... | collective-permute-start | bytes 294920 | tf_op jit(solution)/shard_map/ppermute | solution.py:294
  10.2 12.1 %collective-permute-start.10 = (bf16[2,128,512]{2,1,0:T(8,128)(2,1)S(1)}, bf16[2,128,512]{2,1,0:T(8,128)(2,1)S(1)}, u32[]{:S(2)}, u32[]{:S(2)}) collective-permute-start(bf16[2,128,512]{2,1,0:T(8,128)(2,1)S(1)} %collective-permute-done.9.other_ref), channel_id=1, source_target_pairs={{0,8},{8,0},{16,24},{24,16},{1,9},{9,1},{17,25},{25,17},{2,10},{10... | collective-permute-start | bytes 786440 | tf_op jit(solution)/shard_map/ppermute | solution.py:285
  10.2 12.2 %copy-start.2 = (f32[512]{0:T(512)S(1)}, f32[512]{0:T(512)}, u32[]{:S(2)}) copy-start(f32[512]{0:T(512)} %param.8) | copy-start | bytes 6148
  10.2 12.1 %copy-start.3 = (s32[2,2]{1,0:T(2,128)S(1)}, s32[2,2]{1,0:T(2,128)}, u32[]{:S(2)}) copy-start(s32[2,2]{1,0:T(2,128)} %tracks_ref.1) | copy-start | bytes 52
  10.2 5.7 %collective-permute-start.4 = (bf16[64,1024]{1,0:T(8,128)(2,1)S(1)}, bf16[64,1024]{1,0:T(8,128)(2,1)S(1)}, u32[]{:S(2)}, u32[]{:S(2)}) collective-permute-start(bf16[64,1024]{1,0:T(8,128)(2,1)S(1)} %pad_maximum_fusion.refs_0_), channel_id=1, source_target_pairs={{2,0},{3,1},{0,2},{1,3},{6,4},{7,5},{4,6},{5,7},{11,8},{10,9},{9,1... | collective-permute-start | bytes 393224 | tf_op jit(solution)/shard_map/ppermute | solution.py:294
  12.1 6.6 %collective-permute-start.6 = (bf16[64,1024]{1,0:T(8,128)(2,1)S(1)}, bf16[64,1024]{1,0:T(8,128)(2,1)S(1)}, u32[]{:S(2)}, u32[]{:S(2)}) collective-permute-start(bf16[64,1024]{1,0:T(8,128)(2,1)S(1)} %pad_maximum_fusion.refs_0_), channel_id=1, source_target_pairs={{9,8},{8,9},{11,10},{10,11},{13,12},{12,13},{15,14},{14,15},{25,24... | collective-permute-start | bytes 393224 | tf_op jit(solution)/shard_map/ppermute | solution.py:294
  12.8 6.2 %collective-permute-start.13 = (bf16[64,768]{1,0:T(8,128)(2,1)S(1)}, bf16[64,768]{1,0:T(8,128)(2,1)S(1)}, u32[]{:S(2)}, u32[]{:S(2)}) collective-permute-start(bf16[64,768]{1,0:T(8,128)(2,1)S(1)} %pad_maximum_fusion.1), channel_id=1, source_target_pairs={{4,0},{5,1},{6,2},{7,3},{0,4},{1,5},{2,6},{3,7},{13,8},{12,9},{15,... | collective-permute-start | bytes 294920 | tf_op jit(solution)/shard_map/ppermute | solution.py:294
  16.0 7.7 %collective-permute-start.5 = (bf16[64,1024]{1,0:T(8,128)(2,1)S(1)}, bf16[64,1024]{1,0:T(8,128)(2,1)S(1)}, u32[]{:S(2)}, u32[]{:S(2)}) collective-permute-start(bf16[64,1024]{1,0:T(8,128)(2,1)S(1)} %collective-permute-done.4.refs_5_), channel_id=1, source_target_pairs={{0,8},{8,0},{16,24},{24,16},{1,9},{9,1},{17,25},{25,17},{2,10},{10... | collective-permute-start | bytes 393224 | tf_op jit(solution)/shard_map/ppermute | solution.py:285
  18.7 4.9 %collective-permute-start.7 = (bf16[64,1024]{1,0:T(8,128)(2,1)S(1)}, bf16[64,1024]{1,0:T(8,128)(2,1)S(1)}, u32[]{:S(2)}, u32[]{:S(2)}) collective-permute-start(bf16[64,1024]{1,0:T(8,128)(2,1)S(1)} %collective-permute-done.6.refs_7_), channel_id=1, source_target_pairs={{0,8},{8,0},{16,24},{24,16},{1,9},{9,1},{17,25},{25,17},{2,10},{10... | collective-permute-start | bytes 393224 | tf_op jit(solution)/shard_map/ppermute | solution.py:285
  18.9 4.3 %collective-permute-start.12 = (bf16[64,768]{1,0:T(8,128)(2,1)S(1)}, bf16[64,768]{1,0:T(8,128)(2,1)S(1)}, u32[]{:S(2)}, u32[]{:S(2)}) collective-permute-start(bf16[64,768]{1,0:T(8,128)(2,1)S(1)} %collective-permute-done.11.refs_1_), channel_id=1, source_target_pairs={{0,8},{8,0},{16,24},{24,16},{1,9},{9,1},{17,25},{25,17},{2,10},{10... | collective-permute-start | bytes 294920 | tf_op jit(solution)/shard_map/ppermute | solution.py:285
  22.3 1.3 %collective-permute-start.14 = (bf16[64,768]{1,0:T(8,128)(2,1)S(1)}, bf16[64,768]{1,0:T(8,128)(2,1)S(1)}, u32[]{:S(2)}, u32[]{:S(2)}) collective-permute-start(bf16[64,768]{1,0:T(8,128)(2,1)S(1)} %collective-permute-done.13.refs_3_), channel_id=1, source_target_pairs={{0,8},{8,0},{16,24},{24,16},{1,9},{9,1},{17,25},{25,17},{2,10},{10... | collective-permute-start | bytes 294920 | tf_op jit(solution)/shard_map/ppermute | solution.py:285
  26.7 10.4 %collective-permute-start.15 = (bf16[256,512]{1,0:T(8,128)(2,1)S(1)}, bf16[256,512]{1,0:T(8,128)(2,1)S(1)}, u32[]{:S(2)}, u32[]{:S(2)}) collective-permute-start(bf16[256,512]{1,0:T(8,128)(2,1)S(1)} %shard_map.74.refs_9_), channel_id=1, source_target_pairs={{0,16},{8,24},{16,0},{24,8},{1,17},{9,25},{17,1},{25,9},{2,18},{10... | collective-permute-start | bytes 786440 | tf_op jit(solution)/shard_map/ppermute | solution.py:282
  28.3 5.8 %collective-permute-start = (bf16[64,256]{1,0:T(8,128)(2,1)S(1)}, bf16[64,256]{1,0:T(8,128)(2,1)S(1)}, u32[]{:S(2)}, u32[]{:S(2)}) collective-permute-start(bf16[64,256]{1,0:T(8,128)(2,1)S(1)} %constant_dynamic-slice_fusion), channel_id=1, source_target_pairs={{6,0},{7,1},{4,2},{5,3},{2,4},{3,5},{0,6},{1,7},{15,8},{14,9},{13,... | collective-permute-start | bytes 98312 | tf_op jit(solution)/shard_map/ppermute | solution.py:294
  30.7 4.8 %collective-permute-start.2 = (bf16[64,256]{1,0:T(8,128)(2,1)S(1)}, bf16[64,256]{1,0:T(8,128)(2,1)S(1)}, u32[]{:S(2)}, u32[]{:S(2)}) collective-permute-start(bf16[64,256]{1,0:T(8,128)(2,1)S(1)} %constant_dynamic-slice_fusion), channel_id=1, source_target_pairs={{4,0},{5,1},{6,2},{7,3},{0,4},{1,5},{2,6},{3,7},{13,8},{12,9},{15,... | collective-permute-start | bytes 98312 | tf_op jit(solution)/shard_map/ppermute | solution.py:294
  34.1 1.5 %collective-permute-start.1 = (bf16[64,256]{1,0:T(8,128)(2,1)S(1)}, bf16[64,256]{1,0:T(8,128)(2,1)S(1)}, u32[]{:S(2)}, u32[]{:S(2)}) collective-permute-start(bf16[64,256]{1,0:T(8,128)(2,1)S(1)} %collective-permute-done.refs_1_), channel_id=1, source_target_pairs={{0,8},{8,0},{16,24},{24,16},{1,9},{9,1},{17,25},{25,17},{2,10},{10... | collective-permute-start | bytes 98312 | tf_op jit(solution)/shard_map/ppermute | solution.py:285
  35.5 1.2 %collective-permute-start.3 = (bf16[64,256]{1,0:T(8,128)(2,1)S(1)}, bf16[64,256]{1,0:T(8,128)(2,1)S(1)}, u32[]{:S(2)}, u32[]{:S(2)}) collective-permute-start(bf16[64,256]{1,0:T(8,128)(2,1)S(1)} %collective-permute-done.2.refs_3_), channel_id=1, source_target_pairs={{0,8},{8,0},{16,24},{24,16},{1,9},{9,1},{17,25},{25,17},{2,10},{10... | collective-permute-start | bytes 98312 | tf_op jit(solution)/shard_map/ppermute | solution.py:285
  37.3 1.4 %collective-permute-start.16 = (bf16[128,512]{1,0:T(8,128)(2,1)S(1)}, bf16[128,512]{1,0:T(8,128)(2,1)S(1)}, u32[]{:S(2)}, u32[]{:S(2)}) collective-permute-start(bf16[128,512]{1,0:T(8,128)(2,1)S(1)} %shard_map.76), channel_id=1, source_target_pairs={{0,8},{8,0},{16,24},{24,16},{1,9},{9,1},{17,25},{25,17},{2,10},{10... | collective-permute-start | bytes 393224 | tf_op jit(solution)/shard_map/ppermute | solution.py:285

commit v4 on v3

--- a/solution.py
+++ b/solution.py
@@ -143,17 +143,16 @@
     live_ref[...] = ((position >= start) & (position < end)).astype(jnp.float32)
 
 
-def attend(below_ref, within_ref, live_ref, queries, keys, values, out_ref, first, head_dim):
+def attend(below_ref, within_ref, live_ref, queries, keys, values, out_ref, head_dim):
     steps = out_ref.shape[1]
     block = span = LANES
-    group = pl.ds(first, span)
     ratio = math.log2(math.e) / math.sqrt(head_dim)
     lane = lax.broadcasted_iota(jnp.int32, (block, span), 1)
     diagonal = lane == lax.broadcasted_iota(jnp.int32, (block, span), 0)
     diagonal = diagonal.astype(jnp.float32).astype(jnp.bfloat16)
     for j in range(steps // block):
         here = pl.ds(j * block, block)
-        query_block = queries[here, group]
+        query_block = queries[here, :]
         one = [
             jnp.where((lane >= low) & (lane < low + head_dim), query_block, jnp.zeros_like(query_block))
             for low in range(0, span, head_dim)
@@ -165,7 +164,7 @@
                 rows = pl.ds(begin, count)
                 scores.append(
                     lax.dot_general(
-                        jnp.concatenate([keys[rows, group], mask[rows, :]], axis=1),
+                        jnp.concatenate([keys[rows, :], mask[rows, :]], axis=1),
                         one,
                         (((1,), (1,)), ((), ())),
                         preferred_element_type=jnp.float32,
@@ -178,24 +177,39 @@
         total = sum(jnp.sum(w, axis=0, keepdims=True) for w in weight)
         weight = jnp.concatenate([w.astype(jnp.bfloat16) for w in weight], axis=0)
         summed = jnp.dot(
-            values[group, pl.ds(0, (j + 1) * block)], weight, preferred_element_type=jnp.float32
+            values[:, pl.ds(0, (j + 1) * block)], weight, preferred_element_type=jnp.float32
         )
         live = live_ref[:1, here] > 0.0
         for h in range(span // head_dim):
             rows, lanes = slice(h * head_dim, (h + 1) * head_dim), slice(h * block, (h + 1) * block)
             result = jnp.where(live, summed[rows, lanes] / total[:, lanes], 0.0)
-            out_ref[pl.ds(first + h * head_dim, head_dim), here] = result.astype(jnp.bfloat16)
-
-
-def place(sources, refs, target, begin, columns):
-    depth = refs[0].shape[0]
+            out_ref[pl.ds(h * head_dim, head_dim), here] = result.astype(jnp.bfloat16)
+
+
+def pack_kernel(*refs):
+    sources, out_ref, sems = refs[:-2], refs[-2], refs[-1]
+    span = out_ref.shape[1] // len(sources)
+    first = pl.multiple_of(lax.axis_index("tm") // 2 * span, span)
+    copies = [
+        pltpu.make_async_copy(
+            ref.at[:, pl.ds(first, span)], out_ref.at[:, pl.ds(n * span, span)], sems.at[n]
+        )
+        for n, ref in enumerate(sources)
+    ]
+    for copy in copies:
+        copy.start()
+    for copy in copies:
+        copy.wait()
+
+
+def place(sources, refs, target, begin):
+    depth, columns = refs[0].shape[0], target.shape[1]
     agent = lax.axis_index("agent")
     core = lax.axis_index("tm") % 2
 
     def put(ref, index):
         rows = pl.ds(pl.multiple_of(index * depth, depth), depth)
-        low = min(begin, ref.shape[1] - columns)
-        target[rows, :] = ref[:, low : low + columns]
+        target[rows, :] = ref[:, begin : begin + columns]
 
     put(refs[0], agent)
     for n, pair in enumerate(sources):
@@ -205,19 +219,24 @@
                     pl.when(core == here)(functools.partial(put, ref, agent ^ offset))
 
 
-def attention_kernel(sources, head_dim, normed_ref, below_ref, within_ref, live_ref, *refs):
-    shards = refs[: 1 + 2 * len(sources)]
-    out_ref, weights, queries, keys, values = refs[1 + 2 * len(sources) :]
+def first_kernel(sources, head_dim, normed_ref, below_ref, within_ref, live_ref, *refs):
+    shards, refs = refs[: 1 + 2 * len(sources)], refs[1 + 2 * len(sources) :]
+    out_ref, late, weights, held = refs[0], refs[1:4], refs[4], refs[5:]
     _, columns = weights.shape
     span = columns // 3
-    place(sources, shards, weights, 0, columns)
-    for n, target in enumerate((queries, keys, values)):
+    place(sources, shards, weights, 0)
+    for n in range(3):
         full = jnp.dot(
             normed_ref[...], weights[:, n * span : (n + 1) * span], preferred_element_type=jnp.float32
         )
-        target[...] = (full.T if n == 2 else full).astype(jnp.bfloat16)
-    for first in range(0, span, LANES):
-        attend(below_ref, within_ref, live_ref, queries, keys, values, out_ref, first, head_dim)
+        for m, target in enumerate((held[n], late[n])):
+            part = full[:, m * LANES : (m + 1) * LANES]
+            target[...] = (part.T if n == 2 else part).astype(jnp.bfloat16)
+    attend(below_ref, within_ref, live_ref, *held, out_ref, head_dim)
+
+
+def second_kernel(head_dim, below_ref, within_ref, live_ref, queries, keys, values, out_ref):
+    attend(below_ref, within_ref, live_ref, queries, keys, values, out_ref, head_dim)
 
 
 def transposed_dot(weight, value):
@@ -228,17 +247,25 @@
 
 def partial_kernel(sources, *refs):
     shards, refs = refs[: 1 + 2 * len(sources)], refs[1 + 2 * len(sources) :]
-    value_ref, kept_ref, given_ref, kept_weights, given_weights, weights = refs
+    here, kept_ref, given_ref, kept_weights, given_weights, weights = (
+        refs[:3],
+        *refs[3:7],
+        refs[7],
+    )
     _, columns = weights.shape
     half = columns // 2
     core, y = lax.axis_index("tm") % 2, lax.axis_index("tm") // 2
-    place(sources, shards, weights, 3 * columns, columns)
-    mine = pl.ds(pl.multiple_of(y * columns, columns), columns)
-    other = pl.ds(pl.multiple_of((y ^ 1) * columns, columns), columns)
+    place(sources, shards, weights, 3 * columns)
     for n, (ref, last) in enumerate(((kept_ref, kept_weights), (given_ref, given_weights))):
         lanes = pl.ds(pl.multiple_of((core ^ n) * half, half), half)
-        ref[...] = transposed_dot(weights[mine, lanes], value_ref[...])
-        last[...] = weights[other, lanes]
+        total = None
+        for m, value in enumerate(here):
+            group = ((y ^ (m // 2)) * 2 + m % 2) * LANES
+            rows = pl.ds(pl.multiple_of(group, LANES), LANES)
+            term = transposed_dot(weights[rows, lanes], value[...])
+            total = term if total is None else total + term
+        ref[...] = total
+        last[...] = weights[pl.ds(pl.multiple_of(((y ^ 1) * 2 + 1) * LANES, LANES), LANES), lanes]
 
 
 def given_kernel(partial_ref, weights_ref, value_ref, out_ref):
@@ -260,8 +287,7 @@
     agents_here, rows_here, width = features.shape
     return (
         n_tm == 4
-        and n_agent >= 4
-        and n_agent & (n_agent - 1) == 0
+        and n_agent == 8
         and agents_here == 2
         and width == 4 * LANES
         and LANES % (width // HEADS) == 0
@@ -276,7 +302,6 @@
     head_dim = width // HEADS
     span = width // 2
     steps = n_tm * rows_here
-    y = lax.axis_index("tm") // 2
 
     def across(value):
         return lax.ppermute(value, "tm", [(i, i ^ 2) for i in range(n_tm)])
@@ -303,28 +328,31 @@
             out_shape=[jax.ShapeDtypeStruct(shape, dtype) for shape, dtype in outs],
             in_specs=specs or [vmem] * len(args),
             out_specs=[out_spec] * len(outs),
-            scratch_shapes=[pltpu.VMEM(shape, dtype) for shape, dtype in scratch],
+            scratch_shapes=[pltpu.VMEM(*s) if isinstance(s, tuple) else s for s in scratch],
             input_output_aliases=aliases,
             compiler_params=params(),
             cost_estimate=cost(**estimate),
         )(*args)
 
     half, full = jnp.bfloat16, jnp.float32
-    pieces = [
-        lax.dynamic_slice_in_dim(w, y * span, span, 1) for w in (w_query, w_key, w_value, w_out)
-    ]
-    packed, projections, outward = jnp.concatenate(pieces, 1), jnp.concatenate(pieces[:3], 1), pieces[3]
-    evens = list(range(n_agent - 2, 0, -2))
-    odds = list(range(n_agent - 1, 0, -2))
-    sources = list(zip(evens + [None], odds))
-    near = len(sources) - 2
-    fetched = [fetch(projections if n < near else packed, pair) for n, pair in enumerate(sources)]
-    fetched_out = [fetch(outward, pair) for pair in sources[:near]]
+    (packed,) = kernel(
+        pack_kernel,
+        [((width // n_agent, 4 * span), half)],
+        tuple(
+            pltpu.with_memory_space_constraint(w, pltpu.HBM)
+            for w in (w_query, w_key, w_value, w_out)
+        ),
+        specs=[pl.BlockSpec(memory_space=pltpu.HBM)] * 4,
+        scratch=[pltpu.SemaphoreType.DMA((4,))],
+        flops=0,
+    )
+    sources = [(6, 4), (2, 3), (None, 1), (7, 5)]
+    fetched = [fetch(packed, pair) for pair in sources[:3]]
+    fetched.append(fetch(fetched[0], (1, 1)))
     other_rows = across(features)
     beside = swap(features)
     diagonal = swap(other_rows)
     swapped = [swap(value) for value in fetched]
-    swapped_out = [swap(value) for value in fetched_out]
     masks = kernel(
         norm_kernel,
         [((steps, width), half)] + [((steps, LANES), half)] * 2 + [((8, steps), full)],
@@ -333,26 +361,32 @@
         flops=8 * steps * width,
     )
     shards = [packed] + [v for pair in zip(fetched, swapped) for v in pair]
-    (attended,) = kernel(
-        functools.partial(attention_kernel, sources, head_dim),
-        [((span, steps), half)],
+    head_flops = 4 * steps * steps * LANES
+    heads = [((steps, LANES), half)] * 2 + [((LANES, steps), half)]
+    exponentials = steps * steps * LANES // head_dim
+    attended_first, *late = kernel(
+        functools.partial(first_kernel, sources, head_dim),
+        [((LANES, steps), half)] + heads,
         (*masks, *shards),
-        scratch=[((width, 3 * span), half)] + [((steps, span), half)] * 2 + [((span, steps), half)],
-        flops=6 * steps * width * span + 4 * steps * steps * span,
-        transcendentals=steps * steps * span // head_dim,
-    )
-    other = across(attended)
-    out_shards = [packed] + [
-        v
-        for pair in zip(fetched_out + fetched[near:], swapped_out + swapped[near:])
-        for v in pair
-    ]
+        scratch=[((width, 3 * span), half)] + heads,
+        flops=6 * steps * width * span + head_flops,
+        transcendentals=exponentials,
+    )
+    other_first = across(attended_first)
+    (attended_second,) = kernel(
+        functools.partial(second_kernel, head_dim),
+        [((LANES, steps), half)],
+        (*masks[1:], *late),
+        flops=head_flops,
+        transcendentals=exponentials,
+    )
+    other = across(attended_second)
     kept, given, kept_weights, given_weights = kernel(
         functools.partial(partial_kernel, sources),
-        [((span // 2, steps), full)] * 2 + [((span, span // 2), half)] * 2,
-        (*out_shards, attended),
+        [((span // 2, steps), full)] * 2 + [((LANES, span // 2), half)] * 2,
+        (*shards, attended_first, attended_second, other_first),
         scratch=[((width, span), half)],
-        flops=2 * steps * span * span,
+        flops=2 * steps * width * span,
     )
     (given,) = kernel(
         given_kernel,

time: 39.5 us -> 34.4 us (0.87)
  starting transfers between devices: 22.6 us -> 18.4 us
  waiting for transfers between devices: 9.78 us -> 8.32 us
  Pallas kernels: 5.98 us -> 7.33 us
  local copies, waits for them, and re-layouts: 0.82 us -> 0.01 us
    ppermute x6 -> x4, waiting for transfers between devices: 5.37 us -> 0.9 us  [fetch(): return lax.ppermute(value, ('tm', 'agent'), pairs)]
    ppermute x2 -> x3, waiting for transfers between devices: 2.61 us -> 6.54 us  [across(): return lax.ppermute(value, 'tm', [(i, i ^ 2) for i in range(n_tm)])]
    ppermute x6 -> x4, starting transfers between devices: 11.3 us -> 7.61 us  [fetch(): return lax.ppermute(value, ('tm', 'agent'), pairs)]
    ppermute x9 -> x7, starting transfers between devices: 7.17 us -> 5.65 us  [swap(): return lax.ppermute(value, 'tm', [(i, i ^ 1) for i in range(n_tm)])]
    pallas_call x6 -> x8, Pallas kernels: 5.98 us -> 7.33 us  [kernel(): pl.pallas_call(body, out_shape=[jax.ShapeDtypeStruct(shape, dtype) for sh...]
    ppermute x2 -> x3, starting transfers between devices: 4.16 us -> 5.15 us  [across(): return lax.ppermute(value, 'tm', [(i, i ^ 2) for i in range(n_tm)])]
    ppermute x9 -> x7, waiting for transfers between devices: 1.8 us -> 0.88 us  [swap(): return lax.ppermute(value, 'tm', [(i, i ^ 1) for i in range(n_tm)])]
    dynamic_slice x3 -> x0, local copies, waits for them, and re-layouts: 0.79 us -> none  [split_heads(): lax.dynamic_slice_in_dim(w, y * span, span, 1)]
  transfers between devices with their start and end apart: 17 -> 14, of which waited for: 7 -> 6; matrix products, arithmetic and copies ran while one was open for 2% -> 0% of each run, Pallas kernels for 5% -> 13%
where the time goes in v4:
time: 34.4 us; the launch traced here: 34.2 us
  starting transfers between devices  18.4 us (53%)
  waiting for transfers between devices  8.32 us (24%)
  Pallas kernels  7.33 us (21%)
    ppermute x4, starting transfers between devices, fetch(): return lax.ppermute(value, ('tm', 'agent'), pairs)  7.61 us
    pallas_call x8, Pallas kernels, kernel(): pl.pallas_call(body, out_shape=[jax.ShapeDtypeStruct(shape, dtype) for sh...  7.33 us
    ppermute x3, waiting for transfers between devices, across(): return lax.ppermute(value, 'tm', [(i, i ^ 2) for i in range(n_tm)])  6.54 us
    ppermute x7, starting transfers between devices, swap(): return lax.ppermute(value, 'tm', [(i, i ^ 1) for i in range(n_tm)])  5.65 us
    ppermute x3, starting transfers between devices, across(): return lax.ppermute(value, 'tm', [(i, i ^ 2) for i in range(n_tm)])  5.15 us
    ppermute x4, waiting for transfers between devices, fetch(): return lax.ppermute(value, ('tm', 'agent'), pairs)  0.9 us
    ppermute x7, waiting for transfers between devices, swap(): return lax.ppermute(value, 'tm', [(i, i ^ 1) for i in range(n_tm)])  0.88 us
  transfers between devices with their start and end apart: 14, of which 6 were waited for; matrix products, arithmetic and copies ran while one was open for 0% of the time, Pallas kernels for 13%

profile of v4, /device:TPU:0, one launch (start us, length us, event | category | flops | bytes accessed | tf_op | source)
XLA Modules:
  0.0 34.2 jit_solution(12258265579528595255)
XLA Ops:
  0.0 3.0 %collective-permute-start.9 = (bf16[2,128,512]{2,1,0:T(8,128)(2,1)}, bf16[2,128,512]{2,1,0:T(8,128)(2,1)S(1)}, u32[]{:S(2)}, u32[]{:S(2)}) collective-permute-start(bf16[2,128,512]{2,1,0:T(8,128)(2,1)} %mine_ref.1), channel_id=1, source_target_pairs={{0,16},{8,24},{16,0},{24,8},{1,17},{9,25},{17,1},{25,9},{2,18},{10... | collective-permute-start | bytes 786440 | tf_op jit(solution)/shard_map/ppermute | solution.py:307
  3.0 0.9 %shard_map.73.refs_0_ = bf16[64,1024]{1,0:T(8,128)(2,1)S(1)} custom-call(bf16[64,512]{1,0:T(8,128)(2,1)} %refs_0_.1, bf16[64,512]{1,0:T(8,128)(2,1)} %refs_1_.1, bf16[64,512]{1,0:T(8,128)(2,1)} %refs_2_.1, bf16[64,512]{1,0:T(8,128)(2,1)} %refs_3_.1), custom_call_target="tpu_custom_call" | custom-call | bytes 1048576 | tf_op jit(solution)/shard_map/pallas_call | solution.py:326
  3.9 3.7 %collective-permute-start = (bf16[64,1024]{1,0:T(8,128)(2,1)S(1)}, bf16[64,1024]{1,0:T(8,128)(2,1)S(1)}, u32[]{:S(2)}, u32[]{:S(2)}) collective-permute-start(bf16[64,1024]{1,0:T(8,128)(2,1)S(1)} %shard_map.73.refs_0_), channel_id=1, source_target_pairs={{6,0},{7,1},{4,2},{5,3},{2,4},{3,5},{0,6},{1,7},{12,8},{13,9},{14,... | collective-permute-start | bytes 393224 | tf_op jit(solution)/shard_map/ppermute | solution.py:319
  7.5 2.0 %collective-permute-done.9.other_ref = bf16[2,128,512]{2,1,0:T(8,128)(2,1)S(1)} collective-permute-done((bf16[2,128,512]{2,1,0:T(8,128)(2,1)}, bf16[2,128,512]{2,1,0:T(8,128)(2,1)S(1)}, u32[]{:S(2)}, u32[]{:S(2)}) %collective-permute-start.9) | collective-permute-done | bytes 262176 | tf_op jit(solution)/shard_map/ppermute | solution.py:307
  9.6 0.7 %collective-permute-start.4 = (bf16[64,1024]{1,0:T(8,128)(2,1)S(1)}, bf16[64,1024]{1,0:T(8,128)(2,1)S(1)}, u32[]{:S(2)}, u32[]{:S(2)}) collective-permute-start(bf16[64,1024]{1,0:T(8,128)(2,1)S(1)} %shard_map.73.refs_0_), channel_id=1, source_target_pairs={{9,8},{8,9},{11,10},{10,11},{13,12},{12,13},{15,14},{14,15},{25,24... | collective-permute-start | bytes 393224 | tf_op jit(solution)/shard_map/ppermute | solution.py:319
  10.3 1.8 %collective-permute-start.2 = (bf16[64,1024]{1,0:T(8,128)(2,1)S(1)}, bf16[64,1024]{1,0:T(8,128)(2,1)S(1)}, u32[]{:S(2)}, u32[]{:S(2)}) collective-permute-start(bf16[64,1024]{1,0:T(8,128)(2,1)S(1)} %shard_map.73.refs_0_), channel_id=1, source_target_pairs={{2,0},{3,1},{0,2},{1,3},{6,4},{7,5},{4,6},{5,7},{11,8},{10,9},{9,1... | collective-permute-start | bytes 393224 | tf_op jit(solution)/shard_map/ppermute | solution.py:319
  12.0 1.5 %collective-permute-start.6 = (bf16[64,1024]{1,0:T(8,128)(2,1)S(1)}, bf16[64,1024]{1,0:T(8,128)(2,1)S(1)}, u32[]{:S(2)}, u32[]{:S(2)}) collective-permute-start(bf16[64,1024]{1,0:T(8,128)(2,1)S(1)} %collective-permute-done.refs_1_), channel_id=1, source_target_pairs={{1,0},{0,1},{3,2},{2,3},{5,4},{4,5},{7,6},{6,7},{9,8},{8,9},{11,10... | collective-permute-start | bytes 393224 | tf_op jit(solution)/shard_map/ppermute | solution.py:319
  13.5 3.5 %collective-permute-start.1 = (bf16[64,1024]{1,0:T(8,128)(2,1)S(1)}, bf16[64,1024]{1,0:T(8,128)(2,1)S(1)}, u32[]{:S(2)}, u32[]{:S(2)}) collective-permute-start(bf16[64,1024]{1,0:T(8,128)(2,1)S(1)} %collective-permute-done.refs_1_), channel_id=1, source_target_pairs={{0,8},{8,0},{16,24},{24,16},{1,9},{9,1},{17,25},{25,17},{2,10},{10... | collective-permute-start | bytes 393224 | tf_op jit(solution)/shard_map/ppermute | solution.py:310
  17.0 1.2 %collective-permute-start.5 = (bf16[64,1024]{1,0:T(8,128)(2,1)S(1)}, bf16[64,1024]{1,0:T(8,128)(2,1)S(1)}, u32[]{:S(2)}, u32[]{:S(2)}) collective-permute-start(bf16[64,1024]{1,0:T(8,128)(2,1)S(1)} %collective-permute-done.4.refs_5_), channel_id=1, source_target_pairs={{0,8},{8,0},{16,24},{24,16},{1,9},{9,1},{17,25},{25,17},{2,10},{10... | collective-permute-start | bytes 393224 | tf_op jit(solution)/shard_map/ppermute | solution.py:310
  18.2 0.9 %collective-permute-done.6.refs_7_ = bf16[64,1024]{1,0:T(8,128)(2,1)S(1)} collective-permute-done((bf16[64,1024]{1,0:T(8,128)(2,1)S(1)}, bf16[64,1024]{1,0:T(8,128)(2,1)S(1)}, u32[]{:S(2)}, u32[]{:S(2)}) %collective-permute-start.6) | collective-permute-done | bytes 131104 | tf_op jit(solution)/shard_map/ppermute | solution.py:319
  19.1 0.9 %collective-permute-start.3 = (bf16[64,1024]{1,0:T(8,128)(2,1)S(1)}, bf16[64,1024]{1,0:T(8,128)(2,1)S(1)}, u32[]{:S(2)}, u32[]{:S(2)}) collective-permute-start(bf16[64,1024]{1,0:T(8,128)(2,1)S(1)} %collective-permute-done.2.refs_3_), channel_id=1, source_target_pairs={{0,8},{8,0},{16,24},{24,16},{1,9},{9,1},{17,25},{25,17},{2,10},{10... | collective-permute-start | bytes 393224 | tf_op jit(solution)/shard_map/ppermute | solution.py:310
  20.0 0.9 %shard_map.74 = (bf16[512,512]{1,0:T(8,128)(2,1)S(1)}, bf16[512,128]{1,0:T(8,128)(2,1)S(1)}, bf16[512,128]{1,0:T(8,128)(2,1)S(1)}, f32[8,512]{1,0:T(8,128)S(1)}) custom-call(s32[2,2]{1,0:T(2,128)S(1)} %copy-done.2, f32[1,512]{1,0:T(1,128)S(1)} %bitcast.1, bf16[2,128,512]{2,1,0:T(8,128)(2,1)S(1)} %copy-done, ...), custom_call_target="tpu_custom_call" | custom-call | flops 2097152 | bytes 1048576 | tf_op jit(solution)/shard_map/pallas_call | solution.py:326
  21.0 0.4 %collective-permute-done.7.refs_8_ = bf16[64,1024]{1,0:T(8,128)(2,1)S(1)} collective-permute-done((bf16[64,1024]{1,0:T(8,128)(2,1)S(1)}, bf16[64,1024]{1,0:T(8,128)(2,1)S(1)}, u32[]{:S(2)}, u32[]{:S(2)}) %collective-permute-start.7) | collective-permute-done | bytes 131104 | tf_op jit(solution)/shard_map/ppermute | solution.py:310
  21.4 2.0 %shard_map.75 = (bf16[128,512]{1,0:T(8,128)(2,1)S(1)}, bf16[512,128]{1,0:T(8,128)(2,1)S(1)}, bf16[512,128]{1,0:T(8,128)(2,1)S(1)}, bf16[128,512]{1,0:T(8,128)(2,1)S(1)}) custom-call(bf16[512,512]{1,0:T(8,128)(2,1)S(1)} %get-tuple-element.17.normed_ref, bf16[512,128]{1,0:T(8,128)(2,1)S(1)} %get-tuple-element.18.below_ref, ...), custom_call_target="tpu_custom_call" | custom-call | flops 536870912 | bytes 1048576 | tf_op jit(solution)/shard_map/pallas_call | solution.py:326
  23.4 1.7 %collective-permute-start.11 = (bf16[128,512]{1,0:T(8,128)(2,1)S(1)}, bf16[128,512]{1,0:T(8,128)(2,1)S(1)}, u32[]{:S(2)}, u32[]{:S(2)}) collective-permute-start(bf16[128,512]{1,0:T(8,128)(2,1)S(1)} %get-tuple-element.21.refs_9_), channel_id=1, source_target_pairs={{0,16},{8,24},{16,0},{24,8},{1,17},{9,25},{17,1},{25,9},{2,18},{10... | collective-permute-start | bytes 393224 | tf_op jit(solution)/shard_map/ppermute | solution.py:307
  25.1 1.4 %shard_map.76.refs_10_ = bf16[128,512]{1,0:T(8,128)(2,1)S(1)} custom-call(bf16[512,128]{1,0:T(8,128)(2,1)S(1)} %get-tuple-element.18.below_ref, bf16[512,128]{1,0:T(8,128)(2,1)S(1)} %get-tuple-element.19.within_ref, f32[8,512]{1,0:T(8,128)S(1)} %get-tuple-element.20.live_ref, bf16[512,128]{1,0:T(8,128)(2,1)S(1)} %get-tuple-element.22.queries, ...), custom_call_target="tpu_custom_call" | custom-call | flops 134217728 | bytes 1048576 | tf_op jit(solution)/shard_map/pallas_call | solution.py:326
  26.5 0.4 %collective-permute-start.12 = (bf16[128,512]{1,0:T(8,128)(2,1)S(1)}, bf16[128,512]{1,0:T(8,128)(2,1)S(1)}, u32[]{:S(2)}, u32[]{:S(2)}) collective-permute-start(bf16[128,512]{1,0:T(8,128)(2,1)S(1)} %shard_map.76.refs_10_), channel_id=1, source_target_pairs={{0,16},{8,24},{16,0},{24,8},{1,17},{9,25},{17,1},{25,9},{2,18},{10... | collective-permute-start | bytes 393224 | tf_op jit(solution)/shard_map/ppermute | solution.py:307
  26.9 2.1 %collective-permute-done.11.refs_11_ = bf16[128,512]{1,0:T(8,128)(2,1)S(1)} collective-permute-done((bf16[128,512]{1,0:T(8,128)(2,1)S(1)}, bf16[128,512]{1,0:T(8,128)(2,1)S(1)}, u32[]{:S(2)}, u32[]{:S(2)}) %collective-permute-start.11) | collective-permute-done | bytes 131104 | tf_op jit(solution)/shard_map/ppermute | solution.py:307
  29.0 0.4 %shard_map.77 = (f32[128,512]{1,0:T(8,128)S(1)}, f32[128,512]{1,0:T(8,128)S(1)}, bf16[128,128]{1,0:T(8,128)(2,1)S(1)}, bf16[128,128]{1,0:T(8,128)(2,1)S(1)}) custom-call(bf16[64,1024]{1,0:T(8,128)(2,1)S(1)} %shard_map.73.refs_0_, bf16[64,1024]{1,0:T(8,128)(2,1)S(1)} %collective-permute-done.refs_1_, bf16[64,1024]{1,0:T(8,128)(2,1)S(1)} %collective-permute-done.1.refs_2_, ...), custom_call_target="tpu_custom_call" | custom-call | flops 134217728 | bytes 1048576 | tf_op jit(solution)/shard_map/pallas_call | solution.py:326
  29.5 2.4 %collective-permute-done.12.value_ref = bf16[128,512]{1,0:T(8,128)(2,1)S(1)} collective-permute-done((bf16[128,512]{1,0:T(8,128)(2,1)S(1)}, bf16[128,512]{1,0:T(8,128)(2,1)S(1)}, u32[]{:S(2)}, u32[]{:S(2)}) %collective-permute-start.12) | collective-permute-done | bytes 131104 | tf_op jit(solution)/shard_map/ppermute | solution.py:307
  31.9 0.2 shard_map.78
  32.2 0.9 %shard_map.79.started_ref = bf16[2,128,512]{2,1,0:T(8,128)(2,1)} custom-call(f32[128,512]{1,0:T(8,128)S(1)} %get-tuple-element.27.partial_ref, bf16[128,128]{1,0:T(8,128)(2,1)S(1)} %get-tuple-element.28.weights_ref, bf16[128,512]{1,0:T(8,128)(2,1)S(1)} %collective-permute-done.12.value_ref), custom_call_target="tpu_custom_call" | custom-call | flops 33554432 | bytes 1048576 | tf_op jit(solution)/shard_map/pallas_call | solution.py:326
  33.0 0.5 %collective-permute-done.13.received_ref = bf16[128,512]{1,0:T(8,128)(2,1)S(1)} collective-permute-done((bf16[128,512]{1,0:T(8,128)(2,1)S(1)}, bf16[128,512]{1,0:T(8,128)(2,1)S(1)}, u32[]{:S(2)}, u32[]{:S(2)}) %collective-permute-start.13) | collective-permute-done | bytes 131104 | tf_op jit(solution)/shard_map/ppermute | solution.py:310
  33.5 0.7 %shard_map.80 = bf16[2,128,512]{2,1,0:T(8,128)(2,1)} custom-call(bf16[128,512]{1,0:T(8,128)(2,1)S(1)} %collective-permute-done.13.received_ref, bf16[2,128,512]{2,1,0:T(8,128)(2,1)} %shard_map.79.started_ref), custom_call_target="tpu_custom_call", output_to_operand_aliasing={{}: (1, {})} | custom-call | bytes 1048576 | tf_op jit(solution)/shard_map/pallas_call | solution.py:326
  (18 shorter events, 0.2 us)
Async XLA Ops:
  0.0 7.5 %copy-start = (bf16[2,128,512]{2,1,0:T(8,128)(2,1)S(1)}, bf16[2,128,512]{2,1,0:T(8,128)(2,1)}, u32[]{:S(2)}) copy-start(bf16[2,128,512]{2,1,0:T(8,128)(2,1)} %mine_ref.1) | copy-start | bytes 786436
  0.0 9.6 %collective-permute-start.9 = (bf16[2,128,512]{2,1,0:T(8,128)(2,1)}, bf16[2,128,512]{2,1,0:T(8,128)(2,1)S(1)}, u32[]{:S(2)}, u32[]{:S(2)}) collective-permute-start(bf16[2,128,512]{2,1,0:T(8,128)(2,1)} %mine_ref.1), channel_id=1, source_target_pairs={{0,16},{8,24},{16,0},{24,8},{1,17},{9,25},{17,1},{25,9},{2,18},{10... | collective-permute-start | bytes 786440 | tf_op jit(solution)/shard_map/ppermute | solution.py:307
  3.0 17.0 %copy-start.1 = (f32[512]{0:T(512)S(1)}, f32[512]{0:T(512)}, u32[]{:S(2)}) copy-start(f32[512]{0:T(512)} %param.8) | copy-start | bytes 6148
  3.9 16.2 %copy-start.2 = (s32[2,2]{1,0:T(2,128)S(1)}, s32[2,2]{1,0:T(2,128)}, u32[]{:S(2)}) copy-start(s32[2,2]{1,0:T(2,128)} %tracks_ref.1) | copy-start | bytes 52
  3.9 8.2 %collective-permute-start = (bf16[64,1024]{1,0:T(8,128)(2,1)S(1)}, bf16[64,1024]{1,0:T(8,128)(2,1)S(1)}, u32[]{:S(2)}, u32[]{:S(2)}) collective-permute-start(bf16[64,1024]{1,0:T(8,128)(2,1)S(1)} %shard_map.73.refs_0_), channel_id=1, source_target_pairs={{6,0},{7,1},{4,2},{5,3},{2,4},{3,5},{0,6},{1,7},{12,8},{13,9},{14,... | collective-permute-start | bytes 393224 | tf_op jit(solution)/shard_map/ppermute | solution.py:319
  7.5 12.5 %collective-permute-start.8 = (bf16[2,128,512]{2,1,0:T(8,128)(2,1)S(1)}, bf16[2,128,512]{2,1,0:T(8,128)(2,1)S(1)}, u32[]{:S(2)}, u32[]{:S(2)}) collective-permute-start(bf16[2,128,512]{2,1,0:T(8,128)(2,1)S(1)} %copy-done), channel_id=1, source_target_pairs={{0,8},{8,0},{16,24},{24,16},{1,9},{9,1},{17,25},{25,17},{2,10},{10... | collective-permute-start | bytes 786440 | tf_op jit(solution)/shard_map/ppermute | solution.py:310
  9.6 10.4 %collective-permute-start.10 = (bf16[2,128,512]{2,1,0:T(8,128)(2,1)S(1)}, bf16[2,128,512]{2,1,0:T(8,128)(2,1)S(1)}, u32[]{:S(2)}, u32[]{:S(2)}) collective-permute-start(bf16[2,128,512]{2,1,0:T(8,128)(2,1)S(1)} %collective-permute-done.9.other_ref), channel_id=1, source_target_pairs={{0,8},{8,0},{16,24},{24,16},{1,9},{9,1},{17,25},{25,17},{2,10},{10... | collective-permute-start | bytes 786440 | tf_op jit(solution)/shard_map/ppermute | solution.py:310
  9.6 4.0 %collective-permute-start.4 = (bf16[64,1024]{1,0:T(8,128)(2,1)S(1)}, bf16[64,1024]{1,0:T(8,128)(2,1)S(1)}, u32[]{:S(2)}, u32[]{:S(2)}) collective-permute-start(bf16[64,1024]{1,0:T(8,128)(2,1)S(1)} %shard_map.73.refs_0_), channel_id=1, source_target_pairs={{9,8},{8,9},{11,10},{10,11},{13,12},{12,13},{15,14},{14,15},{25,24... | collective-permute-start | bytes 393224 | tf_op jit(solution)/shard_map/ppermute | solution.py:319
  10.3 6.8 %collective-permute-start.2 = (bf16[64,1024]{1,0:T(8,128)(2,1)S(1)}, bf16[64,1024]{1,0:T(8,128)(2,1)S(1)}, u32[]{:S(2)}, u32[]{:S(2)}) collective-permute-start(bf16[64,1024]{1,0:T(8,128)(2,1)S(1)} %shard_map.73.refs_0_), channel_id=1, source_target_pairs={{2,0},{3,1},{0,2},{1,3},{6,4},{7,5},{4,6},{5,7},{11,8},{10,9},{9,1... | collective-permute-start | bytes 393224 | tf_op jit(solution)/shard_map/ppermute | solution.py:319
  12.0 7.1 %collective-permute-start.6 = (bf16[64,1024]{1,0:T(8,128)(2,1)S(1)}, bf16[64,1024]{1,0:T(8,128)(2,1)S(1)}, u32[]{:S(2)}, u32[]{:S(2)}) collective-permute-start(bf16[64,1024]{1,0:T(8,128)(2,1)S(1)} %collective-permute-done.refs_1_), channel_id=1, source_target_pairs={{1,0},{0,1},{3,2},{2,3},{5,4},{4,5},{7,6},{6,7},{9,8},{8,9},{11,10... | collective-permute-start | bytes 393224 | tf_op jit(solution)/shard_map/ppermute | solution.py:319
  13.5 7.5 %collective-permute-start.1 = (bf16[64,1024]{1,0:T(8,128)(2,1)S(1)}, bf16[64,1024]{1,0:T(8,128)(2,1)S(1)}, u32[]{:S(2)}, u32[]{:S(2)}) collective-permute-start(bf16[64,1024]{1,0:T(8,128)(2,1)S(1)} %collective-permute-done.refs_1_), channel_id=1, source_target_pairs={{0,8},{8,0},{16,24},{24,16},{1,9},{9,1},{17,25},{25,17},{2,10},{10... | collective-permute-start | bytes 393224 | tf_op jit(solution)/shard_map/ppermute | solution.py:310
  17.0 3.9 %collective-permute-start.5 = (bf16[64,1024]{1,0:T(8,128)(2,1)S(1)}, bf16[64,1024]{1,0:T(8,128)(2,1)S(1)}, u32[]{:S(2)}, u32[]{:S(2)}) collective-permute-start(bf16[64,1024]{1,0:T(8,128)(2,1)S(1)} %collective-permute-done.4.refs_5_), channel_id=1, source_target_pairs={{0,8},{8,0},{16,24},{24,16},{1,9},{9,1},{17,25},{25,17},{2,10},{10... | collective-permute-start | bytes 393224 | tf_op jit(solution)/shard_map/ppermute | solution.py:310
  19.1 1.9 %collective-permute-start.3 = (bf16[64,1024]{1,0:T(8,128)(2,1)S(1)}, bf16[64,1024]{1,0:T(8,128)(2,1)S(1)}, u32[]{:S(2)}, u32[]{:S(2)}) collective-permute-start(bf16[64,1024]{1,0:T(8,128)(2,1)S(1)} %collective-permute-done.2.refs_3_), channel_id=1, source_target_pairs={{0,8},{8,0},{16,24},{24,16},{1,9},{9,1},{17,25},{25,17},{2,10},{10... | collective-permute-start | bytes 393224 | tf_op jit(solution)/shard_map/ppermute | solution.py:310
  20.0 1.3 %collective-permute-start.7 = (bf16[64,1024]{1,0:T(8,128)(2,1)S(1)}, bf16[64,1024]{1,0:T(8,128)(2,1)S(1)}, u32[]{:S(2)}, u32[]{:S(2)}) collective-permute-start(bf16[64,1024]{1,0:T(8,128)(2,1)S(1)} %collective-permute-done.6.refs_7_), channel_id=1, source_target_pairs={{0,8},{8,0},{16,24},{24,16},{1,9},{9,1},{17,25},{25,17},{2,10},{10... | collective-permute-start | bytes 393224 | tf_op jit(solution)/shard_map/ppermute | solution.py:310
  23.4 5.6 %collective-permute-start.11 = (bf16[128,512]{1,0:T(8,128)(2,1)S(1)}, bf16[128,512]{1,0:T(8,128)(2,1)S(1)}, u32[]{:S(2)}, u32[]{:S(2)}) collective-permute-start(bf16[128,512]{1,0:T(8,128)(2,1)S(1)} %get-tuple-element.21.refs_9_), channel_id=1, source_target_pairs={{0,16},{8,24},{16,0},{24,8},{1,17},{9,25},{17,1},{25,9},{2,18},{10... | collective-permute-start | bytes 393224 | tf_op jit(solution)/shard_map/ppermute | solution.py:307
  26.5 5.4 %collective-permute-start.12 = (bf16[128,512]{1,0:T(8,128)(2,1)S(1)}, bf16[128,512]{1,0:T(8,128)(2,1)S(1)}, u32[]{:S(2)}, u32[]{:S(2)}) collective-permute-start(bf16[128,512]{1,0:T(8,128)(2,1)S(1)} %shard_map.76.refs_10_), channel_id=1, source_target_pairs={{0,16},{8,24},{16,0},{24,8},{1,17},{9,25},{17,1},{25,9},{2,18},{10... | collective-permute-start | bytes 393224 | tf_op jit(solution)/shard_map/ppermute | solution.py:307
  32.1 1.4 %collective-permute-start.13 = (bf16[128,512]{1,0:T(8,128)(2,1)S(1)}, bf16[128,512]{1,0:T(8,128)(2,1)S(1)}, u32[]{:S(2)}, u32[]{:S(2)}) collective-permute-start(bf16[128,512]{1,0:T(8,128)(2,1)S(1)} %shard_map.78), channel_id=1, source_target_pairs={{0,8},{8,0},{16,24},{24,16},{1,9},{9,1},{17,25},{25,17},{2,10},{10... | collective-permute-start | bytes 393224 | tf_op jit(solution)/shard_map/ppermute | solution.py:310

commit v5 on v4

--- a/solution.py
+++ b/solution.py
@@ -123,7 +123,7 @@
 
 
 def norm_kernel(tracks_ref, gain_ref, mine_ref, beside_ref, other_ref, diagonal_ref, *outs):
-    normed_ref, below_ref, within_ref, live_ref = outs
+    normed_ref, bounds_ref = outs
     rows_here = mine_ref.shape[1]
     tm = lax.axis_index("tm")
     core = tm % 2
@@ -131,70 +131,73 @@
     for k, ref in enumerate((mine_ref, beside_ref, other_ref, diagonal_ref)):
         rows = pl.ds(pl.multiple_of((tm ^ k) * rows_here, rows_here), rows_here)
         normed_ref[rows, :] = normalize(ref[core], gain)
-    start, end = tracks_ref[core, 0], tracks_ref[core, 1]
-    steps, block = below_ref.shape
-    key_pos = lax.broadcasted_iota(jnp.int32, (steps, block), 0)
-    column = lax.broadcasted_iota(jnp.int32, (steps, block), 1)
-    early = key_pos < start
-    barred = early | (lax.rem(key_pos, block) > column)
-    below_ref[...] = jnp.where(early, NEGATIVE, 0.0).astype(below_ref.dtype)
-    within_ref[...] = jnp.where(barred, NEGATIVE, 0.0).astype(within_ref.dtype)
-    position = lax.broadcasted_iota(jnp.int32, live_ref.shape, 1)
-    live_ref[...] = ((position >= start) & (position < end)).astype(jnp.float32)
-
-
-def attend(below_ref, within_ref, live_ref, queries, keys, values, out_ref, head_dim):
+    for n in range(2):
+        bounds_ref[n] = jnp.full(bounds_ref.shape[1:], tracks_ref[core, n], jnp.int32)
+
+
+def attend(bounds_ref, queries, keys, values, out_ref, head_dim):
     steps = out_ref.shape[1]
     block = span = LANES
+    heads = span // head_dim
     ratio = math.log2(math.e) / math.sqrt(head_dim)
+    start, end = bounds_ref[0, :1, :block], bounds_ref[1, :1, :block]
     lane = lax.broadcasted_iota(jnp.int32, (block, span), 1)
-    diagonal = lane == lax.broadcasted_iota(jnp.int32, (block, span), 0)
-    diagonal = diagonal.astype(jnp.float32).astype(jnp.bfloat16)
-    for j in range(steps // block):
-        here = pl.ds(j * block, block)
-        query_block = queries[here, :]
+
+    def score(j):
+        query_block = queries[pl.ds(j * block, block), :]
         one = [
             jnp.where((lane >= low) & (lane < low + head_dim), query_block, jnp.zeros_like(query_block))
             for low in range(0, span, head_dim)
         ]
-        one = jnp.concatenate([jnp.concatenate([o, diagonal], axis=1) for o in one], axis=0)
-        scores = []
-        for begin, count, mask in ((0, j * block, below_ref), (j * block, block, within_ref)):
-            if count:
-                rows = pl.ds(begin, count)
-                scores.append(
-                    lax.dot_general(
-                        jnp.concatenate([keys[rows, :], mask[rows, :]], axis=1),
-                        one,
-                        (((1,), (1,)), ((), ())),
-                        preferred_element_type=jnp.float32,
-                    )
-                )
-        highest = functools.reduce(
-            jnp.maximum, [jnp.max(score, axis=0, keepdims=True) for score in scores]
-        )
-        weight = [jnp.exp2((score - highest) * ratio) for score in scores]
-        total = sum(jnp.sum(w, axis=0, keepdims=True) for w in weight)
-        weight = jnp.concatenate([w.astype(jnp.bfloat16) for w in weight], axis=0)
+        return lax.dot_general(
+            keys[pl.ds(0, (j + 1) * block), :],
+            jnp.concatenate(one, axis=0),
+            (((1,), (1,)), ((), ())),
+            preferred_element_type=jnp.float32,
+        )
+
+    def weigh(j, scores):
+        reach = (j + 1) * block
+        key_pos = lax.broadcasted_iota(jnp.int32, (reach, block), 0)
+        query_pos = j * block + lax.broadcasted_iota(jnp.int32, (reach, block), 1)
+        allowed = (key_pos >= start) & (key_pos <= query_pos)
+        scores = jnp.where(jnp.concatenate([allowed] * heads, axis=1), scores, NEGATIVE)
+        highest = jnp.max(scores, axis=0, keepdims=True)
+        weight = jnp.exp2((scores - highest) * ratio)
+        return weight.astype(jnp.bfloat16), jnp.sum(weight, axis=0, keepdims=True)
+
+    def finish(j, weight, total):
         summed = jnp.dot(
             values[:, pl.ds(0, (j + 1) * block)], weight, preferred_element_type=jnp.float32
         )
-        live = live_ref[:1, here] > 0.0
-        for h in range(span // head_dim):
+        column = j * block + lax.broadcasted_iota(jnp.int32, (1, block), 1)
+        live = (column >= start) & (column < end)
+        for h in range(heads):
             rows, lanes = slice(h * head_dim, (h + 1) * head_dim), slice(h * block, (h + 1) * block)
             result = jnp.where(live, summed[rows, lanes] / total[:, lanes], 0.0)
-            out_ref[pl.ds(h * head_dim, head_dim), here] = result.astype(jnp.bfloat16)
+            out_ref[rows, pl.ds(j * block, block)] = result.astype(jnp.bfloat16)
+
+    blocks = steps // block
+    scores, weights = {}, {}
+    for j in range(blocks + 2):
+        if j < blocks:
+            scores[j] = score(j)
+        if 0 <= j - 1 < blocks:
+            weights[j - 1] = weigh(j - 1, scores.pop(j - 1))
+        if j >= 2:
+            finish(j - 2, *weights.pop(j - 2))
 
 
 def pack_kernel(*refs):
-    sources, out_ref, sems = refs[:-2], refs[-2], refs[-1]
-    span = out_ref.shape[1] // len(sources)
+    sources, outs, sems = refs[:4], refs[4:7], refs[7]
+    span = outs[2].shape[1]
     first = pl.multiple_of(lax.axis_index("tm") // 2 * span, span)
+    parts = [(n, 0, n) for n in range(4)] + [(n, 1, n) for n in range(3)] + [(3, 2, 0)]
     copies = [
         pltpu.make_async_copy(
-            ref.at[:, pl.ds(first, span)], out_ref.at[:, pl.ds(n * span, span)], sems.at[n]
-        )
-        for n, ref in enumerate(sources)
+            sources[n].at[:, pl.ds(first, span)], outs[o].at[:, pl.ds(m * span, span)], sems.at[k]
+        )
+        for k, (n, o, m) in enumerate(parts)
     ]
     for copy in copies:
         copy.start()
@@ -209,7 +212,8 @@
 
     def put(ref, index):
         rows = pl.ds(pl.multiple_of(index * depth, depth), depth)
-        target[rows, :] = ref[:, begin : begin + columns]
+        low = min(begin, ref.shape[1] - columns)
+        target[rows, :] = ref[:, low : low + columns]
 
     put(refs[0], agent)
     for n, pair in enumerate(sources):
@@ -219,7 +223,7 @@
                     pl.when(core == here)(functools.partial(put, ref, agent ^ offset))
 
 
-def first_kernel(sources, head_dim, normed_ref, below_ref, within_ref, live_ref, *refs):
+def first_kernel(sources, head_dim, bounds_ref, normed_ref, *refs):
     shards, refs = refs[: 1 + 2 * len(sources)], refs[1 + 2 * len(sources) :]
     out_ref, late, weights, held = refs[0], refs[1:4], refs[4], refs[5:]
     _, columns = weights.shape
@@ -232,11 +236,11 @@
         for m, target in enumerate((held[n], late[n])):
             part = full[:, m * LANES : (m + 1) * LANES]
             target[...] = (part.T if n == 2 else part).astype(jnp.bfloat16)
-    attend(below_ref, within_ref, live_ref, *held, out_ref, head_dim)
-
-
-def second_kernel(head_dim, below_ref, within_ref, live_ref, queries, keys, values, out_ref):
-    attend(below_ref, within_ref, live_ref, queries, keys, values, out_ref, head_dim)
+    attend(bounds_ref, *held, out_ref, head_dim)
+
+
+def second_kernel(head_dim, bounds_ref, queries, keys, values, out_ref):
+    attend(bounds_ref, queries, keys, values, out_ref, head_dim)
 
 
 def transposed_dot(weight, value):
@@ -335,27 +339,30 @@
         )(*args)
 
     half, full = jnp.bfloat16, jnp.float32
-    (packed,) = kernel(
+    packed, projections, outward = kernel(
         pack_kernel,
-        [((width // n_agent, 4 * span), half)],
+        [((width // n_agent, n * span), half) for n in (4, 3, 1)],
         tuple(
             pltpu.with_memory_space_constraint(w, pltpu.HBM)
             for w in (w_query, w_key, w_value, w_out)
         ),
         specs=[pl.BlockSpec(memory_space=pltpu.HBM)] * 4,
-        scratch=[pltpu.SemaphoreType.DMA((4,))],
+        scratch=[pltpu.SemaphoreType.DMA((8,))],
         flops=0,
     )
     sources = [(6, 4), (2, 3), (None, 1), (7, 5)]
-    fetched = [fetch(packed, pair) for pair in sources[:3]]
+    fetched = [fetch(packed if n else projections, pair) for n, pair in enumerate(sources[:3])]
     fetched.append(fetch(fetched[0], (1, 1)))
+    out_far = fetch(outward, sources[0])
+    out_shards = [out_far, *fetched[1:3], fetch(out_far, (1, 1))]
     other_rows = across(features)
     beside = swap(features)
     diagonal = swap(other_rows)
     swapped = [swap(value) for value in fetched]
-    masks = kernel(
+    swapped_out = [swap(out_shards[0]), *swapped[1:3], swap(out_shards[3])]
+    normed, bounds = kernel(
         norm_kernel,
-        [((steps, width), half)] + [((steps, LANES), half)] * 2 + [((8, steps), full)],
+        [((steps, width), half), ((2, 8, LANES), jnp.int32)],
         (tracks, norm_gain.reshape(1, width), features, beside, other_rows, diagonal),
         specs=[smem] + [vmem] * 5,
         flops=8 * steps * width,
@@ -367,7 +374,7 @@
     attended_first, *late = kernel(
         functools.partial(first_kernel, sources, head_dim),
         [((LANES, steps), half)] + heads,
-        (*masks, *shards),
+        (bounds, normed, *shards),
         scratch=[((width, 3 * span), half)] + heads,
         flops=6 * steps * width * span + head_flops,
         transcendentals=exponentials,
@@ -376,15 +383,16 @@
     (attended_second,) = kernel(
         functools.partial(second_kernel, head_dim),
         [((LANES, steps), half)],
-        (*masks[1:], *late),
+        (bounds, *late),
         flops=head_flops,
         transcendentals=exponentials,
     )
     other = across(attended_second)
+    out_shards = [packed] + [v for pair in zip(out_shards, swapped_out) for v in pair]
     kept, given, kept_weights, given_weights = kernel(
         functools.partial(partial_kernel, sources),
         [((span // 2, steps), full)] * 2 + [((LANES, span // 2), half)] * 2,
-        (*shards, attended_first, attended_second, other_first),
+        (*out_shards, attended_first, attended_second, other_first),
         scratch=[((width, span), half)],
         flops=2 * steps * width * span,
     )

time: 34.4 us -> 38.8 us (1.13)
  starting transfers between devices: 18.4 us -> 21.4 us
  waiting for transfers between devices: 8.32 us -> 10.8 us
  Pallas kernels: 7.33 us -> 6.2 us
    ppermute x4 -> x6, waiting for transfers between devices: 0.9 us -> 6.91 us  [fetch(): return lax.ppermute(value, ('tm', 'agent'), pairs)]
    ppermute x3, waiting for transfers between devices: 6.54 us -> 1.91 us  [across(): return lax.ppermute(value, 'tm', [(i, i ^ 2) for i in range(n_tm)])]
    ppermute x4 -> x6, starting transfers between devices: 7.61 us -> 12.1 us  [fetch(): return lax.ppermute(value, ('tm', 'agent'), pairs)]
    ppermute x7 -> x9, starting transfers between devices: 5.65 us -> 4.12 us  [swap(): return lax.ppermute(value, 'tm', [(i, i ^ 1) for i in range(n_tm)])]
    pallas_call x8, Pallas kernels: 7.33 us -> 6.2 us  [kernel(): pl.pallas_call(body, out_shape=[jax.ShapeDtypeStruct(shape, dtype) for sh...]
    ppermute x7 -> x9, waiting for transfers between devices: 0.88 us -> 2 us  [swap(): return lax.ppermute(value, 'tm', [(i, i ^ 1) for i in range(n_tm)])]
  transfers between devices with their start and end apart: 14 -> 18, of which waited for: 6 -> 8; matrix products, arithmetic and copies ran while one was open for 0% -> 0% of each run, Pallas kernels for 13% -> 10%
where the time goes in v5:
time: 38.8 us; the launch traced here: 38.6 us
  starting transfers between devices  21.4 us (55%)
  waiting for transfers between devices  10.8 us (28%)
  Pallas kernels  6.2 us (16%)
    ppermute x6, starting transfers between devices, fetch(): return lax.ppermute(value, ('tm', 'agent'), pairs)  12.1 us
    ppermute x6, waiting for transfers between devices, fetch(): return lax.ppermute(value, ('tm', 'agent'), pairs)  6.91 us
    pallas_call x8, Pallas kernels, kernel(): pl.pallas_call(body, out_shape=[jax.ShapeDtypeStruct(shape, dtype) for sh...  6.2 us
    ppermute x3, starting transfers between devices, across(): return lax.ppermute(value, 'tm', [(i, i ^ 2) for i in range(n_tm)])  5.15 us
    ppermute x9, starting transfers between devices, swap(): return lax.ppermute(value, 'tm', [(i, i ^ 1) for i in range(n_tm)])  4.12 us
    ppermute x9, waiting for transfers between devices, swap(): return lax.ppermute(value, 'tm', [(i, i ^ 1) for i in range(n_tm)])  2 us
    ppermute x3, waiting for transfers between devices, across(): return lax.ppermute(value, 'tm', [(i, i ^ 2) for i in range(n_tm)])  1.91 us
  transfers between devices with their start and end apart: 18, of which 8 were waited for; matrix products, arithmetic and copies ran while one was open for 0% of the time, Pallas kernels for 10%

profile of v5, /device:TPU:0, one launch (start us, length us, event | category | flops | bytes accessed | tf_op | source)
XLA Modules:
  0.0 38.6 jit_solution(13450597461990154601)
XLA Ops:
  0.0 3.0 %collective-permute-start.9 = (bf16[2,128,512]{2,1,0:T(8,128)(2,1)}, bf16[2,128,512]{2,1,0:T(8,128)(2,1)S(1)}, u32[]{:S(2)}, u32[]{:S(2)}) collective-permute-start(bf16[2,128,512]{2,1,0:T(8,128)(2,1)} %mine_ref.1), channel_id=1, source_target_pairs={{0,16},{8,24},{16,0},{24,8},{1,17},{9,25},{17,1},{25,9},{2,18},{10... | collective-permute-start | bytes 786440 | tf_op jit(solution)/shard_map/ppermute | solution.py:311
  3.0 1.0 %shard_map.73 = (bf16[64,1024]{1,0:T(8,128)(2,1)S(1)}, bf16[64,768]{1,0:T(8,128)(2,1)S(1)}, bf16[64,256]{1,0:T(8,128)(2,1)S(1)}) custom-call(bf16[64,512]{1,0:T(8,128)(2,1)} %refs_0_.1, bf16[64,512]{1,0:T(8,128)(2,1)} %refs_1_.1, bf16[64,512]{1,0:T(8,128)(2,1)} %refs_2_.1, bf16[64,512]{1,0:T(8,128)(2,1)} %refs_3_.1), custom_call_target="tpu_custom_call" | custom-call | bytes 1048576 | tf_op jit(solution)/shard_map/pallas_call | solution.py:330
  4.0 3.7 %collective-permute-start.11 = (bf16[64,768]{1,0:T(8,128)(2,1)S(1)}, bf16[64,768]{1,0:T(8,128)(2,1)S(1)}, u32[]{:S(2)}, u32[]{:S(2)}) collective-permute-start(bf16[64,768]{1,0:T(8,128)(2,1)S(1)} %get-tuple-element.22), channel_id=1, source_target_pairs={{6,0},{7,1},{4,2},{5,3},{2,4},{3,5},{0,6},{1,7},{12,8},{13,9},{14,... | collective-permute-start | bytes 294920 | tf_op jit(solution)/shard_map/ppermute | solution.py:323
  7.7 1.9 %collective-permute-done.9.other_ref = bf16[2,128,512]{2,1,0:T(8,128)(2,1)S(1)} collective-permute-done((bf16[2,128,512]{2,1,0:T(8,128)(2,1)}, bf16[2,128,512]{2,1,0:T(8,128)(2,1)S(1)}, u32[]{:S(2)}, u32[]{:S(2)}) %collective-permute-start.9) | collective-permute-done | bytes 262176 | tf_op jit(solution)/shard_map/ppermute | solution.py:311
  9.6 1.7 %collective-permute-start.2 = (bf16[64,1024]{1,0:T(8,128)(2,1)S(1)}, bf16[64,1024]{1,0:T(8,128)(2,1)S(1)}, u32[]{:S(2)}, u32[]{:S(2)}) collective-permute-start(bf16[64,1024]{1,0:T(8,128)(2,1)S(1)} %get-tuple-element.18.refs_0_), channel_id=1, source_target_pairs={{2,0},{3,1},{0,2},{1,3},{6,4},{7,5},{4,6},{5,7},{11,8},{10,9},{9,1... | collective-permute-start | bytes 393224 | tf_op jit(solution)/shard_map/ppermute | solution.py:323
  11.3 0.7 %collective-permute-start.4 = (bf16[64,1024]{1,0:T(8,128)(2,1)S(1)}, bf16[64,1024]{1,0:T(8,128)(2,1)S(1)}, u32[]{:S(2)}, u32[]{:S(2)}) collective-permute-start(bf16[64,1024]{1,0:T(8,128)(2,1)S(1)} %get-tuple-element.18.refs_0_), channel_id=1, source_target_pairs={{9,8},{8,9},{11,10},{10,11},{13,12},{12,13},{15,14},{14,15},{25,24... | collective-permute-start | bytes 393224 | tf_op jit(solution)/shard_map/ppermute | solution.py:323
  12.0 1.6 %collective-permute-start.13 = (bf16[64,768]{1,0:T(8,128)(2,1)S(1)}, bf16[64,768]{1,0:T(8,128)(2,1)S(1)}, u32[]{:S(2)}, u32[]{:S(2)}) collective-permute-start(bf16[64,768]{1,0:T(8,128)(2,1)S(1)} %collective-permute-done.11.refs_1_), channel_id=1, source_target_pairs={{1,0},{0,1},{3,2},{2,3},{5,4},{4,5},{7,6},{6,7},{9,8},{8,9},{11,10... | collective-permute-start | bytes 294920 | tf_op jit(solution)/shard_map/ppermute | solution.py:323
  13.6 1.8 %collective-permute-done.2.refs_3_ = bf16[64,1024]{1,0:T(8,128)(2,1)S(1)} collective-permute-done((bf16[64,1024]{1,0:T(8,128)(2,1)S(1)}, bf16[64,1024]{1,0:T(8,128)(2,1)S(1)}, u32[]{:S(2)}, u32[]{:S(2)}) %collective-permute-start.2) | collective-permute-done | bytes 131104 | tf_op jit(solution)/shard_map/ppermute | solution.py:323
  15.3 0.6 %collective-permute-start.3 = (bf16[64,1024]{1,0:T(8,128)(2,1)S(1)}, bf16[64,1024]{1,0:T(8,128)(2,1)S(1)}, u32[]{:S(2)}, u32[]{:S(2)}) collective-permute-start(bf16[64,1024]{1,0:T(8,128)(2,1)S(1)} %collective-permute-done.2.refs_3_), channel_id=1, source_target_pairs={{0,8},{8,0},{16,24},{24,16},{1,9},{9,1},{17,25},{25,17},{2,10},{10... | collective-permute-start | bytes 393224 | tf_op jit(solution)/shard_map/ppermute | solution.py:314
  15.9 2.2 %collective-permute-start.5 = (bf16[64,1024]{1,0:T(8,128)(2,1)S(1)}, bf16[64,1024]{1,0:T(8,128)(2,1)S(1)}, u32[]{:S(2)}, u32[]{:S(2)}) collective-permute-start(bf16[64,1024]{1,0:T(8,128)(2,1)S(1)} %collective-permute-done.4.refs_5_), channel_id=1, source_target_pairs={{0,8},{8,0},{16,24},{24,16},{1,9},{9,1},{17,25},{25,17},{2,10},{10... | collective-permute-start | bytes 393224 | tf_op jit(solution)/shard_map/ppermute | solution.py:314
  18.2 1.0 %collective-permute-start.12 = (bf16[64,768]{1,0:T(8,128)(2,1)S(1)}, bf16[64,768]{1,0:T(8,128)(2,1)S(1)}, u32[]{:S(2)}, u32[]{:S(2)}) collective-permute-start(bf16[64,768]{1,0:T(8,128)(2,1)S(1)} %collective-permute-done.11.refs_1_), channel_id=1, source_target_pairs={{0,8},{8,0},{16,24},{24,16},{1,9},{9,1},{17,25},{25,17},{2,10},{10... | collective-permute-start | bytes 294920 | tf_op jit(solution)/shard_map/ppermute | solution.py:314
  19.3 0.8 %shard_map.74 = (bf16[512,512]{1,0:T(8,128)(2,1)S(1)}, s32[2,8,128]{2,1,0:T(8,128)S(1)}) custom-call(s32[2,2]{1,0:T(2,128)S(1)} %copy-done.2, f32[1,512]{1,0:T(1,128)S(1)} %bitcast.1, bf16[2,128,512]{2,1,0:T(8,128)(2,1)S(1)} %copy-done, bf16[2,128,512]{2,1,0:T(8,128)(2,1)S(1)} %collective-permute-done.8.beside_ref, ...), custom_call_target="tpu_custom_call" | custom-call | flops 2097152 | bytes 1048576 | tf_op jit(solution)/shard_map/pallas_call | solution.py:330
  20.5 1.4 %shard_map.75 = (bf16[128,512]{1,0:T(8,128)(2,1)S(1)}, bf16[512,128]{1,0:T(8,128)(2,1)S(1)}, bf16[512,128]{1,0:T(8,128)(2,1)S(1)}, bf16[128,512]{1,0:T(8,128)(2,1)S(1)}) custom-call(s32[2,8,128]{2,1,0:T(8,128)S(1)} %get-tuple-element.20.bounds_ref, bf16[512,512]{1,0:T(8,128)(2,1)S(1)} %get-tuple-element.21.normed_ref, ...), custom_call_target="tpu_custom_call" | custom-call | flops 536870912 | bytes 1048576 | tf_op jit(solution)/shard_map/pallas_call | solution.py:330
  22.0 1.6 %collective-permute-start.15 = (bf16[128,512]{1,0:T(8,128)(2,1)S(1)}, bf16[128,512]{1,0:T(8,128)(2,1)S(1)}, u32[]{:S(2)}, u32[]{:S(2)}) collective-permute-start(bf16[128,512]{1,0:T(8,128)(2,1)S(1)} %get-tuple-element.23.refs_9_), channel_id=1, source_target_pairs={{0,16},{8,24},{16,0},{24,8},{1,17},{9,25},{17,1},{25,9},{2,18},{10... | collective-permute-start | bytes 393224 | tf_op jit(solution)/shard_map/ppermute | solution.py:311
  23.6 0.8 %shard_map.76.refs_10_ = bf16[128,512]{1,0:T(8,128)(2,1)S(1)} custom-call(s32[2,8,128]{2,1,0:T(8,128)S(1)} %get-tuple-element.20.bounds_ref, bf16[512,128]{1,0:T(8,128)(2,1)S(1)} %get-tuple-element.24.queries, bf16[512,128]{1,0:T(8,128)(2,1)S(1)} %get-tuple-element.25.keys, bf16[128,512]{1,0:T(8,128)(2,1)S(1)} %get-tuple-element.26.values), custom_call_target="tpu_custom_call" | custom-call | flops 134217728 | bytes 1048576 | tf_op jit(solution)/shard_map/pallas_call | solution.py:330
  24.4 0.6 %collective-permute-start.16 = (bf16[128,512]{1,0:T(8,128)(2,1)S(1)}, bf16[128,512]{1,0:T(8,128)(2,1)S(1)}, u32[]{:S(2)}, u32[]{:S(2)}) collective-permute-start(bf16[128,512]{1,0:T(8,128)(2,1)S(1)} %shard_map.76.refs_10_), channel_id=1, source_target_pairs={{0,16},{8,24},{16,0},{24,8},{1,17},{9,25},{17,1},{25,9},{2,18},{10... | collective-permute-start | bytes 393224 | tf_op jit(solution)/shard_map/ppermute | solution.py:311
  25.0 3.0 %collective-permute-start = (bf16[64,256]{1,0:T(8,128)(2,1)S(1)}, bf16[64,256]{1,0:T(8,128)(2,1)S(1)}, u32[]{:S(2)}, u32[]{:S(2)}) collective-permute-start(bf16[64,256]{1,0:T(8,128)(2,1)S(1)} %get-tuple-element.19), channel_id=1, source_target_pairs={{6,0},{7,1},{4,2},{5,3},{2,4},{3,5},{0,6},{1,7},{12,8},{13,9},{14,... | collective-permute-start | bytes 98312 | tf_op jit(solution)/shard_map/ppermute | solution.py:323
  28.0 2.7 %collective-permute-done.refs_1_ = bf16[64,256]{1,0:T(8,128)(2,1)S(1)} collective-permute-done((bf16[64,256]{1,0:T(8,128)(2,1)S(1)}, bf16[64,256]{1,0:T(8,128)(2,1)S(1)}, u32[]{:S(2)}, u32[]{:S(2)}) %collective-permute-start) | collective-permute-done | bytes 32800 | tf_op jit(solution)/shard_map/ppermute | solution.py:323
  30.7 1.5 %collective-permute-start.6 = (bf16[64,256]{1,0:T(8,128)(2,1)S(1)}, bf16[64,256]{1,0:T(8,128)(2,1)S(1)}, u32[]{:S(2)}, u32[]{:S(2)}) collective-permute-start(bf16[64,256]{1,0:T(8,128)(2,1)S(1)} %collective-permute-done.refs_1_), channel_id=1, source_target_pairs={{1,0},{0,1},{3,2},{2,3},{5,4},{4,5},{7,6},{6,7},{9,8},{8,9},{11,10... | collective-permute-start | bytes 98312 | tf_op jit(solution)/shard_map/ppermute | solution.py:323
  32.2 2.4 %collective-permute-done.6.refs_7_ = bf16[64,256]{1,0:T(8,128)(2,1)S(1)} collective-permute-done((bf16[64,256]{1,0:T(8,128)(2,1)S(1)}, bf16[64,256]{1,0:T(8,128)(2,1)S(1)}, u32[]{:S(2)}, u32[]{:S(2)}) %collective-permute-start.6) | collective-permute-done | bytes 32800 | tf_op jit(solution)/shard_map/ppermute | solution.py:323
  34.6 1.2 %collective-permute-done.7.refs_8_ = bf16[64,256]{1,0:T(8,128)(2,1)S(1)} collective-permute-done((bf16[64,256]{1,0:T(8,128)(2,1)S(1)}, bf16[64,256]{1,0:T(8,128)(2,1)S(1)}, u32[]{:S(2)}, u32[]{:S(2)}) %collective-permute-start.7) | collective-permute-done | bytes 32800 | tf_op jit(solution)/shard_map/ppermute | solution.py:314
  35.8 0.4 %shard_map.77 = (f32[128,512]{1,0:T(8,128)S(1)}, f32[128,512]{1,0:T(8,128)S(1)}, bf16[128,128]{1,0:T(8,128)(2,1)S(1)}, bf16[128,128]{1,0:T(8,128)(2,1)S(1)}) custom-call(bf16[64,1024]{1,0:T(8,128)(2,1)S(1)} %get-tuple-element.18.refs_0_, bf16[64,256]{1,0:T(8,128)(2,1)S(1)} %collective-permute-done.refs_1_, ...), custom_call_target="tpu_custom_call" | custom-call | flops 134217728 | bytes 1048576 | tf_op jit(solution)/shard_map/pallas_call | solution.py:330
  36.7 0.9 %shard_map.79.started_ref = bf16[2,128,512]{2,1,0:T(8,128)(2,1)} custom-call(f32[128,512]{1,0:T(8,128)S(1)} %get-tuple-element.29.partial_ref, bf16[128,128]{1,0:T(8,128)(2,1)S(1)} %get-tuple-element.30.weights_ref, bf16[128,512]{1,0:T(8,128)(2,1)S(1)} %collective-permute-done.16.value_ref), custom_call_target="tpu_custom_call" | custom-call | flops 33554432 | bytes 1048576 | tf_op jit(solution)/shard_map/pallas_call | solution.py:330
  37.9 0.7 %shard_map.80 = bf16[2,128,512]{2,1,0:T(8,128)(2,1)} custom-call(bf16[128,512]{1,0:T(8,128)(2,1)S(1)} %collective-permute-done.17.received_ref, bf16[2,128,512]{2,1,0:T(8,128)(2,1)} %shard_map.79.started_ref), custom_call_target="tpu_custom_call", output_to_operand_aliasing={{}: (1, {})} | custom-call | bytes 1048576 | tf_op jit(solution)/shard_map/pallas_call | solution.py:330
  (26 shorter events, 1.3 us)
Async XLA Ops:
  0.0 19.2 %copy-start = (bf16[2,128,512]{2,1,0:T(8,128)(2,1)S(1)}, bf16[2,128,512]{2,1,0:T(8,128)(2,1)}, u32[]{:S(2)}) copy-start(bf16[2,128,512]{2,1,0:T(8,128)(2,1)} %mine_ref.1) | copy-start | bytes 786436
  0.0 9.6 %collective-permute-start.9 = (bf16[2,128,512]{2,1,0:T(8,128)(2,1)}, bf16[2,128,512]{2,1,0:T(8,128)(2,1)S(1)}, u32[]{:S(2)}, u32[]{:S(2)}) collective-permute-start(bf16[2,128,512]{2,1,0:T(8,128)(2,1)} %mine_ref.1), channel_id=1, source_target_pairs={{0,16},{8,24},{16,0},{24,8},{1,17},{9,25},{17,1},{25,9},{2,18},{10... | collective-permute-start | bytes 786440 | tf_op jit(solution)/shard_map/ppermute | solution.py:311
  3.0 16.2 %collective-permute-start.8 = (bf16[2,128,512]{2,1,0:T(8,128)(2,1)}, bf16[2,128,512]{2,1,0:T(8,128)(2,1)S(1)}, u32[]{:S(2)}, u32[]{:S(2)}) collective-permute-start(bf16[2,128,512]{2,1,0:T(8,128)(2,1)} %mine_ref.1), channel_id=1, source_target_pairs={{0,8},{8,0},{16,24},{24,16},{1,9},{9,1},{17,25},{25,17},{2,10},{10... | collective-permute-start | bytes 786440 | tf_op jit(solution)/shard_map/ppermute | solution.py:314
  4.0 15.2 %copy-start.1 = (f32[512]{0:T(512)S(1)}, f32[512]{0:T(512)}, u32[]{:S(2)}) copy-start(f32[512]{0:T(512)} %param.8) | copy-start | bytes 6148
  4.0 8.0 %collective-permute-start.11 = (bf16[64,768]{1,0:T(8,128)(2,1)S(1)}, bf16[64,768]{1,0:T(8,128)(2,1)S(1)}, u32[]{:S(2)}, u32[]{:S(2)}) collective-permute-start(bf16[64,768]{1,0:T(8,128)(2,1)S(1)} %get-tuple-element.22), channel_id=1, source_target_pairs={{6,0},{7,1},{4,2},{5,3},{2,4},{3,5},{0,6},{1,7},{12,8},{13,9},{14,... | collective-permute-start | bytes 294920 | tf_op jit(solution)/shard_map/ppermute | solution.py:323
  9.6 9.7 %collective-permute-start.10 = (bf16[2,128,512]{2,1,0:T(8,128)(2,1)S(1)}, bf16[2,128,512]{2,1,0:T(8,128)(2,1)S(1)}, u32[]{:S(2)}, u32[]{:S(2)}) collective-permute-start(bf16[2,128,512]{2,1,0:T(8,128)(2,1)S(1)} %collective-permute-done.9.other_ref), channel_id=1, source_target_pairs={{0,8},{8,0},{16,24},{24,16},{1,9},{9,1},{17,25},{25,17},{2,10},{10... | collective-permute-start | bytes 786440 | tf_op jit(solution)/shard_map/ppermute | solution.py:314
  9.6 9.7 %copy-start.2 = (s32[2,2]{1,0:T(2,128)S(1)}, s32[2,2]{1,0:T(2,128)}, u32[]{:S(2)}) copy-start(s32[2,2]{1,0:T(2,128)} %tracks_ref.1) | copy-start | bytes 52
  9.6 5.8 %collective-permute-start.2 = (bf16[64,1024]{1,0:T(8,128)(2,1)S(1)}, bf16[64,1024]{1,0:T(8,128)(2,1)S(1)}, u32[]{:S(2)}, u32[]{:S(2)}) collective-permute-start(bf16[64,1024]{1,0:T(8,128)(2,1)S(1)} %get-tuple-element.18.refs_0_), channel_id=1, source_target_pairs={{2,0},{3,1},{0,2},{1,3},{6,4},{7,5},{4,6},{5,7},{11,8},{10,9},{9,1... | collective-permute-start | bytes 393224 | tf_op jit(solution)/shard_map/ppermute | solution.py:323
  11.3 4.6 %collective-permute-start.4 = (bf16[64,1024]{1,0:T(8,128)(2,1)S(1)}, bf16[64,1024]{1,0:T(8,128)(2,1)S(1)}, u32[]{:S(2)}, u32[]{:S(2)}) collective-permute-start(bf16[64,1024]{1,0:T(8,128)(2,1)S(1)} %get-tuple-element.18.refs_0_), channel_id=1, source_target_pairs={{9,8},{8,9},{11,10},{10,11},{13,12},{12,13},{15,14},{14,15},{25,24... | collective-permute-start | bytes 393224 | tf_op jit(solution)/shard_map/ppermute | solution.py:323
  12.0 6.2 %collective-permute-start.13 = (bf16[64,768]{1,0:T(8,128)(2,1)S(1)}, bf16[64,768]{1,0:T(8,128)(2,1)S(1)}, u32[]{:S(2)}, u32[]{:S(2)}) collective-permute-start(bf16[64,768]{1,0:T(8,128)(2,1)S(1)} %collective-permute-done.11.refs_1_), channel_id=1, source_target_pairs={{1,0},{0,1},{3,2},{2,3},{5,4},{4,5},{7,6},{6,7},{9,8},{8,9},{11,10... | collective-permute-start | bytes 294920 | tf_op jit(solution)/shard_map/ppermute | solution.py:323
  15.3 4.8 %collective-permute-start.3 = (bf16[64,1024]{1,0:T(8,128)(2,1)S(1)}, bf16[64,1024]{1,0:T(8,128)(2,1)S(1)}, u32[]{:S(2)}, u32[]{:S(2)}) collective-permute-start(bf16[64,1024]{1,0:T(8,128)(2,1)S(1)} %collective-permute-done.2.refs_3_), channel_id=1, source_target_pairs={{0,8},{8,0},{16,24},{24,16},{1,9},{9,1},{17,25},{25,17},{2,10},{10... | collective-permute-start | bytes 393224 | tf_op jit(solution)/shard_map/ppermute | solution.py:314
  15.9 4.3 %collective-permute-start.5 = (bf16[64,1024]{1,0:T(8,128)(2,1)S(1)}, bf16[64,1024]{1,0:T(8,128)(2,1)S(1)}, u32[]{:S(2)}, u32[]{:S(2)}) collective-permute-start(bf16[64,1024]{1,0:T(8,128)(2,1)S(1)} %collective-permute-done.4.refs_5_), channel_id=1, source_target_pairs={{0,8},{8,0},{16,24},{24,16},{1,9},{9,1},{17,25},{25,17},{2,10},{10... | collective-permute-start | bytes 393224 | tf_op jit(solution)/shard_map/ppermute | solution.py:314
  18.2 2.0 %collective-permute-start.12 = (bf16[64,768]{1,0:T(8,128)(2,1)S(1)}, bf16[64,768]{1,0:T(8,128)(2,1)S(1)}, u32[]{:S(2)}, u32[]{:S(2)}) collective-permute-start(bf16[64,768]{1,0:T(8,128)(2,1)S(1)} %collective-permute-done.11.refs_1_), channel_id=1, source_target_pairs={{0,8},{8,0},{16,24},{24,16},{1,9},{9,1},{17,25},{25,17},{2,10},{10... | collective-permute-start | bytes 294920 | tf_op jit(solution)/shard_map/ppermute | solution.py:314
  19.2 1.3 %collective-permute-start.14 = (bf16[64,768]{1,0:T(8,128)(2,1)S(1)}, bf16[64,768]{1,0:T(8,128)(2,1)S(1)}, u32[]{:S(2)}, u32[]{:S(2)}) collective-permute-start(bf16[64,768]{1,0:T(8,128)(2,1)S(1)} %collective-permute-done.13.refs_7_), channel_id=1, source_target_pairs={{0,8},{8,0},{16,24},{24,16},{1,9},{9,1},{17,25},{25,17},{2,10},{10... | collective-permute-start | bytes 294920 | tf_op jit(solution)/shard_map/ppermute | solution.py:314
  22.0 13.8 %collective-permute-start.15 = (bf16[128,512]{1,0:T(8,128)(2,1)S(1)}, bf16[128,512]{1,0:T(8,128)(2,1)S(1)}, u32[]{:S(2)}, u32[]{:S(2)}) collective-permute-start(bf16[128,512]{1,0:T(8,128)(2,1)S(1)} %get-tuple-element.23.refs_9_), channel_id=1, source_target_pairs={{0,16},{8,24},{16,0},{24,8},{1,17},{9,25},{17,1},{25,9},{2,18},{10... | collective-permute-start | bytes 393224 | tf_op jit(solution)/shard_map/ppermute | solution.py:311
  24.4 11.9 %collective-permute-start.16 = (bf16[128,512]{1,0:T(8,128)(2,1)S(1)}, bf16[128,512]{1,0:T(8,128)(2,1)S(1)}, u32[]{:S(2)}, u32[]{:S(2)}) collective-permute-start(bf16[128,512]{1,0:T(8,128)(2,1)S(1)} %shard_map.76.refs_10_), channel_id=1, source_target_pairs={{0,16},{8,24},{16,0},{24,8},{1,17},{9,25},{17,1},{25,9},{2,18},{10... | collective-permute-start | bytes 393224 | tf_op jit(solution)/shard_map/ppermute | solution.py:311
  25.0 5.7 %collective-permute-start = (bf16[64,256]{1,0:T(8,128)(2,1)S(1)}, bf16[64,256]{1,0:T(8,128)(2,1)S(1)}, u32[]{:S(2)}, u32[]{:S(2)}) collective-permute-start(bf16[64,256]{1,0:T(8,128)(2,1)S(1)} %get-tuple-element.19), channel_id=1, source_target_pairs={{6,0},{7,1},{4,2},{5,3},{2,4},{3,5},{0,6},{1,7},{12,8},{13,9},{14,... | collective-permute-start | bytes 98312 | tf_op jit(solution)/shard_map/ppermute | solution.py:323
  30.7 3.9 %collective-permute-start.6 = (bf16[64,256]{1,0:T(8,128)(2,1)S(1)}, bf16[64,256]{1,0:T(8,128)(2,1)S(1)}, u32[]{:S(2)}, u32[]{:S(2)}) collective-permute-start(bf16[64,256]{1,0:T(8,128)(2,1)S(1)} %collective-permute-done.refs_1_), channel_id=1, source_target_pairs={{1,0},{0,1},{3,2},{2,3},{5,4},{4,5},{7,6},{6,7},{9,8},{8,9},{11,10... | collective-permute-start | bytes 98312 | tf_op jit(solution)/shard_map/ppermute | solution.py:323
  32.2 2.4 %collective-permute-start.1 = (bf16[64,256]{1,0:T(8,128)(2,1)S(1)}, bf16[64,256]{1,0:T(8,128)(2,1)S(1)}, u32[]{:S(2)}, u32[]{:S(2)}) collective-permute-start(bf16[64,256]{1,0:T(8,128)(2,1)S(1)} %collective-permute-done.refs_1_), channel_id=1, source_target_pairs={{0,8},{8,0},{16,24},{24,16},{1,9},{9,1},{17,25},{25,17},{2,10},{10... | collective-permute-start | bytes 98312 | tf_op jit(solution)/shard_map/ppermute | solution.py:314
  34.6 1.2 %collective-permute-start.7 = (bf16[64,256]{1,0:T(8,128)(2,1)S(1)}, bf16[64,256]{1,0:T(8,128)(2,1)S(1)}, u32[]{:S(2)}, u32[]{:S(2)}) collective-permute-start(bf16[64,256]{1,0:T(8,128)(2,1)S(1)} %collective-permute-done.6.refs_7_), channel_id=1, source_target_pairs={{0,8},{8,0},{16,24},{24,16},{1,9},{9,1},{17,25},{25,17},{2,10},{10... | collective-permute-start | bytes 98312 | tf_op jit(solution)/shard_map/ppermute | solution.py:314
  36.5 1.4 %collective-permute-start.17 = (bf16[128,512]{1,0:T(8,128)(2,1)S(1)}, bf16[128,512]{1,0:T(8,128)(2,1)S(1)}, u32[]{:S(2)}, u32[]{:S(2)}) collective-permute-start(bf16[128,512]{1,0:T(8,128)(2,1)S(1)} %shard_map.78), channel_id=1, source_target_pairs={{0,8},{8,0},{16,24},{24,16},{1,9},{9,1},{17,25},{25,17},{2,10},{10... | collective-permute-start | bytes 393224 | tf_op jit(solution)/shard_map/ppermute | solution.py:314

commit v6 on v5

--- a/solution.py
+++ b/solution.py
@@ -135,57 +135,61 @@
         bounds_ref[n] = jnp.full(bounds_ref.shape[1:], tracks_ref[core, n], jnp.int32)
 
 
-def attend(bounds_ref, queries, keys, values, out_ref, head_dim):
-    steps = out_ref.shape[1]
-    block = span = LANES
-    heads = span // head_dim
+def attend(bounds_ref, first, queries, keys, values, out_ref, head_dim):
+    span, steps = out_ref.shape
+    block = LANES
+    heads = block // head_dim
     ratio = math.log2(math.e) / math.sqrt(head_dim)
     start, end = bounds_ref[0, :1, :block], bounds_ref[1, :1, :block]
-    lane = lax.broadcasted_iota(jnp.int32, (block, span), 1)
-
-    def score(j):
-        query_block = queries[pl.ds(j * block, block), :]
+    lane = lax.broadcasted_iota(jnp.int32, (block, block), 1)
+
+    def score(t, group):
+        query_block = queries[pl.ds(t, block), pl.ds(group, block)]
         one = [
             jnp.where((lane >= low) & (lane < low + head_dim), query_block, jnp.zeros_like(query_block))
-            for low in range(0, span, head_dim)
+            for low in range(0, block, head_dim)
         ]
         return lax.dot_general(
-            keys[pl.ds(0, (j + 1) * block), :],
+            keys[pl.ds(0, first + t + block), pl.ds(group, block)],
             jnp.concatenate(one, axis=0),
             (((1,), (1,)), ((), ())),
             preferred_element_type=jnp.float32,
         )
 
-    def weigh(j, scores):
-        reach = (j + 1) * block
+    def weigh(t, scores):
+        reach = first + t + block
         key_pos = lax.broadcasted_iota(jnp.int32, (reach, block), 0)
-        query_pos = j * block + lax.broadcasted_iota(jnp.int32, (reach, block), 1)
+        query_pos = first + t + lax.broadcasted_iota(jnp.int32, (reach, block), 1)
         allowed = (key_pos >= start) & (key_pos <= query_pos)
         scores = jnp.where(jnp.concatenate([allowed] * heads, axis=1), scores, NEGATIVE)
         highest = jnp.max(scores, axis=0, keepdims=True)
         weight = jnp.exp2((scores - highest) * ratio)
         return weight.astype(jnp.bfloat16), jnp.sum(weight, axis=0, keepdims=True)
 
-    def finish(j, weight, total):
+    def finish(t, group, weight, total):
         summed = jnp.dot(
-            values[:, pl.ds(0, (j + 1) * block)], weight, preferred_element_type=jnp.float32
-        )
-        column = j * block + lax.broadcasted_iota(jnp.int32, (1, block), 1)
+            values[pl.ds(group, block), pl.ds(0, first + t + block)],
+            weight,
+            preferred_element_type=jnp.float32,
+        )
+        column = first + t + lax.broadcasted_iota(jnp.int32, (1, block), 1)
         live = (column >= start) & (column < end)
         for h in range(heads):
             rows, lanes = slice(h * head_dim, (h + 1) * head_dim), slice(h * block, (h + 1) * block)
             result = jnp.where(live, summed[rows, lanes] / total[:, lanes], 0.0)
-            out_ref[rows, pl.ds(j * block, block)] = result.astype(jnp.bfloat16)
-
-    blocks = steps // block
+            out_ref[pl.ds(group + h * head_dim, head_dim), pl.ds(t, block)] = result.astype(
+                jnp.bfloat16
+            )
+
+    tasks = [(t, group) for t in range(0, steps, block) for group in range(0, span, block)]
     scores, weights = {}, {}
-    for j in range(blocks + 2):
-        if j < blocks:
-            scores[j] = score(j)
-        if 0 <= j - 1 < blocks:
-            weights[j - 1] = weigh(j - 1, scores.pop(j - 1))
-        if j >= 2:
-            finish(j - 2, *weights.pop(j - 2))
+    for n in range(len(tasks) + 2):
+        if n < len(tasks):
+            scores[n] = score(*tasks[n])
+        if 0 <= n - 1 < len(tasks):
+            weights[n - 1] = weigh(tasks[n - 1][0], scores.pop(n - 1))
+        if n >= 2:
+            finish(*tasks[n - 2], *weights.pop(n - 2))
 
 
 def pack_kernel(*refs):
@@ -223,68 +227,92 @@
                     pl.when(core == here)(functools.partial(put, ref, agent ^ offset))
 
 
-def first_kernel(sources, head_dim, bounds_ref, normed_ref, *refs):
+def project_rows(normed, weights, queries, keys, values):
+    span = queries.shape[1]
+    for n, target in enumerate((queries, keys, values)):
+        full = jnp.dot(
+            normed, weights[:, n * span : (n + 1) * span], preferred_element_type=jnp.float32
+        )
+        target[...] = (full.T if n == 2 else full).astype(jnp.bfloat16)
+
+
+def low_kernel(sources, head_dim, bounds_ref, normed_ref, *refs):
     shards, refs = refs[: 1 + 2 * len(sources)], refs[1 + 2 * len(sources) :]
-    out_ref, late, weights, held = refs[0], refs[1:4], refs[4], refs[5:]
-    _, columns = weights.shape
-    span = columns // 3
+    out_ref, weights, keys, values, queries = refs
     place(sources, shards, weights, 0)
-    for n in range(3):
-        full = jnp.dot(
-            normed_ref[...], weights[:, n * span : (n + 1) * span], preferred_element_type=jnp.float32
-        )
-        for m, target in enumerate((held[n], late[n])):
-            part = full[:, m * LANES : (m + 1) * LANES]
-            target[...] = (part.T if n == 2 else part).astype(jnp.bfloat16)
-    attend(bounds_ref, *held, out_ref, head_dim)
-
-
-def second_kernel(head_dim, bounds_ref, queries, keys, values, out_ref):
-    attend(bounds_ref, queries, keys, values, out_ref, head_dim)
-
-
-def transposed_dot(weight, value):
+    steps = out_ref.shape[1]
+    project_rows(normed_ref[:steps, :], weights, queries, keys, values)
+    attend(bounds_ref, 0, queries, keys, values, out_ref, head_dim)
+
+
+def high_kernel(head_dim, bounds_ref, normed_ref, weights, low_keys, low_values, *refs):
+    out_ref, queries, keys, values = refs
+    first = low_keys.shape[0]
+    keys[:first, :] = low_keys[...]
+    values[:, :first] = low_values[...]
+    later = pl.ds(first, keys.shape[0] - first)
+    project_rows(
+        normed_ref[first:, :], weights, queries, keys.at[later, :], values.at[:, later]
+    )
+    attend(bounds_ref, first, queries, keys, values, out_ref, head_dim)
+
+
+def channel_terms(weights, ref, chip, core):
+    span = ref.shape[0]
+    half = weights.shape[1] // 2
+    rows = pl.ds(pl.multiple_of(chip * span, span), span)
+    lanes = pl.ds(pl.multiple_of(core * half, half), half)
     return lax.dot_general(
-        weight, value, (((0,), (0,)), ((), ())), preferred_element_type=jnp.float32
-    )
-
-
-def partial_kernel(sources, *refs):
+        weights[rows, lanes], ref[...], (((0,), (0,)), ((), ())), preferred_element_type=jnp.float32
+    )
+
+
+def low_output_kernel(sources, *refs):
     shards, refs = refs[: 1 + 2 * len(sources)], refs[1 + 2 * len(sources) :]
-    here, kept_ref, given_ref, kept_weights, given_weights, weights = (
-        refs[:3],
-        *refs[3:7],
-        refs[7],
-    )
-    _, columns = weights.shape
-    half = columns // 2
+    mine_ref, other_ref, kept_ref, given_ref, weights = refs
     core, y = lax.axis_index("tm") % 2, lax.axis_index("tm") // 2
-    place(sources, shards, weights, 3 * columns)
-    for n, (ref, last) in enumerate(((kept_ref, kept_weights), (given_ref, given_weights))):
-        lanes = pl.ds(pl.multiple_of((core ^ n) * half, half), half)
-        total = None
-        for m, value in enumerate(here):
-            group = ((y ^ (m // 2)) * 2 + m % 2) * LANES
-            rows = pl.ds(pl.multiple_of(group, LANES), LANES)
-            term = transposed_dot(weights[rows, lanes], value[...])
-            total = term if total is None else total + term
-        ref[...] = total
-        last[...] = weights[pl.ds(pl.multiple_of(((y ^ 1) * 2 + 1) * LANES, LANES), LANES), lanes]
-
-
-def given_kernel(partial_ref, weights_ref, value_ref, out_ref):
-    out_ref[...] = (partial_ref[...] + transposed_dot(weights_ref[...], value_ref[...])).astype(
-        jnp.bfloat16
-    )
-
-
-def kept_kernel(partial_ref, weights_ref, value_ref, out_ref, held):
-    given_kernel(partial_ref, weights_ref, value_ref, held)
-    pltpu.sync_copy(held, out_ref.at[lax.axis_index("tm") % 2])
-
-
-def final_kernel(received_ref, started_ref, out_ref):
-    pltpu.sync_copy(received_ref, out_ref.at[1 - lax.axis_index("tm") % 2])
+    place(sources, shards, weights, 3 * weights.shape[1])
+    for n, ref in enumerate((kept_ref, given_ref)):
+        total = channel_terms(weights, mine_ref, y, core ^ n)
+        total = total + channel_terms(weights, other_ref, y ^ 1, core ^ n)
+        ref[...] = total.astype(ref.dtype)
+
+
+def partial_kernel(weights, mine_ref, kept_ref, given_ref):
+    core, y = lax.axis_index("tm") % 2, lax.axis_index("tm") // 2
+    for n, ref in enumerate((kept_ref, given_ref)):
+        ref[...] = channel_terms(weights, mine_ref, y, core ^ n)
+
+
+def given_kernel(weights, partial_ref, other_ref, out_ref):
+    core, y = lax.axis_index("tm") % 2, lax.axis_index("tm") // 2
+    total = partial_ref[...] + channel_terms(weights, other_ref, y ^ 1, core ^ 1)
+    out_ref[...] = total.astype(out_ref.dtype)
+
+
+def kept_kernel(weights, partial_ref, other_ref, low_ref, received_ref, out_ref, held, sems):
+    core, y = lax.axis_index("tm") % 2, lax.axis_index("tm") // 2
+    low, high = low_ref.shape[1], held.shape[1]
+    copies = [
+        pltpu.make_async_copy(low_ref, out_ref.at[core, :, pl.ds(0, low)], sems.at[0]),
+        pltpu.make_async_copy(received_ref, out_ref.at[1 - core, :, pl.ds(0, low)], sems.at[1]),
+        pltpu.make_async_copy(held, out_ref.at[core, :, pl.ds(low, high)], sems.at[2]),
+    ]
+    copies[0].start()
+    copies[1].start()
+    total = partial_ref[...] + channel_terms(weights, other_ref, y ^ 1, core)
+    held[...] = total.astype(held.dtype)
+    copies[2].start()
+    for copy in copies:
+        copy.wait()
+
+
+def final_kernel(received_ref, begun_ref, out_ref):
+    count = received_ref.shape[1]
+    pltpu.sync_copy(
+        received_ref,
+        out_ref.at[1 - lax.axis_index("tm") % 2, :, pl.ds(out_ref.shape[2] - count, count)],
+    )
 
 
 def fits(n_tm, n_agent, features):
@@ -368,53 +396,65 @@
         flops=8 * steps * width,
     )
     shards = [packed] + [v for pair in zip(fetched, swapped) for v in pair]
-    head_flops = 4 * steps * steps * LANES
-    heads = [((steps, LANES), half)] * 2 + [((LANES, steps), half)]
-    exponentials = steps * steps * LANES // head_dim
-    attended_first, *late = kernel(
-        functools.partial(first_kernel, sources, head_dim),
-        [((LANES, steps), half)] + heads,
+    low = steps // 2
+    high = steps - low
+    exponentials = span // head_dim
+    low_attended, weights, *low_held = kernel(
+        functools.partial(low_kernel, sources, head_dim),
+        [
+            ((span, low), half),
+            ((width, 3 * span), half),
+            ((low, span), half),
+            ((span, low), half),
+        ],
         (bounds, normed, *shards),
-        scratch=[((width, 3 * span), half)] + heads,
-        flops=6 * steps * width * span + head_flops,
-        transcendentals=exponentials,
-    )
-    other_first = across(attended_first)
-    (attended_second,) = kernel(
-        functools.partial(second_kernel, head_dim),
-        [((LANES, steps), half)],
-        (bounds, *late),
-        flops=head_flops,
-        transcendentals=exponentials,
-    )
-    other = across(attended_second)
+        scratch=[((low, span), half)],
+        flops=6 * low * width * span + 4 * low * low * span,
+        transcendentals=low * low * exponentials,
+    )
+    low_other = across(low_attended)
+    (high_attended,) = kernel(
+        functools.partial(high_kernel, head_dim),
+        [((span, high), half)],
+        (bounds, normed, weights, *low_held),
+        scratch=[((high, span), half), ((steps, span), half), ((span, steps), half)],
+        flops=6 * high * width * span + 4 * high * steps * span,
+        transcendentals=high * steps * exponentials,
+    )
+    high_other = across(high_attended)
     out_shards = [packed] + [v for pair in zip(out_shards, swapped_out) for v in pair]
-    kept, given, kept_weights, given_weights = kernel(
-        functools.partial(partial_kernel, sources),
-        [((span // 2, steps), full)] * 2 + [((LANES, span // 2), half)] * 2,
-        (*out_shards, attended_first, attended_second, other_first),
-        scratch=[((width, span), half)],
-        flops=2 * steps * width * span,
+    low_kept, low_given, out_weights = kernel(
+        functools.partial(low_output_kernel, sources),
+        [((span // 2, low), half)] * 2 + [((width, span), half)],
+        (*out_shards, low_attended, low_other),
+        flops=4 * low * span * span,
+    )
+    low_received = swap(low_given)
+    kept, given = kernel(
+        partial_kernel,
+        [((span // 2, high), full)] * 2,
+        (out_weights, high_attended),
+        flops=2 * high * span * span,
     )
     (given,) = kernel(
         given_kernel,
-        [((span // 2, steps), half)],
-        (given, given_weights, other),
-        flops=steps * span * span,
+        [((span // 2, high), half)],
+        (out_weights, given, high_other),
+        flops=high * span * span,
     )
     received = swap(given)
-    (started,) = kernel(
+    (begun,) = kernel(
         kept_kernel,
         [((2, span // 2, steps), half)],
-        (kept, kept_weights, other),
-        scratch=[((span // 2, steps), half)],
+        (out_weights, kept, high_other, low_kept, low_received),
+        scratch=[((span // 2, high), half), pltpu.SemaphoreType.DMA((3,))],
         out_spec=anywhere,
-        flops=steps * span * span,
+        flops=high * span * span,
     )
     (out,) = kernel(
         final_kernel,
         [((2, span // 2, steps), half)],
-        (received, started),
+        (received, begun),
         specs=[vmem, anywhere],
         out_spec=anywhere,
         aliases={1: 0},

time: 38.8 us -> 39.3 us (1.013)
  starting transfers between devices: 21.4 us -> 21.8 us
    ppermute x9 -> x10, starting transfers between devices: 4.12 us -> 4.53 us  [swap(): return lax.ppermute(value, 'tm', [(i, i ^ 1) for i in range(n_tm)])]
    ppermute x9 -> x10, waiting for transfers between devices: 2 us -> 2.15 us  [swap(): return lax.ppermute(value, 'tm', [(i, i ^ 1) for i in range(n_tm)])]
    pallas_call x8 -> x9, Pallas kernels: 6.2 us -> 6.18 us  [kernel(): pl.pallas_call(body, out_shape=[jax.ShapeDtypeStruct(shape, dtype) for sh...]
  transfers between devices with their start and end apart: 18 -> 19, of which waited for: 8 -> 8; matrix products, arithmetic and copies ran while one was open for 0% -> 0% of each run, Pallas kernels for 10% -> 12%
where the time goes in v6:
time: 39.3 us; the launch traced here: 39.1 us
  starting transfers between devices  21.8 us (55%)
  waiting for transfers between devices  11 us (28%)
  Pallas kernels  6.18 us (16%)
    ppermute x6, starting transfers between devices, fetch(): return lax.ppermute(value, ('tm', 'agent'), pairs)  12.1 us
    ppermute x6, waiting for transfers between devices, fetch(): return lax.ppermute(value, ('tm', 'agent'), pairs)  6.91 us
    pallas_call x9, Pallas kernels, kernel(): pl.pallas_call(body, out_shape=[jax.ShapeDtypeStruct(shape, dtype) for sh...  6.18 us
    ppermute x3, starting transfers between devices, across(): return lax.ppermute(value, 'tm', [(i, i ^ 2) for i in range(n_tm)])  5.15 us
    ppermute x10, starting transfers between devices, swap(): return lax.ppermute(value, 'tm', [(i, i ^ 1) for i in range(n_tm)])  4.53 us
    ppermute x10, waiting for transfers between devices, swap(): return lax.ppermute(value, 'tm', [(i, i ^ 1) for i in range(n_tm)])  2.15 us
    ppermute x3, waiting for transfers between devices, across(): return lax.ppermute(value, 'tm', [(i, i ^ 2) for i in range(n_tm)])  1.91 us
  transfers between devices with their start and end apart: 19, of which 8 were waited for; matrix products, arithmetic and copies ran while one was open for 0% of the time, Pallas kernels for 12%

profile of v6, /device:TPU:0, one launch (start us, length us, event | category | flops | bytes accessed | tf_op | source)
XLA Modules:
  0.0 39.1 jit_solution(713355979365192369)
XLA Ops:
  0.0 3.0 %collective-permute-start.9 = (bf16[2,128,512]{2,1,0:T(8,128)(2,1)}, bf16[2,128,512]{2,1,0:T(8,128)(2,1)S(1)}, u32[]{:S(2)}, u32[]{:S(2)}) collective-permute-start(bf16[2,128,512]{2,1,0:T(8,128)(2,1)} %mine_ref.1), channel_id=1, source_target_pairs={{0,16},{8,24},{16,0},{24,8},{1,17},{9,25},{17,1},{25,9},{2,18},{10... | collective-permute-start | bytes 786440 | tf_op jit(solution)/shard_map/ppermute | solution.py:339
  3.0 1.0 %shard_map.73 = (bf16[64,1024]{1,0:T(8,128)(2,1)S(1)}, bf16[64,768]{1,0:T(8,128)(2,1)S(1)}, bf16[64,256]{1,0:T(8,128)(2,1)S(1)}) custom-call(bf16[64,512]{1,0:T(8,128)(2,1)} %refs_0_.1, bf16[64,512]{1,0:T(8,128)(2,1)} %refs_1_.1, bf16[64,512]{1,0:T(8,128)(2,1)} %refs_2_.1, bf16[64,512]{1,0:T(8,128)(2,1)} %refs_3_.1), custom_call_target="tpu_custom_call" | custom-call | bytes 1048576 | tf_op jit(solution)/shard_map/pallas_call | solution.py:358
  4.0 3.7 %collective-permute-start.11 = (bf16[64,768]{1,0:T(8,128)(2,1)S(1)}, bf16[64,768]{1,0:T(8,128)(2,1)S(1)}, u32[]{:S(2)}, u32[]{:S(2)}) collective-permute-start(bf16[64,768]{1,0:T(8,128)(2,1)S(1)} %get-tuple-element.23), channel_id=1, source_target_pairs={{6,0},{7,1},{4,2},{5,3},{2,4},{3,5},{0,6},{1,7},{12,8},{13,9},{14,... | collective-permute-start | bytes 294920 | tf_op jit(solution)/shard_map/ppermute | solution.py:351
  7.7 1.9 %collective-permute-done.9.other_ref = bf16[2,128,512]{2,1,0:T(8,128)(2,1)S(1)} collective-permute-done((bf16[2,128,512]{2,1,0:T(8,128)(2,1)}, bf16[2,128,512]{2,1,0:T(8,128)(2,1)S(1)}, u32[]{:S(2)}, u32[]{:S(2)}) %collective-permute-start.9) | collective-permute-done | bytes 262176 | tf_op jit(solution)/shard_map/ppermute | solution.py:339
  9.6 1.7 %collective-permute-start.2 = (bf16[64,1024]{1,0:T(8,128)(2,1)S(1)}, bf16[64,1024]{1,0:T(8,128)(2,1)S(1)}, u32[]{:S(2)}, u32[]{:S(2)}) collective-permute-start(bf16[64,1024]{1,0:T(8,128)(2,1)S(1)} %get-tuple-element.19.refs_0_), channel_id=1, source_target_pairs={{2,0},{3,1},{0,2},{1,3},{6,4},{7,5},{4,6},{5,7},{11,8},{10,9},{9,1... | collective-permute-start | bytes 393224 | tf_op jit(solution)/shard_map/ppermute | solution.py:351
  11.3 0.7 %collective-permute-start.4 = (bf16[64,1024]{1,0:T(8,128)(2,1)S(1)}, bf16[64,1024]{1,0:T(8,128)(2,1)S(1)}, u32[]{:S(2)}, u32[]{:S(2)}) collective-permute-start(bf16[64,1024]{1,0:T(8,128)(2,1)S(1)} %get-tuple-element.19.refs_0_), channel_id=1, source_target_pairs={{9,8},{8,9},{11,10},{10,11},{13,12},{12,13},{15,14},{14,15},{25,24... | collective-permute-start | bytes 393224 | tf_op jit(solution)/shard_map/ppermute | solution.py:351
  12.0 1.6 %collective-permute-start.13 = (bf16[64,768]{1,0:T(8,128)(2,1)S(1)}, bf16[64,768]{1,0:T(8,128)(2,1)S(1)}, u32[]{:S(2)}, u32[]{:S(2)}) collective-permute-start(bf16[64,768]{1,0:T(8,128)(2,1)S(1)} %collective-permute-done.11.refs_1_), channel_id=1, source_target_pairs={{1,0},{0,1},{3,2},{2,3},{5,4},{4,5},{7,6},{6,7},{9,8},{8,9},{11,10... | collective-permute-start | bytes 294920 | tf_op jit(solution)/shard_map/ppermute | solution.py:351
  13.6 1.8 %collective-permute-done.2.refs_3_ = bf16[64,1024]{1,0:T(8,128)(2,1)S(1)} collective-permute-done((bf16[64,1024]{1,0:T(8,128)(2,1)S(1)}, bf16[64,1024]{1,0:T(8,128)(2,1)S(1)}, u32[]{:S(2)}, u32[]{:S(2)}) %collective-permute-start.2) | collective-permute-done | bytes 131104 | tf_op jit(solution)/shard_map/ppermute | solution.py:351
  15.3 0.6 %collective-permute-start.3 = (bf16[64,1024]{1,0:T(8,128)(2,1)S(1)}, bf16[64,1024]{1,0:T(8,128)(2,1)S(1)}, u32[]{:S(2)}, u32[]{:S(2)}) collective-permute-start(bf16[64,1024]{1,0:T(8,128)(2,1)S(1)} %collective-permute-done.2.refs_3_), channel_id=1, source_target_pairs={{0,8},{8,0},{16,24},{24,16},{1,9},{9,1},{17,25},{25,17},{2,10},{10... | collective-permute-start | bytes 393224 | tf_op jit(solution)/shard_map/ppermute | solution.py:342
  15.9 2.2 %collective-permute-start.5 = (bf16[64,1024]{1,0:T(8,128)(2,1)S(1)}, bf16[64,1024]{1,0:T(8,128)(2,1)S(1)}, u32[]{:S(2)}, u32[]{:S(2)}) collective-permute-start(bf16[64,1024]{1,0:T(8,128)(2,1)S(1)} %collective-permute-done.4.refs_5_), channel_id=1, source_target_pairs={{0,8},{8,0},{16,24},{24,16},{1,9},{9,1},{17,25},{25,17},{2,10},{10... | collective-permute-start | bytes 393224 | tf_op jit(solution)/shard_map/ppermute | solution.py:342
  18.2 1.0 %collective-permute-start.12 = (bf16[64,768]{1,0:T(8,128)(2,1)S(1)}, bf16[64,768]{1,0:T(8,128)(2,1)S(1)}, u32[]{:S(2)}, u32[]{:S(2)}) collective-permute-start(bf16[64,768]{1,0:T(8,128)(2,1)S(1)} %collective-permute-done.11.refs_1_), channel_id=1, source_target_pairs={{0,8},{8,0},{16,24},{24,16},{1,9},{9,1},{17,25},{25,17},{2,10},{10... | collective-permute-start | bytes 294920 | tf_op jit(solution)/shard_map/ppermute | solution.py:342
  19.3 0.8 %shard_map.74 = (bf16[512,512]{1,0:T(8,128)(2,1)S(1)}, s32[2,8,128]{2,1,0:T(8,128)S(1)}) custom-call(s32[2,2]{1,0:T(2,128)S(1)} %copy-done.2, f32[1,512]{1,0:T(1,128)S(1)} %bitcast.1, bf16[2,128,512]{2,1,0:T(8,128)(2,1)S(1)} %copy-done, bf16[2,128,512]{2,1,0:T(8,128)(2,1)S(1)} %collective-permute-done.8.beside_ref, ...), custom_call_target="tpu_custom_call" | custom-call | flops 2097152 | bytes 1048576 | tf_op jit(solution)/shard_map/pallas_call | solution.py:358
  20.5 1.0 %shard_map.75 = (bf16[256,256]{1,0:T(8,128)(2,1)S(1)}, bf16[512,768]{1,0:T(8,128)(2,1)S(1)}, bf16[256,256]{1,0:T(8,128)(2,1)S(1)}, bf16[256,256]{1,0:T(8,128)(2,1)S(1)}) custom-call(s32[2,8,128]{2,1,0:T(8,128)S(1)} %get-tuple-element.21.bounds_ref, bf16[512,512]{1,0:T(8,128)(2,1)S(1)} %get-tuple-element.22.normed_ref, ...), custom_call_target="tpu_custom_call" | custom-call | flops 268435456 | bytes 1048576 | tf_op jit(solution)/shard_map/pallas_call | solution.py:358
  21.5 1.6 %collective-permute-start.15 = (bf16[256,256]{1,0:T(8,128)(2,1)S(1)}, bf16[256,256]{1,0:T(8,128)(2,1)S(1)}, u32[]{:S(2)}, u32[]{:S(2)}) collective-permute-start(bf16[256,256]{1,0:T(8,128)(2,1)S(1)} %get-tuple-element.24.refs_9_), channel_id=1, source_target_pairs={{0,16},{8,24},{16,0},{24,8},{1,17},{9,25},{17,1},{25,9},{2,18},{10... | collective-permute-start | bytes 393224 | tf_op jit(solution)/shard_map/ppermute | solution.py:339
  23.1 1.1 %shard_map.77.mine_ref = bf16[256,256]{1,0:T(8,128)(2,1)S(1)} custom-call(s32[2,8,128]{2,1,0:T(8,128)S(1)} %get-tuple-element.21.bounds_ref, bf16[512,512]{1,0:T(8,128)(2,1)S(1)} %get-tuple-element.22.normed_ref, bf16[512,768]{1,0:T(8,128)(2,1)S(1)} %get-tuple-element.26.weights, bf16[256,256]{1,0:T(8,128)(2,1)S(1)} %get-tuple-element.27.low_keys, ...), custom_call_target="tpu_custom_call" | custom-call | flops 335544320 | bytes 1048576 | tf_op jit(solution)/shard_map/pallas_call | solution.py:358
  24.2 0.6 %collective-permute-start.16 = (bf16[256,256]{1,0:T(8,128)(2,1)S(1)}, bf16[256,256]{1,0:T(8,128)(2,1)S(1)}, u32[]{:S(2)}, u32[]{:S(2)}) collective-permute-start(bf16[256,256]{1,0:T(8,128)(2,1)S(1)} %shard_map.77.mine_ref), channel_id=1, source_target_pairs={{0,16},{8,24},{16,0},{24,8},{1,17},{9,25},{17,1},{25,9},{2,18},{10... | collective-permute-start | bytes 393224 | tf_op jit(solution)/shard_map/ppermute | solution.py:339
  24.8 3.0 %collective-permute-start = (bf16[64,256]{1,0:T(8,128)(2,1)S(1)}, bf16[64,256]{1,0:T(8,128)(2,1)S(1)}, u32[]{:S(2)}, u32[]{:S(2)}) collective-permute-start(bf16[64,256]{1,0:T(8,128)(2,1)S(1)} %get-tuple-element.20), channel_id=1, source_target_pairs={{6,0},{7,1},{4,2},{5,3},{2,4},{3,5},{0,6},{1,7},{12,8},{13,9},{14,... | collective-permute-start | bytes 98312 | tf_op jit(solution)/shard_map/ppermute | solution.py:351
  27.8 2.7 %collective-permute-done.refs_1_ = bf16[64,256]{1,0:T(8,128)(2,1)S(1)} collective-permute-done((bf16[64,256]{1,0:T(8,128)(2,1)S(1)}, bf16[64,256]{1,0:T(8,128)(2,1)S(1)}, u32[]{:S(2)}, u32[]{:S(2)}) %collective-permute-start) | collective-permute-done | bytes 32800 | tf_op jit(solution)/shard_map/ppermute | solution.py:351
  30.5 1.5 %collective-permute-start.6 = (bf16[64,256]{1,0:T(8,128)(2,1)S(1)}, bf16[64,256]{1,0:T(8,128)(2,1)S(1)}, u32[]{:S(2)}, u32[]{:S(2)}) collective-permute-start(bf16[64,256]{1,0:T(8,128)(2,1)S(1)} %collective-permute-done.refs_1_), channel_id=1, source_target_pairs={{1,0},{0,1},{3,2},{2,3},{5,4},{4,5},{7,6},{6,7},{9,8},{8,9},{11,10... | collective-permute-start | bytes 98312 | tf_op jit(solution)/shard_map/ppermute | solution.py:351
  32.0 2.4 %collective-permute-done.6.refs_7_ = bf16[64,256]{1,0:T(8,128)(2,1)S(1)} collective-permute-done((bf16[64,256]{1,0:T(8,128)(2,1)S(1)}, bf16[64,256]{1,0:T(8,128)(2,1)S(1)}, u32[]{:S(2)}, u32[]{:S(2)}) %collective-permute-start.6) | collective-permute-done | bytes 32800 | tf_op jit(solution)/shard_map/ppermute | solution.py:351
  34.4 1.2 %collective-permute-done.7.refs_8_ = bf16[64,256]{1,0:T(8,128)(2,1)S(1)} collective-permute-done((bf16[64,256]{1,0:T(8,128)(2,1)S(1)}, bf16[64,256]{1,0:T(8,128)(2,1)S(1)}, u32[]{:S(2)}, u32[]{:S(2)}) %collective-permute-start.7) | collective-permute-done | bytes 32800 | tf_op jit(solution)/shard_map/ppermute | solution.py:342
  37.1 0.5 %collective-permute-done.18.received_ref = bf16[128,256]{1,0:T(8,128)(2,1)S(1)} collective-permute-done((bf16[128,256]{1,0:T(8,128)(2,1)S(1)}, bf16[128,256]{1,0:T(8,128)(2,1)S(1)}, u32[]{:S(2)}, u32[]{:S(2)}) %collective-permute-start.18) | collective-permute-done | bytes 65568 | tf_op jit(solution)/shard_map/ppermute | solution.py:342
  37.6 0.9 %shard_map.80.begun_ref = bf16[2,128,512]{2,1,0:T(8,128)(2,1)} custom-call(bf16[512,256]{1,0:T(8,128)(2,1)S(1)} %get-tuple-element.25.weights, f32[128,256]{1,0:T(8,128)S(1)} %get-tuple-element.30.partial_ref, bf16[256,256]{1,0:T(8,128)(2,1)S(1)} %collective-permute-done.16.other_ref, bf16[128,256]{1,0:T(8,128)(2,1)S(1)} %get-tuple-element.31.low_ref, ...), custom_call_target="tpu_custom_call" | custom-call | flops 16777216 | bytes 1048576 | tf_op jit(solution)/shard_map/pallas_call | solution.py:358
  38.4 0.6 %shard_map.81 = bf16[2,128,512]{2,1,0:T(8,128)(2,1)} custom-call(bf16[128,256]{1,0:T(8,128)(2,1)S(1)} %collective-permute-done.17.received_ref, bf16[2,128,512]{2,1,0:T(8,128)(2,1)} %shard_map.80.begun_ref), custom_call_target="tpu_custom_call", output_to_operand_aliasing={{}: (1, {})} | custom-call | bytes 1048576 | tf_op jit(solution)/shard_map/pallas_call | solution.py:358
  (29 shorter events, 2.0 us)
Async XLA Ops:
  0.0 19.2 %copy-start = (bf16[2,128,512]{2,1,0:T(8,128)(2,1)S(1)}, bf16[2,128,512]{2,1,0:T(8,128)(2,1)}, u32[]{:S(2)}) copy-start(bf16[2,128,512]{2,1,0:T(8,128)(2,1)} %mine_ref.1) | copy-start | bytes 786436
  0.0 9.6 %collective-permute-start.9 = (bf16[2,128,512]{2,1,0:T(8,128)(2,1)}, bf16[2,128,512]{2,1,0:T(8,128)(2,1)S(1)}, u32[]{:S(2)}, u32[]{:S(2)}) collective-permute-start(bf16[2,128,512]{2,1,0:T(8,128)(2,1)} %mine_ref.1), channel_id=1, source_target_pairs={{0,16},{8,24},{16,0},{24,8},{1,17},{9,25},{17,1},{25,9},{2,18},{10... | collective-permute-start | bytes 786440 | tf_op jit(solution)/shard_map/ppermute | solution.py:339
  3.0 16.2 %collective-permute-start.8 = (bf16[2,128,512]{2,1,0:T(8,128)(2,1)}, bf16[2,128,512]{2,1,0:T(8,128)(2,1)S(1)}, u32[]{:S(2)}, u32[]{:S(2)}) collective-permute-start(bf16[2,128,512]{2,1,0:T(8,128)(2,1)} %mine_ref.1), channel_id=1, source_target_pairs={{0,8},{8,0},{16,24},{24,16},{1,9},{9,1},{17,25},{25,17},{2,10},{10... | collective-permute-start | bytes 786440 | tf_op jit(solution)/shard_map/ppermute | solution.py:342
  4.0 15.2 %copy-start.1 = (f32[512]{0:T(512)S(1)}, f32[512]{0:T(512)}, u32[]{:S(2)}) copy-start(f32[512]{0:T(512)} %param.8) | copy-start | bytes 6148
  4.0 8.0 %collective-permute-start.11 = (bf16[64,768]{1,0:T(8,128)(2,1)S(1)}, bf16[64,768]{1,0:T(8,128)(2,1)S(1)}, u32[]{:S(2)}, u32[]{:S(2)}) collective-permute-start(bf16[64,768]{1,0:T(8,128)(2,1)S(1)} %get-tuple-element.23), channel_id=1, source_target_pairs={{6,0},{7,1},{4,2},{5,3},{2,4},{3,5},{0,6},{1,7},{12,8},{13,9},{14,... | collective-permute-start | bytes 294920 | tf_op jit(solution)/shard_map/ppermute | solution.py:351
  9.6 9.7 %collective-permute-start.10 = (bf16[2,128,512]{2,1,0:T(8,128)(2,1)S(1)}, bf16[2,128,512]{2,1,0:T(8,128)(2,1)S(1)}, u32[]{:S(2)}, u32[]{:S(2)}) collective-permute-start(bf16[2,128,512]{2,1,0:T(8,128)(2,1)S(1)} %collective-permute-done.9.other_ref), channel_id=1, source_target_pairs={{0,8},{8,0},{16,24},{24,16},{1,9},{9,1},{17,25},{25,17},{2,10},{10... | collective-permute-start | bytes 786440 | tf_op jit(solution)/shard_map/ppermute | solution.py:342
  9.6 9.7 %copy-start.2 = (s32[2,2]{1,0:T(2,128)S(1)}, s32[2,2]{1,0:T(2,128)}, u32[]{:S(2)}) copy-start(s32[2,2]{1,0:T(2,128)} %tracks_ref.1) | copy-start | bytes 52
  9.6 5.8 %collective-permute-start.2 = (bf16[64,1024]{1,0:T(8,128)(2,1)S(1)}, bf16[64,1024]{1,0:T(8,128)(2,1)S(1)}, u32[]{:S(2)}, u32[]{:S(2)}) collective-permute-start(bf16[64,1024]{1,0:T(8,128)(2,1)S(1)} %get-tuple-element.19.refs_0_), channel_id=1, source_target_pairs={{2,0},{3,1},{0,2},{1,3},{6,4},{7,5},{4,6},{5,7},{11,8},{10,9},{9,1... | collective-permute-start | bytes 393224 | tf_op jit(solution)/shard_map/ppermute | solution.py:351
  11.3 4.6 %collective-permute-start.4 = (bf16[64,1024]{1,0:T(8,128)(2,1)S(1)}, bf16[64,1024]{1,0:T(8,128)(2,1)S(1)}, u32[]{:S(2)}, u32[]{:S(2)}) collective-permute-start(bf16[64,1024]{1,0:T(8,128)(2,1)S(1)} %get-tuple-element.19.refs_0_), channel_id=1, source_target_pairs={{9,8},{8,9},{11,10},{10,11},{13,12},{12,13},{15,14},{14,15},{25,24... | collective-permute-start | bytes 393224 | tf_op jit(solution)/shard_map/ppermute | solution.py:351
  12.0 6.2 %collective-permute-start.13 = (bf16[64,768]{1,0:T(8,128)(2,1)S(1)}, bf16[64,768]{1,0:T(8,128)(2,1)S(1)}, u32[]{:S(2)}, u32[]{:S(2)}) collective-permute-start(bf16[64,768]{1,0:T(8,128)(2,1)S(1)} %collective-permute-done.11.refs_1_), channel_id=1, source_target_pairs={{1,0},{0,1},{3,2},{2,3},{5,4},{4,5},{7,6},{6,7},{9,8},{8,9},{11,10... | collective-permute-start | bytes 294920 | tf_op jit(solution)/shard_map/ppermute | solution.py:351
  15.3 4.8 %collective-permute-start.3 = (bf16[64,1024]{1,0:T(8,128)(2,1)S(1)}, bf16[64,1024]{1,0:T(8,128)(2,1)S(1)}, u32[]{:S(2)}, u32[]{:S(2)}) collective-permute-start(bf16[64,1024]{1,0:T(8,128)(2,1)S(1)} %collective-permute-done.2.refs_3_), channel_id=1, source_target_pairs={{0,8},{8,0},{16,24},{24,16},{1,9},{9,1},{17,25},{25,17},{2,10},{10... | collective-permute-start | bytes 393224 | tf_op jit(solution)/shard_map/ppermute | solution.py:342
  15.9 4.3 %collective-permute-start.5 = (bf16[64,1024]{1,0:T(8,128)(2,1)S(1)}, bf16[64,1024]{1,0:T(8,128)(2,1)S(1)}, u32[]{:S(2)}, u32[]{:S(2)}) collective-permute-start(bf16[64,1024]{1,0:T(8,128)(2,1)S(1)} %collective-permute-done.4.refs_5_), channel_id=1, source_target_pairs={{0,8},{8,0},{16,24},{24,16},{1,9},{9,1},{17,25},{25,17},{2,10},{10... | collective-permute-start | bytes 393224 | tf_op jit(solution)/shard_map/ppermute | solution.py:342
  18.2 2.0 %collective-permute-start.12 = (bf16[64,768]{1,0:T(8,128)(2,1)S(1)}, bf16[64,768]{1,0:T(8,128)(2,1)S(1)}, u32[]{:S(2)}, u32[]{:S(2)}) collective-permute-start(bf16[64,768]{1,0:T(8,128)(2,1)S(1)} %collective-permute-done.11.refs_1_), channel_id=1, source_target_pairs={{0,8},{8,0},{16,24},{24,16},{1,9},{9,1},{17,25},{25,17},{2,10},{10... | collective-permute-start | bytes 294920 | tf_op jit(solution)/shard_map/ppermute | solution.py:342
  19.2 1.3 %collective-permute-start.14 = (bf16[64,768]{1,0:T(8,128)(2,1)S(1)}, bf16[64,768]{1,0:T(8,128)(2,1)S(1)}, u32[]{:S(2)}, u32[]{:S(2)}) collective-permute-start(bf16[64,768]{1,0:T(8,128)(2,1)S(1)} %collective-permute-done.13.refs_7_), channel_id=1, source_target_pairs={{0,8},{8,0},{16,24},{24,16},{1,9},{9,1},{17,25},{25,17},{2,10},{10... | collective-permute-start | bytes 294920 | tf_op jit(solution)/shard_map/ppermute | solution.py:342
  21.5 14.1 %collective-permute-start.15 = (bf16[256,256]{1,0:T(8,128)(2,1)S(1)}, bf16[256,256]{1,0:T(8,128)(2,1)S(1)}, u32[]{:S(2)}, u32[]{:S(2)}) collective-permute-start(bf16[256,256]{1,0:T(8,128)(2,1)S(1)} %get-tuple-element.24.refs_9_), channel_id=1, source_target_pairs={{0,16},{8,24},{16,0},{24,8},{1,17},{9,25},{17,1},{25,9},{2,18},{10... | collective-permute-start | bytes 393224 | tf_op jit(solution)/shard_map/ppermute | solution.py:339
  24.2 12.2 %collective-permute-start.16 = (bf16[256,256]{1,0:T(8,128)(2,1)S(1)}, bf16[256,256]{1,0:T(8,128)(2,1)S(1)}, u32[]{:S(2)}, u32[]{:S(2)}) collective-permute-start(bf16[256,256]{1,0:T(8,128)(2,1)S(1)} %shard_map.77.mine_ref), channel_id=1, source_target_pairs={{0,16},{8,24},{16,0},{24,8},{1,17},{9,25},{17,1},{25,9},{2,18},{10... | collective-permute-start | bytes 393224 | tf_op jit(solution)/shard_map/ppermute | solution.py:339
  24.8 5.7 %collective-permute-start = (bf16[64,256]{1,0:T(8,128)(2,1)S(1)}, bf16[64,256]{1,0:T(8,128)(2,1)S(1)}, u32[]{:S(2)}, u32[]{:S(2)}) collective-permute-start(bf16[64,256]{1,0:T(8,128)(2,1)S(1)} %get-tuple-element.20), channel_id=1, source_target_pairs={{6,0},{7,1},{4,2},{5,3},{2,4},{3,5},{0,6},{1,7},{12,8},{13,9},{14,... | collective-permute-start | bytes 98312 | tf_op jit(solution)/shard_map/ppermute | solution.py:351
  30.5 3.9 %collective-permute-start.6 = (bf16[64,256]{1,0:T(8,128)(2,1)S(1)}, bf16[64,256]{1,0:T(8,128)(2,1)S(1)}, u32[]{:S(2)}, u32[]{:S(2)}) collective-permute-start(bf16[64,256]{1,0:T(8,128)(2,1)S(1)} %collective-permute-done.refs_1_), channel_id=1, source_target_pairs={{1,0},{0,1},{3,2},{2,3},{5,4},{4,5},{7,6},{6,7},{9,8},{8,9},{11,10... | collective-permute-start | bytes 98312 | tf_op jit(solution)/shard_map/ppermute | solution.py:351
  32.0 2.4 %collective-permute-start.1 = (bf16[64,256]{1,0:T(8,128)(2,1)S(1)}, bf16[64,256]{1,0:T(8,128)(2,1)S(1)}, u32[]{:S(2)}, u32[]{:S(2)}) collective-permute-start(bf16[64,256]{1,0:T(8,128)(2,1)S(1)} %collective-permute-done.refs_1_), channel_id=1, source_target_pairs={{0,8},{8,0},{16,24},{24,16},{1,9},{9,1},{17,25},{25,17},{2,10},{10... | collective-permute-start | bytes 98312 | tf_op jit(solution)/shard_map/ppermute | solution.py:342
  34.4 1.2 %collective-permute-start.7 = (bf16[64,256]{1,0:T(8,128)(2,1)S(1)}, bf16[64,256]{1,0:T(8,128)(2,1)S(1)}, u32[]{:S(2)}, u32[]{:S(2)}) collective-permute-start(bf16[64,256]{1,0:T(8,128)(2,1)S(1)} %collective-permute-done.6.refs_7_), channel_id=1, source_target_pairs={{0,8},{8,0},{16,24},{24,16},{1,9},{9,1},{17,25},{25,17},{2,10},{10... | collective-permute-start | bytes 98312 | tf_op jit(solution)/shard_map/ppermute | solution.py:342
  36.2 1.3 %collective-permute-start.18 = (bf16[128,256]{1,0:T(8,128)(2,1)S(1)}, bf16[128,256]{1,0:T(8,128)(2,1)S(1)}, u32[]{:S(2)}, u32[]{:S(2)}) collective-permute-start(bf16[128,256]{1,0:T(8,128)(2,1)S(1)} %get-tuple-element.32), channel_id=1, source_target_pairs={{0,8},{8,0},{16,24},{24,16},{1,9},{9,1},{17,25},{25,17},{2,10},{10... | collective-permute-start | bytes 196616 | tf_op jit(solution)/shard_map/ppermute | solution.py:342
  36.7 1.8 %collective-permute-start.17 = (bf16[128,256]{1,0:T(8,128)(2,1)S(1)}, bf16[128,256]{1,0:T(8,128)(2,1)S(1)}, u32[]{:S(2)}, u32[]{:S(2)}) collective-permute-start(bf16[128,256]{1,0:T(8,128)(2,1)S(1)} %shard_map.79), channel_id=1, source_target_pairs={{0,8},{8,0},{16,24},{24,16},{1,9},{9,1},{17,25},{25,17},{2,10},{10... | collective-permute-start | bytes 196616 | tf_op jit(solution)/shard_map/ppermute | solution.py:342

commit v7 on v6

--- a/solution.py
+++ b/solution.py
@@ -193,15 +193,14 @@
 
 
 def pack_kernel(*refs):
-    sources, outs, sems = refs[:4], refs[4:7], refs[7]
-    span = outs[2].shape[1]
+    sources, out_ref, sems = refs[:-2], refs[-2], refs[-1]
+    span = out_ref.shape[1] // len(sources)
     first = pl.multiple_of(lax.axis_index("tm") // 2 * span, span)
-    parts = [(n, 0, n) for n in range(4)] + [(n, 1, n) for n in range(3)] + [(3, 2, 0)]
     copies = [
         pltpu.make_async_copy(
-            sources[n].at[:, pl.ds(first, span)], outs[o].at[:, pl.ds(m * span, span)], sems.at[k]
-        )
-        for k, (n, o, m) in enumerate(parts)
+            ref.at[:, pl.ds(first, span)], out_ref.at[:, pl.ds(n * span, span)], sems.at[n]
+        )
+        for n, ref in enumerate(sources)
     ]
     for copy in copies:
         copy.start()
@@ -307,14 +306,6 @@
         copy.wait()
 
 
-def final_kernel(received_ref, begun_ref, out_ref):
-    count = received_ref.shape[1]
-    pltpu.sync_copy(
-        received_ref,
-        out_ref.at[1 - lax.axis_index("tm") % 2, :, pl.ds(out_ref.shape[2] - count, count)],
-    )
-
-
 def fits(n_tm, n_agent, features):
     agents_here, rows_here, width = features.shape
     return (
@@ -367,18 +358,19 @@
         )(*args)
 
     half, full = jnp.bfloat16, jnp.float32
-    packed, projections, outward = kernel(
+    (packed,) = kernel(
         pack_kernel,
-        [((width // n_agent, n * span), half) for n in (4, 3, 1)],
+        [((width // n_agent, 4 * span), half)],
         tuple(
             pltpu.with_memory_space_constraint(w, pltpu.HBM)
             for w in (w_query, w_key, w_value, w_out)
         ),
         specs=[pl.BlockSpec(memory_space=pltpu.HBM)] * 4,
-        scratch=[pltpu.SemaphoreType.DMA((8,))],
+        scratch=[pltpu.SemaphoreType.DMA((4,))],
         flops=0,
     )
-    sources = [(6, 4), (2, 3), (None, 1), (7, 5)]
+    projections, outward = packed[:, : 3 * span], packed[:, 3 * span :]
+    sources = [(6, 4), (1, 3), (None, 2), (7, 5)]
     fetched = [fetch(packed if n else projections, pair) for n, pair in enumerate(sources[:3])]
     fetched.append(fetch(fetched[0], (1, 1)))
     out_far = fetch(outward, sources[0])
@@ -451,14 +443,8 @@
         out_spec=anywhere,
         flops=high * span * span,
     )
-    (out,) = kernel(
-        final_kernel,
-        [((2, span // 2, steps), half)],
-        (received, begun),
-        specs=[vmem, anywhere],
-        out_spec=anywhere,
-        aliases={1: 0},
-        flops=0,
+    out = lax.dynamic_update_slice(
+        begun, received[None], (1 - lax.axis_index("tm") % 2, 0, low)
     )
     return out
 

time: 39.3 us -> 38.4 us (0.977)
  starting transfers between devices: 21.8 us -> 20.1 us
  Pallas kernels: 6.18 us -> 5.37 us
  waiting for transfers between devices: 11 us -> 11.8 us
  local copies, waits for them, and re-layouts: 0.01 us -> 0.67 us
    ppermute x10, starting transfers between devices: 4.53 us -> 3.37 us  [swap(): return lax.ppermute(value, 'tm', [(i, i ^ 1) for i in range(n_tm)])]
    ppermute x6, waiting for transfers between devices: 6.91 us -> 8.03 us  [fetch(): return lax.ppermute(value, ('tm', 'agent'), pairs)]
    pallas_call x9 -> x8, Pallas kernels: 6.18 us -> 5.37 us  [kernel(): pl.pallas_call(body, out_shape=[jax.ShapeDtypeStruct(shape, dtype) for sh...]
    dynamic_update_slice x0 -> x1, local copies, waits for them, and re-layouts: none -> 0.64 us  [split_heads(): lax.dynamic_update_slice(begun, received[None], (1 - lax.axis_index('tm')...]
    ppermute x6, starting transfers between devices: 12.1 us -> 11.6 us  [fetch(): return lax.ppermute(value, ('tm', 'agent'), pairs)]
  transfers between devices with their start and end apart: 19 -> 19, of which waited for: 8 -> 7; matrix products, arithmetic and copies ran while one was open for 0% -> 0% of each run, Pallas kernels for 12% -> 12%
where the time goes in v7:
time: 38.4 us; the launch traced here: 38.2 us
  starting transfers between devices  20.1 us (52%)
  waiting for transfers between devices  11.8 us (31%)
  Pallas kernels  5.37 us (14%)
  local copies, waits for them, and re-layouts  0.67 us (2%)
    ppermute x6, starting transfers between devices, fetch(): return lax.ppermute(value, ('tm', 'agent'), pairs)  11.6 us
    ppermute x6, waiting for transfers between devices, fetch(): return lax.ppermute(value, ('tm', 'agent'), pairs)  8.03 us
    pallas_call x8, Pallas kernels, kernel(): pl.pallas_call(body, out_shape=[jax.ShapeDtypeStruct(shape, dtype) for sh...  5.37 us
    ppermute x3, starting transfers between devices, across(): return lax.ppermute(value, 'tm', [(i, i ^ 2) for i in range(n_tm)])  5.15 us
    ppermute x10, starting transfers between devices, swap(): return lax.ppermute(value, 'tm', [(i, i ^ 1) for i in range(n_tm)])  3.37 us
    ppermute x3, waiting for transfers between devices, across(): return lax.ppermute(value, 'tm', [(i, i ^ 2) for i in range(n_tm)])  2.03 us
    ppermute x10, waiting for transfers between devices, swap(): return lax.ppermute(value, 'tm', [(i, i ^ 1) for i in range(n_tm)])  1.79 us
  transfers between devices with their start and end apart: 19, of which 7 were waited for; matrix products, arithmetic and copies ran while one was open for 0% of the time, Pallas kernels for 12%

profile of v7, /device:TPU:0, one launch (start us, length us, event | category | flops | bytes accessed | tf_op | source)
XLA Modules:
  0.0 38.2 jit_solution(10091231558143629804)
XLA Ops:
  0.0 3.0 %collective-permute-start.9 = (bf16[2,128,512]{2,1,0:T(8,128)(2,1)}, bf16[2,128,512]{2,1,0:T(8,128)(2,1)S(1)}, u32[]{:S(2)}, u32[]{:S(2)}) collective-permute-start(bf16[2,128,512]{2,1,0:T(8,128)(2,1)} %mine_ref.1), channel_id=1, source_target_pairs={{0,16},{8,24},{16,0},{24,8},{1,17},{9,25},{17,1},{25,9},{2,18},{10... | collective-permute-start | bytes 786440 | tf_op jit(solution)/shard_map/ppermute | solution.py:330
  3.0 0.8 %shard_map.73.refs_0_ = bf16[64,1024]{1,0:T(8,128)(2,1)S(1)} custom-call(bf16[64,512]{1,0:T(8,128)(2,1)} %refs_0_.1, bf16[64,512]{1,0:T(8,128)(2,1)} %refs_1_.1, bf16[64,512]{1,0:T(8,128)(2,1)} %refs_2_.1, bf16[64,512]{1,0:T(8,128)(2,1)} %refs_3_.1), custom_call_target="tpu_custom_call" | custom-call | bytes 1048576 | tf_op jit(solution)/shard_map/pallas_call | solution.py:349
  3.9 3.7 %collective-permute-start.11 = (bf16[64,768]{1,0:T(8,128)(2,1)S(1)}, bf16[64,768]{1,0:T(8,128)(2,1)S(1)}, u32[]{:S(2)}, u32[]{:S(2)}) collective-permute-start(bf16[64,768]{1,0:T(8,128)(2,1)S(1)} %slice.9), channel_id=1, source_target_pairs={{6,0},{7,1},{4,2},{5,3},{2,4},{3,5},{0,6},{1,7},{12,8},{13,9},{14,... | collective-permute-start | bytes 294920 | tf_op jit(solution)/shard_map/ppermute | solution.py:342
  7.6 2.0 %collective-permute-done.9.other_ref = bf16[2,128,512]{2,1,0:T(8,128)(2,1)S(1)} collective-permute-done((bf16[2,128,512]{2,1,0:T(8,128)(2,1)}, bf16[2,128,512]{2,1,0:T(8,128)(2,1)S(1)}, u32[]{:S(2)}, u32[]{:S(2)}) %collective-permute-start.9) | collective-permute-done | bytes 262176 | tf_op jit(solution)/shard_map/ppermute | solution.py:330
  9.6 1.6 %collective-permute-start.2 = (bf16[64,1024]{1,0:T(8,128)(2,1)S(1)}, bf16[64,1024]{1,0:T(8,128)(2,1)S(1)}, u32[]{:S(2)}, u32[]{:S(2)}) collective-permute-start(bf16[64,1024]{1,0:T(8,128)(2,1)S(1)} %shard_map.73.refs_0_), channel_id=1, source_target_pairs={{1,0},{0,1},{3,2},{2,3},{5,4},{4,5},{7,6},{6,7},{11,8},{10,9},{9,1... | collective-permute-start | bytes 393224 | tf_op jit(solution)/shard_map/ppermute | solution.py:342
  11.2 0.7 %collective-permute-start.4 = (bf16[64,1024]{1,0:T(8,128)(2,1)S(1)}, bf16[64,1024]{1,0:T(8,128)(2,1)S(1)}, u32[]{:S(2)}, u32[]{:S(2)}) collective-permute-start(bf16[64,1024]{1,0:T(8,128)(2,1)S(1)} %shard_map.73.refs_0_), channel_id=1, source_target_pairs={{10,8},{11,9},{8,10},{9,11},{14,12},{15,13},{12,14},{13,15},{26,24... | collective-permute-start | bytes 393224 | tf_op jit(solution)/shard_map/ppermute | solution.py:342
  11.9 0.8 %collective-permute-start.13 = (bf16[64,768]{1,0:T(8,128)(2,1)S(1)}, bf16[64,768]{1,0:T(8,128)(2,1)S(1)}, u32[]{:S(2)}, u32[]{:S(2)}) collective-permute-start(bf16[64,768]{1,0:T(8,128)(2,1)S(1)} %collective-permute-done.11.refs_1_), channel_id=1, source_target_pairs={{1,0},{0,1},{3,2},{2,3},{5,4},{4,5},{7,6},{6,7},{9,8},{8,9},{11,10... | collective-permute-start | bytes 294920 | tf_op jit(solution)/shard_map/ppermute | solution.py:342
  12.7 3.3 %collective-permute-done.2.refs_3_ = bf16[64,1024]{1,0:T(8,128)(2,1)S(1)} collective-permute-done((bf16[64,1024]{1,0:T(8,128)(2,1)S(1)}, bf16[64,1024]{1,0:T(8,128)(2,1)S(1)}, u32[]{:S(2)}, u32[]{:S(2)}) %collective-permute-start.2) | collective-permute-done | bytes 131104 | tf_op jit(solution)/shard_map/ppermute | solution.py:342
  16.0 2.2 %collective-permute-start.5 = (bf16[64,1024]{1,0:T(8,128)(2,1)S(1)}, bf16[64,1024]{1,0:T(8,128)(2,1)S(1)}, u32[]{:S(2)}, u32[]{:S(2)}) collective-permute-start(bf16[64,1024]{1,0:T(8,128)(2,1)S(1)} %collective-permute-done.4.refs_5_), channel_id=1, source_target_pairs={{0,8},{8,0},{16,24},{24,16},{1,9},{9,1},{17,25},{25,17},{2,10},{10... | collective-permute-start | bytes 393224 | tf_op jit(solution)/shard_map/ppermute | solution.py:333
  18.2 0.5 %collective-permute-start.14 = (bf16[64,768]{1,0:T(8,128)(2,1)S(1)}, bf16[64,768]{1,0:T(8,128)(2,1)S(1)}, u32[]{:S(2)}, u32[]{:S(2)}) collective-permute-start(bf16[64,768]{1,0:T(8,128)(2,1)S(1)} %collective-permute-done.13.refs_7_), channel_id=1, source_target_pairs={{0,8},{8,0},{16,24},{24,16},{1,9},{9,1},{17,25},{25,17},{2,10},{10... | collective-permute-start | bytes 294920 | tf_op jit(solution)/shard_map/ppermute | solution.py:333
  18.7 0.8 %shard_map.74 = (bf16[512,512]{1,0:T(8,128)(2,1)S(1)}, s32[2,8,128]{2,1,0:T(8,128)S(1)}) custom-call(s32[2,2]{1,0:T(2,128)S(1)} %copy-done.2, f32[1,512]{1,0:T(1,128)S(1)} %bitcast.3, bf16[2,128,512]{2,1,0:T(8,128)(2,1)S(1)} %copy-done, bf16[2,128,512]{2,1,0:T(8,128)(2,1)S(1)} %collective-permute-done.8.beside_ref, ...), custom_call_target="tpu_custom_call" | custom-call | flops 2097152 | bytes 1048576 | tf_op jit(solution)/shard_map/pallas_call | solution.py:349
  19.6 0.9 %shard_map.75 = (bf16[256,256]{1,0:T(8,128)(2,1)S(1)}, bf16[512,768]{1,0:T(8,128)(2,1)S(1)}, bf16[256,256]{1,0:T(8,128)(2,1)S(1)}, bf16[256,256]{1,0:T(8,128)(2,1)S(1)}) custom-call(s32[2,8,128]{2,1,0:T(8,128)S(1)} %get-tuple-element.16.bounds_ref, bf16[512,512]{1,0:T(8,128)(2,1)S(1)} %get-tuple-element.17.normed_ref, ...), custom_call_target="tpu_custom_call" | custom-call | flops 268435456 | bytes 1048576 | tf_op jit(solution)/shard_map/pallas_call | solution.py:349
  20.6 1.6 %collective-permute-start.15 = (bf16[256,256]{1,0:T(8,128)(2,1)S(1)}, bf16[256,256]{1,0:T(8,128)(2,1)S(1)}, u32[]{:S(2)}, u32[]{:S(2)}) collective-permute-start(bf16[256,256]{1,0:T(8,128)(2,1)S(1)} %get-tuple-element.18.refs_9_), channel_id=1, source_target_pairs={{0,16},{8,24},{16,0},{24,8},{1,17},{9,25},{17,1},{25,9},{2,18},{10... | collective-permute-start | bytes 393224 | tf_op jit(solution)/shard_map/ppermute | solution.py:330
  22.2 1.1 %shard_map.77.mine_ref = bf16[256,256]{1,0:T(8,128)(2,1)S(1)} custom-call(s32[2,8,128]{2,1,0:T(8,128)S(1)} %get-tuple-element.16.bounds_ref, bf16[512,512]{1,0:T(8,128)(2,1)S(1)} %get-tuple-element.17.normed_ref, bf16[512,768]{1,0:T(8,128)(2,1)S(1)} %get-tuple-element.20.weights, bf16[256,256]{1,0:T(8,128)(2,1)S(1)} %get-tuple-element.21.low_keys, ...), custom_call_target="tpu_custom_call" | custom-call | flops 335544320 | bytes 1048576 | tf_op jit(solution)/shard_map/pallas_call | solution.py:349
  23.3 0.6 %collective-permute-start.16 = (bf16[256,256]{1,0:T(8,128)(2,1)S(1)}, bf16[256,256]{1,0:T(8,128)(2,1)S(1)}, u32[]{:S(2)}, u32[]{:S(2)}) collective-permute-start(bf16[256,256]{1,0:T(8,128)(2,1)S(1)} %shard_map.77.mine_ref), channel_id=1, source_target_pairs={{0,16},{8,24},{16,0},{24,8},{1,17},{9,25},{17,1},{25,9},{2,18},{10... | collective-permute-start | bytes 393224 | tf_op jit(solution)/shard_map/ppermute | solution.py:330
  23.9 3.4 %collective-permute-start = (bf16[64,256]{1,0:T(8,128)(2,1)S(1)}, bf16[64,256]{1,0:T(8,128)(2,1)S(1)}, u32[]{:S(2)}, u32[]{:S(2)}) collective-permute-start(bf16[64,256]{1,0:T(8,128)(2,1)S(1)} %slice.8), channel_id=1, source_target_pairs={{6,0},{7,1},{4,2},{5,3},{2,4},{3,5},{0,6},{1,7},{12,8},{13,9},{14,... | collective-permute-start | bytes 98312 | tf_op jit(solution)/shard_map/ppermute | solution.py:342
  27.3 2.3 %collective-permute-done.refs_1_ = bf16[64,256]{1,0:T(8,128)(2,1)S(1)} collective-permute-done((bf16[64,256]{1,0:T(8,128)(2,1)S(1)}, bf16[64,256]{1,0:T(8,128)(2,1)S(1)}, u32[]{:S(2)}, u32[]{:S(2)}) %collective-permute-start) | collective-permute-done | bytes 32800 | tf_op jit(solution)/shard_map/ppermute | solution.py:342
  29.6 1.5 %collective-permute-start.6 = (bf16[64,256]{1,0:T(8,128)(2,1)S(1)}, bf16[64,256]{1,0:T(8,128)(2,1)S(1)}, u32[]{:S(2)}, u32[]{:S(2)}) collective-permute-start(bf16[64,256]{1,0:T(8,128)(2,1)S(1)} %collective-permute-done.refs_1_), channel_id=1, source_target_pairs={{1,0},{0,1},{3,2},{2,3},{5,4},{4,5},{7,6},{6,7},{9,8},{8,9},{11,10... | collective-permute-start | bytes 98312 | tf_op jit(solution)/shard_map/ppermute | solution.py:342
  31.1 2.4 %collective-permute-done.6.refs_7_ = bf16[64,256]{1,0:T(8,128)(2,1)S(1)} collective-permute-done((bf16[64,256]{1,0:T(8,128)(2,1)S(1)}, bf16[64,256]{1,0:T(8,128)(2,1)S(1)}, u32[]{:S(2)}, u32[]{:S(2)}) %collective-permute-start.6) | collective-permute-done | bytes 32800 | tf_op jit(solution)/shard_map/ppermute | solution.py:342
  33.5 1.2 %collective-permute-done.7.refs_8_ = bf16[64,256]{1,0:T(8,128)(2,1)S(1)} collective-permute-done((bf16[64,256]{1,0:T(8,128)(2,1)S(1)}, bf16[64,256]{1,0:T(8,128)(2,1)S(1)}, u32[]{:S(2)}, u32[]{:S(2)}) %collective-permute-start.7) | collective-permute-done | bytes 32800 | tf_op jit(solution)/shard_map/ppermute | solution.py:333
  35.8 0.4 %collective-permute-start.18 = (bf16[128,256]{1,0:T(8,128)(2,1)S(1)}, bf16[128,256]{1,0:T(8,128)(2,1)S(1)}, u32[]{:S(2)}, u32[]{:S(2)}) collective-permute-start(bf16[128,256]{1,0:T(8,128)(2,1)S(1)} %shard_map.80), channel_id=1, source_target_pairs={{0,8},{8,0},{16,24},{24,16},{1,9},{9,1},{17,25},{25,17},{2,10},{10... | collective-permute-start | bytes 196616 | tf_op jit(solution)/shard_map/ppermute | solution.py:333
  36.2 0.5 %collective-permute-done.17.received_ref = bf16[128,256]{1,0:T(8,128)(2,1)S(1)} collective-permute-done((bf16[128,256]{1,0:T(8,128)(2,1)S(1)}, bf16[128,256]{1,0:T(8,128)(2,1)S(1)}, u32[]{:S(2)}, u32[]{:S(2)}) %collective-permute-start.17) | collective-permute-done | bytes 65568 | tf_op jit(solution)/shard_map/ppermute | solution.py:333
  36.7 0.9 %shard_map.79 = bf16[2,128,512]{2,1,0:T(8,128)(2,1)} custom-call(bf16[512,256]{1,0:T(8,128)(2,1)S(1)} %get-tuple-element.19.weights, f32[128,256]{1,0:T(8,128)S(1)} %get-tuple-element.23.partial_ref, bf16[256,256]{1,0:T(8,128)(2,1)S(1)} %collective-permute-done.16.other_ref, bf16[128,256]{1,0:T(8,128)(2,1)S(1)} %get-tuple-element.24.low_ref, ...), custom_call_target="tpu_custom_call" | custom-call | flops 16777216 | bytes 1048576 | tf_op jit(solution)/shard_map/pallas_call | solution.py:349
  37.5 0.6 %bitcast_dynamic-update-slice_fusion = bf16[2,128,512]{2,1,0:T(8,128)(2,1)} fusion(bf16[2,128,512]{2,1,0:T(8,128)(2,1)} %shard_map.79, s32[]{:T(128)S(6)} %select_n.11, bf16[128,256]{1,0:T(8,128)(2,1)S(1)} %collective-permute-done.18), kind=kLoop, calls=%fused_computation | loop fusion | bytes 131076 | tf_op jit(solution)/shard_map/dynamic_update_slice | solution.py:446
  (31 shorter events, 1.2 us)
Async XLA Ops:
  0.0 18.7 %copy-start = (bf16[2,128,512]{2,1,0:T(8,128)(2,1)S(1)}, bf16[2,128,512]{2,1,0:T(8,128)(2,1)}, u32[]{:S(2)}) copy-start(bf16[2,128,512]{2,1,0:T(8,128)(2,1)} %mine_ref.1) | copy-start | bytes 786436
  0.0 9.6 %collective-permute-start.9 = (bf16[2,128,512]{2,1,0:T(8,128)(2,1)}, bf16[2,128,512]{2,1,0:T(8,128)(2,1)S(1)}, u32[]{:S(2)}, u32[]{:S(2)}) collective-permute-start(bf16[2,128,512]{2,1,0:T(8,128)(2,1)} %mine_ref.1), channel_id=1, source_target_pairs={{0,16},{8,24},{16,0},{24,8},{1,17},{9,25},{17,1},{25,9},{2,18},{10... | collective-permute-start | bytes 786440 | tf_op jit(solution)/shard_map/ppermute | solution.py:330
  3.0 15.2 %collective-permute-start.8 = (bf16[2,128,512]{2,1,0:T(8,128)(2,1)}, bf16[2,128,512]{2,1,0:T(8,128)(2,1)S(1)}, u32[]{:S(2)}, u32[]{:S(2)}) collective-permute-start(bf16[2,128,512]{2,1,0:T(8,128)(2,1)} %mine_ref.1), channel_id=1, source_target_pairs={{0,8},{8,0},{16,24},{24,16},{1,9},{9,1},{17,25},{25,17},{2,10},{10... | collective-permute-start | bytes 786440 | tf_op jit(solution)/shard_map/ppermute | solution.py:333
  3.8 14.8 %copy-start.1 = (f32[512]{0:T(512)S(1)}, f32[512]{0:T(512)}, u32[]{:S(2)}) copy-start(f32[512]{0:T(512)} %param.8) | copy-start | bytes 6148
  3.9 14.8 %copy-start.2 = (s32[2,2]{1,0:T(2,128)S(1)}, s32[2,2]{1,0:T(2,128)}, u32[]{:S(2)}) copy-start(s32[2,2]{1,0:T(2,128)} %tracks_ref.1) | copy-start | bytes 52
  3.9 8.0 %collective-permute-start.11 = (bf16[64,768]{1,0:T(8,128)(2,1)S(1)}, bf16[64,768]{1,0:T(8,128)(2,1)S(1)}, u32[]{:S(2)}, u32[]{:S(2)}) collective-permute-start(bf16[64,768]{1,0:T(8,128)(2,1)S(1)} %slice.9), channel_id=1, source_target_pairs={{6,0},{7,1},{4,2},{5,3},{2,4},{3,5},{0,6},{1,7},{12,8},{13,9},{14,... | collective-permute-start | bytes 294920 | tf_op jit(solution)/shard_map/ppermute | solution.py:342
  9.6 9.1 %collective-permute-start.10 = (bf16[2,128,512]{2,1,0:T(8,128)(2,1)S(1)}, bf16[2,128,512]{2,1,0:T(8,128)(2,1)S(1)}, u32[]{:S(2)}, u32[]{:S(2)}) collective-permute-start(bf16[2,128,512]{2,1,0:T(8,128)(2,1)S(1)} %collective-permute-done.9.other_ref), channel_id=1, source_target_pairs={{0,8},{8,0},{16,24},{24,16},{1,9},{9,1},{17,25},{25,17},{2,10},{10... | collective-permute-start | bytes 786440 | tf_op jit(solution)/shard_map/ppermute | solution.py:333
  9.6 6.4 %collective-permute-start.2 = (bf16[64,1024]{1,0:T(8,128)(2,1)S(1)}, bf16[64,1024]{1,0:T(8,128)(2,1)S(1)}, u32[]{:S(2)}, u32[]{:S(2)}) collective-permute-start(bf16[64,1024]{1,0:T(8,128)(2,1)S(1)} %shard_map.73.refs_0_), channel_id=1, source_target_pairs={{1,0},{0,1},{3,2},{2,3},{5,4},{4,5},{7,6},{6,7},{11,8},{10,9},{9,1... | collective-permute-start | bytes 393224 | tf_op jit(solution)/shard_map/ppermute | solution.py:342
  11.2 4.7 %collective-permute-start.4 = (bf16[64,1024]{1,0:T(8,128)(2,1)S(1)}, bf16[64,1024]{1,0:T(8,128)(2,1)S(1)}, u32[]{:S(2)}, u32[]{:S(2)}) collective-permute-start(bf16[64,1024]{1,0:T(8,128)(2,1)S(1)} %shard_map.73.refs_0_), channel_id=1, source_target_pairs={{10,8},{11,9},{8,10},{9,11},{14,12},{15,13},{12,14},{13,15},{26,24... | collective-permute-start | bytes 393224 | tf_op jit(solution)/shard_map/ppermute | solution.py:342
  11.9 6.3 %collective-permute-start.13 = (bf16[64,768]{1,0:T(8,128)(2,1)S(1)}, bf16[64,768]{1,0:T(8,128)(2,1)S(1)}, u32[]{:S(2)}, u32[]{:S(2)}) collective-permute-start(bf16[64,768]{1,0:T(8,128)(2,1)S(1)} %collective-permute-done.11.refs_1_), channel_id=1, source_target_pairs={{1,0},{0,1},{3,2},{2,3},{5,4},{4,5},{7,6},{6,7},{9,8},{8,9},{11,10... | collective-permute-start | bytes 294920 | tf_op jit(solution)/shard_map/ppermute | solution.py:342
  16.0 3.5 %collective-permute-start.3 = (bf16[64,1024]{1,0:T(8,128)(2,1)S(1)}, bf16[64,1024]{1,0:T(8,128)(2,1)S(1)}, u32[]{:S(2)}, u32[]{:S(2)}) collective-permute-start(bf16[64,1024]{1,0:T(8,128)(2,1)S(1)} %collective-permute-done.2.refs_3_), channel_id=1, source_target_pairs={{0,8},{8,0},{16,24},{24,16},{1,9},{9,1},{17,25},{25,17},{2,10},{10... | collective-permute-start | bytes 393224 | tf_op jit(solution)/shard_map/ppermute | solution.py:333
  16.0 3.6 %collective-permute-start.5 = (bf16[64,1024]{1,0:T(8,128)(2,1)S(1)}, bf16[64,1024]{1,0:T(8,128)(2,1)S(1)}, u32[]{:S(2)}, u32[]{:S(2)}) collective-permute-start(bf16[64,1024]{1,0:T(8,128)(2,1)S(1)} %collective-permute-done.4.refs_5_), channel_id=1, source_target_pairs={{0,8},{8,0},{16,24},{24,16},{1,9},{9,1},{17,25},{25,17},{2,10},{10... | collective-permute-start | bytes 393224 | tf_op jit(solution)/shard_map/ppermute | solution.py:333
  18.2 1.3 %collective-permute-start.12 = (bf16[64,768]{1,0:T(8,128)(2,1)S(1)}, bf16[64,768]{1,0:T(8,128)(2,1)S(1)}, u32[]{:S(2)}, u32[]{:S(2)}) collective-permute-start(bf16[64,768]{1,0:T(8,128)(2,1)S(1)} %collective-permute-done.11.refs_1_), channel_id=1, source_target_pairs={{0,8},{8,0},{16,24},{24,16},{1,9},{9,1},{17,25},{25,17},{2,10},{10... | collective-permute-start | bytes 294920 | tf_op jit(solution)/shard_map/ppermute | solution.py:333
  18.2 1.5 %collective-permute-start.14 = (bf16[64,768]{1,0:T(8,128)(2,1)S(1)}, bf16[64,768]{1,0:T(8,128)(2,1)S(1)}, u32[]{:S(2)}, u32[]{:S(2)}) collective-permute-start(bf16[64,768]{1,0:T(8,128)(2,1)S(1)} %collective-permute-done.13.refs_7_), channel_id=1, source_target_pairs={{0,8},{8,0},{16,24},{24,16},{1,9},{9,1},{17,25},{25,17},{2,10},{10... | collective-permute-start | bytes 294920 | tf_op jit(solution)/shard_map/ppermute | solution.py:333
  20.6 14.1 %collective-permute-start.15 = (bf16[256,256]{1,0:T(8,128)(2,1)S(1)}, bf16[256,256]{1,0:T(8,128)(2,1)S(1)}, u32[]{:S(2)}, u32[]{:S(2)}) collective-permute-start(bf16[256,256]{1,0:T(8,128)(2,1)S(1)} %get-tuple-element.18.refs_9_), channel_id=1, source_target_pairs={{0,16},{8,24},{16,0},{24,8},{1,17},{9,25},{17,1},{25,9},{2,18},{10... | collective-permute-start | bytes 393224 | tf_op jit(solution)/shard_map/ppermute | solution.py:330
  23.3 12.2 %collective-permute-start.16 = (bf16[256,256]{1,0:T(8,128)(2,1)S(1)}, bf16[256,256]{1,0:T(8,128)(2,1)S(1)}, u32[]{:S(2)}, u32[]{:S(2)}) collective-permute-start(bf16[256,256]{1,0:T(8,128)(2,1)S(1)} %shard_map.77.mine_ref), channel_id=1, source_target_pairs={{0,16},{8,24},{16,0},{24,8},{1,17},{9,25},{17,1},{25,9},{2,18},{10... | collective-permute-start | bytes 393224 | tf_op jit(solution)/shard_map/ppermute | solution.py:330
  23.9 5.7 %collective-permute-start = (bf16[64,256]{1,0:T(8,128)(2,1)S(1)}, bf16[64,256]{1,0:T(8,128)(2,1)S(1)}, u32[]{:S(2)}, u32[]{:S(2)}) collective-permute-start(bf16[64,256]{1,0:T(8,128)(2,1)S(1)} %slice.8), channel_id=1, source_target_pairs={{6,0},{7,1},{4,2},{5,3},{2,4},{3,5},{0,6},{1,7},{12,8},{13,9},{14,... | collective-permute-start | bytes 98312 | tf_op jit(solution)/shard_map/ppermute | solution.py:342
  29.6 3.9 %collective-permute-start.6 = (bf16[64,256]{1,0:T(8,128)(2,1)S(1)}, bf16[64,256]{1,0:T(8,128)(2,1)S(1)}, u32[]{:S(2)}, u32[]{:S(2)}) collective-permute-start(bf16[64,256]{1,0:T(8,128)(2,1)S(1)} %collective-permute-done.refs_1_), channel_id=1, source_target_pairs={{1,0},{0,1},{3,2},{2,3},{5,4},{4,5},{7,6},{6,7},{9,8},{8,9},{11,10... | collective-permute-start | bytes 98312 | tf_op jit(solution)/shard_map/ppermute | solution.py:342
  31.1 2.4 %collective-permute-start.1 = (bf16[64,256]{1,0:T(8,128)(2,1)S(1)}, bf16[64,256]{1,0:T(8,128)(2,1)S(1)}, u32[]{:S(2)}, u32[]{:S(2)}) collective-permute-start(bf16[64,256]{1,0:T(8,128)(2,1)S(1)} %collective-permute-done.refs_1_), channel_id=1, source_target_pairs={{0,8},{8,0},{16,24},{24,16},{1,9},{9,1},{17,25},{25,17},{2,10},{10... | collective-permute-start | bytes 98312 | tf_op jit(solution)/shard_map/ppermute | solution.py:333
  33.5 1.2 %collective-permute-start.7 = (bf16[64,256]{1,0:T(8,128)(2,1)S(1)}, bf16[64,256]{1,0:T(8,128)(2,1)S(1)}, u32[]{:S(2)}, u32[]{:S(2)}) collective-permute-start(bf16[64,256]{1,0:T(8,128)(2,1)S(1)} %collective-permute-done.6.refs_7_), channel_id=1, source_target_pairs={{0,8},{8,0},{16,24},{24,16},{1,9},{9,1},{17,25},{25,17},{2,10},{10... | collective-permute-start | bytes 98312 | tf_op jit(solution)/shard_map/ppermute | solution.py:333
  35.3 1.3 %collective-permute-start.17 = (bf16[128,256]{1,0:T(8,128)(2,1)S(1)}, bf16[128,256]{1,0:T(8,128)(2,1)S(1)}, u32[]{:S(2)}, u32[]{:S(2)}) collective-permute-start(bf16[128,256]{1,0:T(8,128)(2,1)S(1)} %get-tuple-element.25), channel_id=1, source_target_pairs={{0,8},{8,0},{16,24},{24,16},{1,9},{9,1},{17,25},{25,17},{2,10},{10... | collective-permute-start | bytes 196616 | tf_op jit(solution)/shard_map/ppermute | solution.py:333
  35.8 1.8 %collective-permute-start.18 = (bf16[128,256]{1,0:T(8,128)(2,1)S(1)}, bf16[128,256]{1,0:T(8,128)(2,1)S(1)}, u32[]{:S(2)}, u32[]{:S(2)}) collective-permute-start(bf16[128,256]{1,0:T(8,128)(2,1)S(1)} %shard_map.80), channel_id=1, source_target_pairs={{0,8},{8,0},{16,24},{24,16},{1,9},{9,1},{17,25},{25,17},{2,10},{10... | collective-permute-start | bytes 196616 | tf_op jit(solution)/shard_map/ppermute | solution.py:333

commit v8 on v7

--- a/solution.py
+++ b/solution.py
@@ -213,17 +213,22 @@
     agent = lax.axis_index("agent")
     core = lax.axis_index("tm") % 2
 
-    def put(ref, index):
-        rows = pl.ds(pl.multiple_of(index * depth, depth), depth)
+    def read(ref):
         low = min(begin, ref.shape[1] - columns)
-        target[rows, :] = ref[:, low : low + columns]
-
-    put(refs[0], agent)
-    for n, pair in enumerate(sources):
-        for here in (0, 1):
-            for ref, offset in zip(refs[1 + 2 * n : 3 + 2 * n], (pair[here], pair[1 - here])):
-                if offset is not None:
-                    pl.when(core == here)(functools.partial(put, ref, agent ^ offset))
+        return ref[:, low : low + columns]
+
+    def put(value, offset):
+        rows = pl.ds(pl.multiple_of((agent ^ offset) * depth, depth), depth)
+        target[rows, :] = value
+
+    put(read(refs[0]), 0)
+    for n, (first, second) in enumerate(sources):
+        fetched, swapped = refs[1 + 2 * n : 3 + 2 * n]
+        if first is None:
+            put(jnp.where(core == 0, read(swapped), read(fetched)), second)
+        else:
+            put(read(fetched), jnp.where(core == 0, first, second))
+            put(read(swapped), jnp.where(core == 0, second, first))
 
 
 def project_rows(normed, weights, queries, keys, values):

time: 38.4 us -> 38.3 us (level)
  no operation moved by 1% of the time
where the time goes in v8:
time: 38.3 us; the launch traced here: 38.1 us
  starting transfers between devices  20.1 us (52%)
  waiting for transfers between devices  11.9 us (31%)
  Pallas kernels  5.32 us (14%)
  local copies, waits for them, and re-layouts  0.67 us (2%)
    ppermute x6, starting transfers between devices, fetch(): return lax.ppermute(value, ('tm', 'agent'), pairs)  11.6 us
    ppermute x6, waiting for transfers between devices, fetch(): return lax.ppermute(value, ('tm', 'agent'), pairs)  8.04 us
    pallas_call x8, Pallas kernels, kernel(): pl.pallas_call(body, out_shape=[jax.ShapeDtypeStruct(shape, dtype) for sh...  5.32 us
    ppermute x3, starting transfers between devices, across(): return lax.ppermute(value, 'tm', [(i, i ^ 2) for i in range(n_tm)])  5.15 us
    ppermute x10, starting transfers between devices, swap(): return lax.ppermute(value, 'tm', [(i, i ^ 1) for i in range(n_tm)])  3.37 us
    ppermute x3, waiting for transfers between devices, across(): return lax.ppermute(value, 'tm', [(i, i ^ 2) for i in range(n_tm)])  2.03 us
    ppermute x10, waiting for transfers between devices, swap(): return lax.ppermute(value, 'tm', [(i, i ^ 1) for i in range(n_tm)])  1.79 us
  transfers between devices with their start and end apart: 19, of which 7 were waited for; matrix products, arithmetic and copies ran while one was open for 0% of the time, Pallas kernels for 12%

profile of v8, /device:TPU:0, one launch (start us, length us, event | category | flops | bytes accessed | tf_op | source)
XLA Modules:
  0.0 38.1 jit_solution(14953475987511318407)
XLA Ops:
  0.0 3.0 %collective-permute-start.9 = (bf16[2,128,512]{2,1,0:T(8,128)(2,1)}, bf16[2,128,512]{2,1,0:T(8,128)(2,1)S(1)}, u32[]{:S(2)}, u32[]{:S(2)}) collective-permute-start(bf16[2,128,512]{2,1,0:T(8,128)(2,1)} %mine_ref.1), channel_id=1, source_target_pairs={{0,16},{8,24},{16,0},{24,8},{1,17},{9,25},{17,1},{25,9},{2,18},{10... | collective-permute-start | bytes 786440 | tf_op jit(solution)/shard_map/ppermute | solution.py:335
  3.0 0.8 %shard_map.73.refs_0_ = bf16[64,1024]{1,0:T(8,128)(2,1)S(1)} custom-call(bf16[64,512]{1,0:T(8,128)(2,1)} %refs_0_.1, bf16[64,512]{1,0:T(8,128)(2,1)} %refs_1_.1, bf16[64,512]{1,0:T(8,128)(2,1)} %refs_2_.1, bf16[64,512]{1,0:T(8,128)(2,1)} %refs_3_.1), custom_call_target="tpu_custom_call" | custom-call | bytes 1048576 | tf_op jit(solution)/shard_map/pallas_call | solution.py:354
  3.9 3.7 %collective-permute-start.11 = (bf16[64,768]{1,0:T(8,128)(2,1)S(1)}, bf16[64,768]{1,0:T(8,128)(2,1)S(1)}, u32[]{:S(2)}, u32[]{:S(2)}) collective-permute-start(bf16[64,768]{1,0:T(8,128)(2,1)S(1)} %slice.9), channel_id=1, source_target_pairs={{6,0},{7,1},{4,2},{5,3},{2,4},{3,5},{0,6},{1,7},{12,8},{13,9},{14,... | collective-permute-start | bytes 294920 | tf_op jit(solution)/shard_map/ppermute | solution.py:347
  7.6 2.0 %collective-permute-done.9.other_ref = bf16[2,128,512]{2,1,0:T(8,128)(2,1)S(1)} collective-permute-done((bf16[2,128,512]{2,1,0:T(8,128)(2,1)}, bf16[2,128,512]{2,1,0:T(8,128)(2,1)S(1)}, u32[]{:S(2)}, u32[]{:S(2)}) %collective-permute-start.9) | collective-permute-done | bytes 262176 | tf_op jit(solution)/shard_map/ppermute | solution.py:335
  9.6 1.6 %collective-permute-start.2 = (bf16[64,1024]{1,0:T(8,128)(2,1)S(1)}, bf16[64,1024]{1,0:T(8,128)(2,1)S(1)}, u32[]{:S(2)}, u32[]{:S(2)}) collective-permute-start(bf16[64,1024]{1,0:T(8,128)(2,1)S(1)} %shard_map.73.refs_0_), channel_id=1, source_target_pairs={{1,0},{0,1},{3,2},{2,3},{5,4},{4,5},{7,6},{6,7},{11,8},{10,9},{9,1... | collective-permute-start | bytes 393224 | tf_op jit(solution)/shard_map/ppermute | solution.py:347
  11.2 0.7 %collective-permute-start.4 = (bf16[64,1024]{1,0:T(8,128)(2,1)S(1)}, bf16[64,1024]{1,0:T(8,128)(2,1)S(1)}, u32[]{:S(2)}, u32[]{:S(2)}) collective-permute-start(bf16[64,1024]{1,0:T(8,128)(2,1)S(1)} %shard_map.73.refs_0_), channel_id=1, source_target_pairs={{10,8},{11,9},{8,10},{9,11},{14,12},{15,13},{12,14},{13,15},{26,24... | collective-permute-start | bytes 393224 | tf_op jit(solution)/shard_map/ppermute | solution.py:347
  11.9 0.8 %collective-permute-start.13 = (bf16[64,768]{1,0:T(8,128)(2,1)S(1)}, bf16[64,768]{1,0:T(8,128)(2,1)S(1)}, u32[]{:S(2)}, u32[]{:S(2)}) collective-permute-start(bf16[64,768]{1,0:T(8,128)(2,1)S(1)} %collective-permute-done.11.refs_1_), channel_id=1, source_target_pairs={{1,0},{0,1},{3,2},{2,3},{5,4},{4,5},{7,6},{6,7},{9,8},{8,9},{11,10... | collective-permute-start | bytes 294920 | tf_op jit(solution)/shard_map/ppermute | solution.py:347
  12.7 3.3 %collective-permute-done.2.refs_3_ = bf16[64,1024]{1,0:T(8,128)(2,1)S(1)} collective-permute-done((bf16[64,1024]{1,0:T(8,128)(2,1)S(1)}, bf16[64,1024]{1,0:T(8,128)(2,1)S(1)}, u32[]{:S(2)}, u32[]{:S(2)}) %collective-permute-start.2) | collective-permute-done | bytes 131104 | tf_op jit(solution)/shard_map/ppermute | solution.py:347
  16.0 2.2 %collective-permute-start.5 = (bf16[64,1024]{1,0:T(8,128)(2,1)S(1)}, bf16[64,1024]{1,0:T(8,128)(2,1)S(1)}, u32[]{:S(2)}, u32[]{:S(2)}) collective-permute-start(bf16[64,1024]{1,0:T(8,128)(2,1)S(1)} %collective-permute-done.4.refs_5_), channel_id=1, source_target_pairs={{0,8},{8,0},{16,24},{24,16},{1,9},{9,1},{17,25},{25,17},{2,10},{10... | collective-permute-start | bytes 393224 | tf_op jit(solution)/shard_map/ppermute | solution.py:338
  18.2 0.5 %collective-permute-start.14 = (bf16[64,768]{1,0:T(8,128)(2,1)S(1)}, bf16[64,768]{1,0:T(8,128)(2,1)S(1)}, u32[]{:S(2)}, u32[]{:S(2)}) collective-permute-start(bf16[64,768]{1,0:T(8,128)(2,1)S(1)} %collective-permute-done.13.refs_7_), channel_id=1, source_target_pairs={{0,8},{8,0},{16,24},{24,16},{1,9},{9,1},{17,25},{25,17},{2,10},{10... | collective-permute-start | bytes 294920 | tf_op jit(solution)/shard_map/ppermute | solution.py:338
  18.7 0.8 %shard_map.74 = (bf16[512,512]{1,0:T(8,128)(2,1)S(1)}, s32[2,8,128]{2,1,0:T(8,128)S(1)}) custom-call(s32[2,2]{1,0:T(2,128)S(1)} %copy-done.2, f32[1,512]{1,0:T(1,128)S(1)} %bitcast.3, bf16[2,128,512]{2,1,0:T(8,128)(2,1)S(1)} %copy-done, bf16[2,128,512]{2,1,0:T(8,128)(2,1)S(1)} %collective-permute-done.8.beside_ref, ...), custom_call_target="tpu_custom_call" | custom-call | flops 2097152 | bytes 1048576 | tf_op jit(solution)/shard_map/pallas_call | solution.py:354
  19.6 0.9 %shard_map.75 = (bf16[256,256]{1,0:T(8,128)(2,1)S(1)}, bf16[512,768]{1,0:T(8,128)(2,1)S(1)}, bf16[256,256]{1,0:T(8,128)(2,1)S(1)}, bf16[256,256]{1,0:T(8,128)(2,1)S(1)}) custom-call(s32[2,8,128]{2,1,0:T(8,128)S(1)} %get-tuple-element.16.bounds_ref, bf16[512,512]{1,0:T(8,128)(2,1)S(1)} %get-tuple-element.17.normed_ref, ...), custom_call_target="tpu_custom_call" | custom-call | flops 268435456 | bytes 1048576 | tf_op jit(solution)/shard_map/pallas_call | solution.py:354
  20.6 1.6 %collective-permute-start.15 = (bf16[256,256]{1,0:T(8,128)(2,1)S(1)}, bf16[256,256]{1,0:T(8,128)(2,1)S(1)}, u32[]{:S(2)}, u32[]{:S(2)}) collective-permute-start(bf16[256,256]{1,0:T(8,128)(2,1)S(1)} %get-tuple-element.18.refs_9_), channel_id=1, source_target_pairs={{0,16},{8,24},{16,0},{24,8},{1,17},{9,25},{17,1},{25,9},{2,18},{10... | collective-permute-start | bytes 393224 | tf_op jit(solution)/shard_map/ppermute | solution.py:335
  22.2 1.1 %shard_map.77.mine_ref = bf16[256,256]{1,0:T(8,128)(2,1)S(1)} custom-call(s32[2,8,128]{2,1,0:T(8,128)S(1)} %get-tuple-element.16.bounds_ref, bf16[512,512]{1,0:T(8,128)(2,1)S(1)} %get-tuple-element.17.normed_ref, bf16[512,768]{1,0:T(8,128)(2,1)S(1)} %get-tuple-element.20.weights, bf16[256,256]{1,0:T(8,128)(2,1)S(1)} %get-tuple-element.21.low_keys, ...), custom_call_target="tpu_custom_call" | custom-call | flops 335544320 | bytes 1048576 | tf_op jit(solution)/shard_map/pallas_call | solution.py:354
  23.3 0.6 %collective-permute-start.16 = (bf16[256,256]{1,0:T(8,128)(2,1)S(1)}, bf16[256,256]{1,0:T(8,128)(2,1)S(1)}, u32[]{:S(2)}, u32[]{:S(2)}) collective-permute-start(bf16[256,256]{1,0:T(8,128)(2,1)S(1)} %shard_map.77.mine_ref), channel_id=1, source_target_pairs={{0,16},{8,24},{16,0},{24,8},{1,17},{9,25},{17,1},{25,9},{2,18},{10... | collective-permute-start | bytes 393224 | tf_op jit(solution)/shard_map/ppermute | solution.py:335
  23.9 3.4 %collective-permute-start = (bf16[64,256]{1,0:T(8,128)(2,1)S(1)}, bf16[64,256]{1,0:T(8,128)(2,1)S(1)}, u32[]{:S(2)}, u32[]{:S(2)}) collective-permute-start(bf16[64,256]{1,0:T(8,128)(2,1)S(1)} %slice.8), channel_id=1, source_target_pairs={{6,0},{7,1},{4,2},{5,3},{2,4},{3,5},{0,6},{1,7},{12,8},{13,9},{14,... | collective-permute-start | bytes 98312 | tf_op jit(solution)/shard_map/ppermute | solution.py:347
  27.2 2.4 %collective-permute-done.refs_1_ = bf16[64,256]{1,0:T(8,128)(2,1)S(1)} collective-permute-done((bf16[64,256]{1,0:T(8,128)(2,1)S(1)}, bf16[64,256]{1,0:T(8,128)(2,1)S(1)}, u32[]{:S(2)}, u32[]{:S(2)}) %collective-permute-start) | collective-permute-done | bytes 32800 | tf_op jit(solution)/shard_map/ppermute | solution.py:347
  29.6 1.5 %collective-permute-start.6 = (bf16[64,256]{1,0:T(8,128)(2,1)S(1)}, bf16[64,256]{1,0:T(8,128)(2,1)S(1)}, u32[]{:S(2)}, u32[]{:S(2)}) collective-permute-start(bf16[64,256]{1,0:T(8,128)(2,1)S(1)} %collective-permute-done.refs_1_), channel_id=1, source_target_pairs={{1,0},{0,1},{3,2},{2,3},{5,4},{4,5},{7,6},{6,7},{9,8},{8,9},{11,10... | collective-permute-start | bytes 98312 | tf_op jit(solution)/shard_map/ppermute | solution.py:347
  31.1 2.4 %collective-permute-done.6.refs_7_ = bf16[64,256]{1,0:T(8,128)(2,1)S(1)} collective-permute-done((bf16[64,256]{1,0:T(8,128)(2,1)S(1)}, bf16[64,256]{1,0:T(8,128)(2,1)S(1)}, u32[]{:S(2)}, u32[]{:S(2)}) %collective-permute-start.6) | collective-permute-done | bytes 32800 | tf_op jit(solution)/shard_map/ppermute | solution.py:347
  33.5 1.2 %collective-permute-done.7.refs_8_ = bf16[64,256]{1,0:T(8,128)(2,1)S(1)} collective-permute-done((bf16[64,256]{1,0:T(8,128)(2,1)S(1)}, bf16[64,256]{1,0:T(8,128)(2,1)S(1)}, u32[]{:S(2)}, u32[]{:S(2)}) %collective-permute-start.7) | collective-permute-done | bytes 32800 | tf_op jit(solution)/shard_map/ppermute | solution.py:338
  35.7 0.4 %collective-permute-start.18 = (bf16[128,256]{1,0:T(8,128)(2,1)S(1)}, bf16[128,256]{1,0:T(8,128)(2,1)S(1)}, u32[]{:S(2)}, u32[]{:S(2)}) collective-permute-start(bf16[128,256]{1,0:T(8,128)(2,1)S(1)} %shard_map.80), channel_id=1, source_target_pairs={{0,8},{8,0},{16,24},{24,16},{1,9},{9,1},{17,25},{25,17},{2,10},{10... | collective-permute-start | bytes 196616 | tf_op jit(solution)/shard_map/ppermute | solution.py:338
  36.1 0.5 %collective-permute-done.17.received_ref = bf16[128,256]{1,0:T(8,128)(2,1)S(1)} collective-permute-done((bf16[128,256]{1,0:T(8,128)(2,1)S(1)}, bf16[128,256]{1,0:T(8,128)(2,1)S(1)}, u32[]{:S(2)}, u32[]{:S(2)}) %collective-permute-start.17) | collective-permute-done | bytes 65568 | tf_op jit(solution)/shard_map/ppermute | solution.py:338
  36.6 0.9 %shard_map.79 = bf16[2,128,512]{2,1,0:T(8,128)(2,1)} custom-call(bf16[512,256]{1,0:T(8,128)(2,1)S(1)} %get-tuple-element.19.weights, f32[128,256]{1,0:T(8,128)S(1)} %get-tuple-element.23.partial_ref, bf16[256,256]{1,0:T(8,128)(2,1)S(1)} %collective-permute-done.16.other_ref, bf16[128,256]{1,0:T(8,128)(2,1)S(1)} %get-tuple-element.24.low_ref, ...), custom_call_target="tpu_custom_call" | custom-call | flops 16777216 | bytes 1048576 | tf_op jit(solution)/shard_map/pallas_call | solution.py:354
  37.5 0.6 %bitcast_dynamic-update-slice_fusion = bf16[2,128,512]{2,1,0:T(8,128)(2,1)} fusion(bf16[2,128,512]{2,1,0:T(8,128)(2,1)} %shard_map.79, s32[]{:T(128)S(6)} %select_n.11, bf16[128,256]{1,0:T(8,128)(2,1)S(1)} %collective-permute-done.18), kind=kLoop, calls=%fused_computation | loop fusion | bytes 131076 | tf_op jit(solution)/shard_map/dynamic_update_slice | solution.py:451
  (31 shorter events, 1.2 us)
Async XLA Ops:
  0.0 18.7 %copy-start = (bf16[2,128,512]{2,1,0:T(8,128)(2,1)S(1)}, bf16[2,128,512]{2,1,0:T(8,128)(2,1)}, u32[]{:S(2)}) copy-start(bf16[2,128,512]{2,1,0:T(8,128)(2,1)} %mine_ref.1) | copy-start | bytes 786436
  0.0 9.6 %collective-permute-start.9 = (bf16[2,128,512]{2,1,0:T(8,128)(2,1)}, bf16[2,128,512]{2,1,0:T(8,128)(2,1)S(1)}, u32[]{:S(2)}, u32[]{:S(2)}) collective-permute-start(bf16[2,128,512]{2,1,0:T(8,128)(2,1)} %mine_ref.1), channel_id=1, source_target_pairs={{0,16},{8,24},{16,0},{24,8},{1,17},{9,25},{17,1},{25,9},{2,18},{10... | collective-permute-start | bytes 786440 | tf_op jit(solution)/shard_map/ppermute | solution.py:335
  3.0 15.2 %collective-permute-start.8 = (bf16[2,128,512]{2,1,0:T(8,128)(2,1)}, bf16[2,128,512]{2,1,0:T(8,128)(2,1)S(1)}, u32[]{:S(2)}, u32[]{:S(2)}) collective-permute-start(bf16[2,128,512]{2,1,0:T(8,128)(2,1)} %mine_ref.1), channel_id=1, source_target_pairs={{0,8},{8,0},{16,24},{24,16},{1,9},{9,1},{17,25},{25,17},{2,10},{10... | collective-permute-start | bytes 786440 | tf_op jit(solution)/shard_map/ppermute | solution.py:338
  3.8 14.8 %copy-start.1 = (f32[512]{0:T(512)S(1)}, f32[512]{0:T(512)}, u32[]{:S(2)}) copy-start(f32[512]{0:T(512)} %param.8) | copy-start | bytes 6148
  3.9 14.8 %copy-start.2 = (s32[2,2]{1,0:T(2,128)S(1)}, s32[2,2]{1,0:T(2,128)}, u32[]{:S(2)}) copy-start(s32[2,2]{1,0:T(2,128)} %tracks_ref.1) | copy-start | bytes 52
  3.9 8.0 %collective-permute-start.11 = (bf16[64,768]{1,0:T(8,128)(2,1)S(1)}, bf16[64,768]{1,0:T(8,128)(2,1)S(1)}, u32[]{:S(2)}, u32[]{:S(2)}) collective-permute-start(bf16[64,768]{1,0:T(8,128)(2,1)S(1)} %slice.9), channel_id=1, source_target_pairs={{6,0},{7,1},{4,2},{5,3},{2,4},{3,5},{0,6},{1,7},{12,8},{13,9},{14,... | collective-permute-start | bytes 294920 | tf_op jit(solution)/shard_map/ppermute | solution.py:347
  9.6 9.1 %collective-permute-start.10 = (bf16[2,128,512]{2,1,0:T(8,128)(2,1)S(1)}, bf16[2,128,512]{2,1,0:T(8,128)(2,1)S(1)}, u32[]{:S(2)}, u32[]{:S(2)}) collective-permute-start(bf16[2,128,512]{2,1,0:T(8,128)(2,1)S(1)} %collective-permute-done.9.other_ref), channel_id=1, source_target_pairs={{0,8},{8,0},{16,24},{24,16},{1,9},{9,1},{17,25},{25,17},{2,10},{10... | collective-permute-start | bytes 786440 | tf_op jit(solution)/shard_map/ppermute | solution.py:338
  9.6 6.4 %collective-permute-start.2 = (bf16[64,1024]{1,0:T(8,128)(2,1)S(1)}, bf16[64,1024]{1,0:T(8,128)(2,1)S(1)}, u32[]{:S(2)}, u32[]{:S(2)}) collective-permute-start(bf16[64,1024]{1,0:T(8,128)(2,1)S(1)} %shard_map.73.refs_0_), channel_id=1, source_target_pairs={{1,0},{0,1},{3,2},{2,3},{5,4},{4,5},{7,6},{6,7},{11,8},{10,9},{9,1... | collective-permute-start | bytes 393224 | tf_op jit(solution)/shard_map/ppermute | solution.py:347
  11.2 4.7 %collective-permute-start.4 = (bf16[64,1024]{1,0:T(8,128)(2,1)S(1)}, bf16[64,1024]{1,0:T(8,128)(2,1)S(1)}, u32[]{:S(2)}, u32[]{:S(2)}) collective-permute-start(bf16[64,1024]{1,0:T(8,128)(2,1)S(1)} %shard_map.73.refs_0_), channel_id=1, source_target_pairs={{10,8},{11,9},{8,10},{9,11},{14,12},{15,13},{12,14},{13,15},{26,24... | collective-permute-start | bytes 393224 | tf_op jit(solution)/shard_map/ppermute | solution.py:347
  11.9 6.3 %collective-permute-start.13 = (bf16[64,768]{1,0:T(8,128)(2,1)S(1)}, bf16[64,768]{1,0:T(8,128)(2,1)S(1)}, u32[]{:S(2)}, u32[]{:S(2)}) collective-permute-start(bf16[64,768]{1,0:T(8,128)(2,1)S(1)} %collective-permute-done.11.refs_1_), channel_id=1, source_target_pairs={{1,0},{0,1},{3,2},{2,3},{5,4},{4,5},{7,6},{6,7},{9,8},{8,9},{11,10... | collective-permute-start | bytes 294920 | tf_op jit(solution)/shard_map/ppermute | solution.py:347
  16.0 3.5 %collective-permute-start.3 = (bf16[64,1024]{1,0:T(8,128)(2,1)S(1)}, bf16[64,1024]{1,0:T(8,128)(2,1)S(1)}, u32[]{:S(2)}, u32[]{:S(2)}) collective-permute-start(bf16[64,1024]{1,0:T(8,128)(2,1)S(1)} %collective-permute-done.2.refs_3_), channel_id=1, source_target_pairs={{0,8},{8,0},{16,24},{24,16},{1,9},{9,1},{17,25},{25,17},{2,10},{10... | collective-permute-start | bytes 393224 | tf_op jit(solution)/shard_map/ppermute | solution.py:338
  16.0 3.6 %collective-permute-start.5 = (bf16[64,1024]{1,0:T(8,128)(2,1)S(1)}, bf16[64,1024]{1,0:T(8,128)(2,1)S(1)}, u32[]{:S(2)}, u32[]{:S(2)}) collective-permute-start(bf16[64,1024]{1,0:T(8,128)(2,1)S(1)} %collective-permute-done.4.refs_5_), channel_id=1, source_target_pairs={{0,8},{8,0},{16,24},{24,16},{1,9},{9,1},{17,25},{25,17},{2,10},{10... | collective-permute-start | bytes 393224 | tf_op jit(solution)/shard_map/ppermute | solution.py:338
  18.2 1.3 %collective-permute-start.12 = (bf16[64,768]{1,0:T(8,128)(2,1)S(1)}, bf16[64,768]{1,0:T(8,128)(2,1)S(1)}, u32[]{:S(2)}, u32[]{:S(2)}) collective-permute-start(bf16[64,768]{1,0:T(8,128)(2,1)S(1)} %collective-permute-done.11.refs_1_), channel_id=1, source_target_pairs={{0,8},{8,0},{16,24},{24,16},{1,9},{9,1},{17,25},{25,17},{2,10},{10... | collective-permute-start | bytes 294920 | tf_op jit(solution)/shard_map/ppermute | solution.py:338
  18.2 1.5 %collective-permute-start.14 = (bf16[64,768]{1,0:T(8,128)(2,1)S(1)}, bf16[64,768]{1,0:T(8,128)(2,1)S(1)}, u32[]{:S(2)}, u32[]{:S(2)}) collective-permute-start(bf16[64,768]{1,0:T(8,128)(2,1)S(1)} %collective-permute-done.13.refs_7_), channel_id=1, source_target_pairs={{0,8},{8,0},{16,24},{24,16},{1,9},{9,1},{17,25},{25,17},{2,10},{10... | collective-permute-start | bytes 294920 | tf_op jit(solution)/shard_map/ppermute | solution.py:338
  20.6 14.1 %collective-permute-start.15 = (bf16[256,256]{1,0:T(8,128)(2,1)S(1)}, bf16[256,256]{1,0:T(8,128)(2,1)S(1)}, u32[]{:S(2)}, u32[]{:S(2)}) collective-permute-start(bf16[256,256]{1,0:T(8,128)(2,1)S(1)} %get-tuple-element.18.refs_9_), channel_id=1, source_target_pairs={{0,16},{8,24},{16,0},{24,8},{1,17},{9,25},{17,1},{25,9},{2,18},{10... | collective-permute-start | bytes 393224 | tf_op jit(solution)/shard_map/ppermute | solution.py:335
  23.3 12.2 %collective-permute-start.16 = (bf16[256,256]{1,0:T(8,128)(2,1)S(1)}, bf16[256,256]{1,0:T(8,128)(2,1)S(1)}, u32[]{:S(2)}, u32[]{:S(2)}) collective-permute-start(bf16[256,256]{1,0:T(8,128)(2,1)S(1)} %shard_map.77.mine_ref), channel_id=1, source_target_pairs={{0,16},{8,24},{16,0},{24,8},{1,17},{9,25},{17,1},{25,9},{2,18},{10... | collective-permute-start | bytes 393224 | tf_op jit(solution)/shard_map/ppermute | solution.py:335
  23.9 5.7 %collective-permute-start = (bf16[64,256]{1,0:T(8,128)(2,1)S(1)}, bf16[64,256]{1,0:T(8,128)(2,1)S(1)}, u32[]{:S(2)}, u32[]{:S(2)}) collective-permute-start(bf16[64,256]{1,0:T(8,128)(2,1)S(1)} %slice.8), channel_id=1, source_target_pairs={{6,0},{7,1},{4,2},{5,3},{2,4},{3,5},{0,6},{1,7},{12,8},{13,9},{14,... | collective-permute-start | bytes 98312 | tf_op jit(solution)/shard_map/ppermute | solution.py:347
  29.6 3.9 %collective-permute-start.6 = (bf16[64,256]{1,0:T(8,128)(2,1)S(1)}, bf16[64,256]{1,0:T(8,128)(2,1)S(1)}, u32[]{:S(2)}, u32[]{:S(2)}) collective-permute-start(bf16[64,256]{1,0:T(8,128)(2,1)S(1)} %collective-permute-done.refs_1_), channel_id=1, source_target_pairs={{1,0},{0,1},{3,2},{2,3},{5,4},{4,5},{7,6},{6,7},{9,8},{8,9},{11,10... | collective-permute-start | bytes 98312 | tf_op jit(solution)/shard_map/ppermute | solution.py:347
  31.1 2.4 %collective-permute-start.1 = (bf16[64,256]{1,0:T(8,128)(2,1)S(1)}, bf16[64,256]{1,0:T(8,128)(2,1)S(1)}, u32[]{:S(2)}, u32[]{:S(2)}) collective-permute-start(bf16[64,256]{1,0:T(8,128)(2,1)S(1)} %collective-permute-done.refs_1_), channel_id=1, source_target_pairs={{0,8},{8,0},{16,24},{24,16},{1,9},{9,1},{17,25},{25,17},{2,10},{10... | collective-permute-start | bytes 98312 | tf_op jit(solution)/shard_map/ppermute | solution.py:338
  33.5 1.2 %collective-permute-start.7 = (bf16[64,256]{1,0:T(8,128)(2,1)S(1)}, bf16[64,256]{1,0:T(8,128)(2,1)S(1)}, u32[]{:S(2)}, u32[]{:S(2)}) collective-permute-start(bf16[64,256]{1,0:T(8,128)(2,1)S(1)} %collective-permute-done.6.refs_7_), channel_id=1, source_target_pairs={{0,8},{8,0},{16,24},{24,16},{1,9},{9,1},{17,25},{25,17},{2,10},{10... | collective-permute-start | bytes 98312 | tf_op jit(solution)/shard_map/ppermute | solution.py:338
  35.3 1.3 %collective-permute-start.17 = (bf16[128,256]{1,0:T(8,128)(2,1)S(1)}, bf16[128,256]{1,0:T(8,128)(2,1)S(1)}, u32[]{:S(2)}, u32[]{:S(2)}) collective-permute-start(bf16[128,256]{1,0:T(8,128)(2,1)S(1)} %get-tuple-element.25), channel_id=1, source_target_pairs={{0,8},{8,0},{16,24},{24,16},{1,9},{9,1},{17,25},{25,17},{2,10},{10... | collective-permute-start | bytes 196616 | tf_op jit(solution)/shard_map/ppermute | solution.py:338
  35.7 1.8 %collective-permute-start.18 = (bf16[128,256]{1,0:T(8,128)(2,1)S(1)}, bf16[128,256]{1,0:T(8,128)(2,1)S(1)}, u32[]{:S(2)}, u32[]{:S(2)}) collective-permute-start(bf16[128,256]{1,0:T(8,128)(2,1)S(1)} %shard_map.80), channel_id=1, source_target_pairs={{0,8},{8,0},{16,24},{24,16},{1,9},{9,1},{17,25},{25,17},{2,10},{10... | collective-permute-start | bytes 196616 | tf_op jit(solution)/shard_map/ppermute | solution.py:338

commit v9 on v8

--- a/solution.py
+++ b/solution.py
@@ -263,19 +263,18 @@
 
 def channel_terms(weights, ref, chip, core):
     span = ref.shape[0]
-    half = weights.shape[1] // 2
-    rows = pl.ds(pl.multiple_of(chip * span, span), span)
-    lanes = pl.ds(pl.multiple_of(core * half, half), half)
-    return lax.dot_general(
-        weights[rows, lanes], ref[...], (((0,), (0,)), ((), ())), preferred_element_type=jnp.float32
-    )
+    half = weights.shape[0] // 2
+    rows = pl.ds(pl.multiple_of(core * half, half), half)
+    lanes = pl.ds(pl.multiple_of(chip * span, span), span)
+    return jnp.dot(weights[rows, lanes], ref[...], preferred_element_type=jnp.float32)
 
 
 def low_output_kernel(sources, *refs):
     shards, refs = refs[: 1 + 2 * len(sources)], refs[1 + 2 * len(sources) :]
-    mine_ref, other_ref, kept_ref, given_ref, weights = refs
+    mine_ref, other_ref, kept_ref, given_ref, weights, placed = refs
     core, y = lax.axis_index("tm") % 2, lax.axis_index("tm") // 2
-    place(sources, shards, weights, 3 * weights.shape[1])
+    place(sources, shards, placed, 3 * placed.shape[1])
+    weights[...] = placed[...].astype(jnp.float32).T.astype(weights.dtype)
     for n, ref in enumerate((kept_ref, given_ref)):
         total = channel_terms(weights, mine_ref, y, core ^ n)
         total = total + channel_terms(weights, other_ref, y ^ 1, core ^ n)
@@ -422,8 +421,9 @@
     out_shards = [packed] + [v for pair in zip(out_shards, swapped_out) for v in pair]
     low_kept, low_given, out_weights = kernel(
         functools.partial(low_output_kernel, sources),
-        [((span // 2, low), half)] * 2 + [((width, span), half)],
+        [((span // 2, low), half)] * 2 + [((span, width), half)],
         (*out_shards, low_attended, low_other),
+        scratch=[((width, span), half)],
         flops=4 * low * span * span,
     )
     low_received = swap(low_given)

time: 38.3 us -> 38.3 us (level)
  transfers between devices with their start and end apart: 19 -> 19, of which waited for: 7 -> 7; matrix products, arithmetic and copies ran while one was open for 0% -> 0% of each run, Pallas kernels for 12% -> 11%
where the time goes in v9:
time: 38.3 us; the launch traced here: 38.1 us
  starting transfers between devices  20.1 us (52%)
  waiting for transfers between devices  11.9 us (31%)
  Pallas kernels  5.21 us (14%)
  local copies, waits for them, and re-layouts  0.67 us (2%)
    ppermute x6, starting transfers between devices, fetch(): return lax.ppermute(value, ('tm', 'agent'), pairs)  11.6 us
    ppermute x6, waiting for transfers between devices, fetch(): return lax.ppermute(value, ('tm', 'agent'), pairs)  8.04 us
    pallas_call x8, Pallas kernels, kernel(): pl.pallas_call(body, out_shape=[jax.ShapeDtypeStruct(shape, dtype) for sh...  5.21 us
    ppermute x3, starting transfers between devices, across(): return lax.ppermute(value, 'tm', [(i, i ^ 2) for i in range(n_tm)])  5.15 us
    ppermute x10, starting transfers between devices, swap(): return lax.ppermute(value, 'tm', [(i, i ^ 1) for i in range(n_tm)])  3.37 us
    ppermute x3, waiting for transfers between devices, across(): return lax.ppermute(value, 'tm', [(i, i ^ 2) for i in range(n_tm)])  2.03 us
    ppermute x10, waiting for transfers between devices, swap(): return lax.ppermute(value, 'tm', [(i, i ^ 1) for i in range(n_tm)])  1.84 us
  transfers between devices with their start and end apart: 19, of which 7 were waited for; matrix products, arithmetic and copies ran while one was open for 0% of the time, Pallas kernels for 11%

profile of v9, /device:TPU:0, one launch (start us, length us, event | category | flops | bytes accessed | tf_op | source)
XLA Modules:
  0.0 38.1 jit_solution(9846088059681850991)
XLA Ops:
  0.0 3.0 %collective-permute-start.9 = (bf16[2,128,512]{2,1,0:T(8,128)(2,1)}, bf16[2,128,512]{2,1,0:T(8,128)(2,1)S(1)}, u32[]{:S(2)}, u32[]{:S(2)}) collective-permute-start(bf16[2,128,512]{2,1,0:T(8,128)(2,1)} %mine_ref.1), channel_id=1, source_target_pairs={{0,16},{8,24},{16,0},{24,8},{1,17},{9,25},{17,1},{25,9},{2,18},{10... | collective-permute-start | bytes 786440 | tf_op jit(solution)/shard_map/ppermute | solution.py:334
  3.0 0.8 %shard_map.73.refs_0_ = bf16[64,1024]{1,0:T(8,128)(2,1)S(1)} custom-call(bf16[64,512]{1,0:T(8,128)(2,1)} %refs_0_.1, bf16[64,512]{1,0:T(8,128)(2,1)} %refs_1_.1, bf16[64,512]{1,0:T(8,128)(2,1)} %refs_2_.1, bf16[64,512]{1,0:T(8,128)(2,1)} %refs_3_.1), custom_call_target="tpu_custom_call" | custom-call | bytes 1048576 | tf_op jit(solution)/shard_map/pallas_call | solution.py:353
  3.9 3.7 %collective-permute-start.11 = (bf16[64,768]{1,0:T(8,128)(2,1)S(1)}, bf16[64,768]{1,0:T(8,128)(2,1)S(1)}, u32[]{:S(2)}, u32[]{:S(2)}) collective-permute-start(bf16[64,768]{1,0:T(8,128)(2,1)S(1)} %slice.9), channel_id=1, source_target_pairs={{6,0},{7,1},{4,2},{5,3},{2,4},{3,5},{0,6},{1,7},{12,8},{13,9},{14,... | collective-permute-start | bytes 294920 | tf_op jit(solution)/shard_map/ppermute | solution.py:346
  7.6 2.0 %collective-permute-done.9.other_ref = bf16[2,128,512]{2,1,0:T(8,128)(2,1)S(1)} collective-permute-done((bf16[2,128,512]{2,1,0:T(8,128)(2,1)}, bf16[2,128,512]{2,1,0:T(8,128)(2,1)S(1)}, u32[]{:S(2)}, u32[]{:S(2)}) %collective-permute-start.9) | collective-permute-done | bytes 262176 | tf_op jit(solution)/shard_map/ppermute | solution.py:334
  9.6 1.6 %collective-permute-start.2 = (bf16[64,1024]{1,0:T(8,128)(2,1)S(1)}, bf16[64,1024]{1,0:T(8,128)(2,1)S(1)}, u32[]{:S(2)}, u32[]{:S(2)}) collective-permute-start(bf16[64,1024]{1,0:T(8,128)(2,1)S(1)} %shard_map.73.refs_0_), channel_id=1, source_target_pairs={{1,0},{0,1},{3,2},{2,3},{5,4},{4,5},{7,6},{6,7},{11,8},{10,9},{9,1... | collective-permute-start | bytes 393224 | tf_op jit(solution)/shard_map/ppermute | solution.py:346
  11.2 0.7 %collective-permute-start.4 = (bf16[64,1024]{1,0:T(8,128)(2,1)S(1)}, bf16[64,1024]{1,0:T(8,128)(2,1)S(1)}, u32[]{:S(2)}, u32[]{:S(2)}) collective-permute-start(bf16[64,1024]{1,0:T(8,128)(2,1)S(1)} %shard_map.73.refs_0_), channel_id=1, source_target_pairs={{10,8},{11,9},{8,10},{9,11},{14,12},{15,13},{12,14},{13,15},{26,24... | collective-permute-start | bytes 393224 | tf_op jit(solution)/shard_map/ppermute | solution.py:346
  11.9 0.8 %collective-permute-start.13 = (bf16[64,768]{1,0:T(8,128)(2,1)S(1)}, bf16[64,768]{1,0:T(8,128)(2,1)S(1)}, u32[]{:S(2)}, u32[]{:S(2)}) collective-permute-start(bf16[64,768]{1,0:T(8,128)(2,1)S(1)} %collective-permute-done.11.refs_1_), channel_id=1, source_target_pairs={{1,0},{0,1},{3,2},{2,3},{5,4},{4,5},{7,6},{6,7},{9,8},{8,9},{11,10... | collective-permute-start | bytes 294920 | tf_op jit(solution)/shard_map/ppermute | solution.py:346
  12.7 3.3 %collective-permute-done.2.refs_3_ = bf16[64,1024]{1,0:T(8,128)(2,1)S(1)} collective-permute-done((bf16[64,1024]{1,0:T(8,128)(2,1)S(1)}, bf16[64,1024]{1,0:T(8,128)(2,1)S(1)}, u32[]{:S(2)}, u32[]{:S(2)}) %collective-permute-start.2) | collective-permute-done | bytes 131104 | tf_op jit(solution)/shard_map/ppermute | solution.py:346
  16.0 2.2 %collective-permute-start.5 = (bf16[64,1024]{1,0:T(8,128)(2,1)S(1)}, bf16[64,1024]{1,0:T(8,128)(2,1)S(1)}, u32[]{:S(2)}, u32[]{:S(2)}) collective-permute-start(bf16[64,1024]{1,0:T(8,128)(2,1)S(1)} %collective-permute-done.4.refs_5_), channel_id=1, source_target_pairs={{0,8},{8,0},{16,24},{24,16},{1,9},{9,1},{17,25},{25,17},{2,10},{10... | collective-permute-start | bytes 393224 | tf_op jit(solution)/shard_map/ppermute | solution.py:337
  18.2 0.5 %collective-permute-start.14 = (bf16[64,768]{1,0:T(8,128)(2,1)S(1)}, bf16[64,768]{1,0:T(8,128)(2,1)S(1)}, u32[]{:S(2)}, u32[]{:S(2)}) collective-permute-start(bf16[64,768]{1,0:T(8,128)(2,1)S(1)} %collective-permute-done.13.refs_7_), channel_id=1, source_target_pairs={{0,8},{8,0},{16,24},{24,16},{1,9},{9,1},{17,25},{25,17},{2,10},{10... | collective-permute-start | bytes 294920 | tf_op jit(solution)/shard_map/ppermute | solution.py:337
  18.7 0.8 %shard_map.74 = (bf16[512,512]{1,0:T(8,128)(2,1)S(1)}, s32[2,8,128]{2,1,0:T(8,128)S(1)}) custom-call(s32[2,2]{1,0:T(2,128)S(1)} %copy-done.2, f32[1,512]{1,0:T(1,128)S(1)} %bitcast.3, bf16[2,128,512]{2,1,0:T(8,128)(2,1)S(1)} %copy-done, bf16[2,128,512]{2,1,0:T(8,128)(2,1)S(1)} %collective-permute-done.8.beside_ref, ...), custom_call_target="tpu_custom_call" | custom-call | flops 2097152 | bytes 1048576 | tf_op jit(solution)/shard_map/pallas_call | solution.py:353
  19.6 0.9 %shard_map.75 = (bf16[256,256]{1,0:T(8,128)(2,1)S(1)}, bf16[512,768]{1,0:T(8,128)(2,1)S(1)}, bf16[256,256]{1,0:T(8,128)(2,1)S(1)}, bf16[256,256]{1,0:T(8,128)(2,1)S(1)}) custom-call(s32[2,8,128]{2,1,0:T(8,128)S(1)} %get-tuple-element.16.bounds_ref, bf16[512,512]{1,0:T(8,128)(2,1)S(1)} %get-tuple-element.17.normed_ref, ...), custom_call_target="tpu_custom_call" | custom-call | flops 268435456 | bytes 1048576 | tf_op jit(solution)/shard_map/pallas_call | solution.py:353
  20.6 1.6 %collective-permute-start.15 = (bf16[256,256]{1,0:T(8,128)(2,1)S(1)}, bf16[256,256]{1,0:T(8,128)(2,1)S(1)}, u32[]{:S(2)}, u32[]{:S(2)}) collective-permute-start(bf16[256,256]{1,0:T(8,128)(2,1)S(1)} %get-tuple-element.18.refs_9_), channel_id=1, source_target_pairs={{0,16},{8,24},{16,0},{24,8},{1,17},{9,25},{17,1},{25,9},{2,18},{10... | collective-permute-start | bytes 393224 | tf_op jit(solution)/shard_map/ppermute | solution.py:334
  22.2 1.1 %shard_map.77.mine_ref = bf16[256,256]{1,0:T(8,128)(2,1)S(1)} custom-call(s32[2,8,128]{2,1,0:T(8,128)S(1)} %get-tuple-element.16.bounds_ref, bf16[512,512]{1,0:T(8,128)(2,1)S(1)} %get-tuple-element.17.normed_ref, bf16[512,768]{1,0:T(8,128)(2,1)S(1)} %get-tuple-element.20.weights, bf16[256,256]{1,0:T(8,128)(2,1)S(1)} %get-tuple-element.21.low_keys, ...), custom_call_target="tpu_custom_call" | custom-call | flops 335544320 | bytes 1048576 | tf_op jit(solution)/shard_map/pallas_call | solution.py:353
  23.3 0.6 %collective-permute-start.16 = (bf16[256,256]{1,0:T(8,128)(2,1)S(1)}, bf16[256,256]{1,0:T(8,128)(2,1)S(1)}, u32[]{:S(2)}, u32[]{:S(2)}) collective-permute-start(bf16[256,256]{1,0:T(8,128)(2,1)S(1)} %shard_map.77.mine_ref), channel_id=1, source_target_pairs={{0,16},{8,24},{16,0},{24,8},{1,17},{9,25},{17,1},{25,9},{2,18},{10... | collective-permute-start | bytes 393224 | tf_op jit(solution)/shard_map/ppermute | solution.py:334
  23.9 3.4 %collective-permute-start = (bf16[64,256]{1,0:T(8,128)(2,1)S(1)}, bf16[64,256]{1,0:T(8,128)(2,1)S(1)}, u32[]{:S(2)}, u32[]{:S(2)}) collective-permute-start(bf16[64,256]{1,0:T(8,128)(2,1)S(1)} %slice.8), channel_id=1, source_target_pairs={{6,0},{7,1},{4,2},{5,3},{2,4},{3,5},{0,6},{1,7},{12,8},{13,9},{14,... | collective-permute-start | bytes 98312 | tf_op jit(solution)/shard_map/ppermute | solution.py:346
  27.2 2.4 %collective-permute-done.refs_1_ = bf16[64,256]{1,0:T(8,128)(2,1)S(1)} collective-permute-done((bf16[64,256]{1,0:T(8,128)(2,1)S(1)}, bf16[64,256]{1,0:T(8,128)(2,1)S(1)}, u32[]{:S(2)}, u32[]{:S(2)}) %collective-permute-start) | collective-permute-done | bytes 32800 | tf_op jit(solution)/shard_map/ppermute | solution.py:346
  29.6 1.5 %collective-permute-start.6 = (bf16[64,256]{1,0:T(8,128)(2,1)S(1)}, bf16[64,256]{1,0:T(8,128)(2,1)S(1)}, u32[]{:S(2)}, u32[]{:S(2)}) collective-permute-start(bf16[64,256]{1,0:T(8,128)(2,1)S(1)} %collective-permute-done.refs_1_), channel_id=1, source_target_pairs={{1,0},{0,1},{3,2},{2,3},{5,4},{4,5},{7,6},{6,7},{9,8},{8,9},{11,10... | collective-permute-start | bytes 98312 | tf_op jit(solution)/shard_map/ppermute | solution.py:346
  31.1 2.4 %collective-permute-done.6.refs_7_ = bf16[64,256]{1,0:T(8,128)(2,1)S(1)} collective-permute-done((bf16[64,256]{1,0:T(8,128)(2,1)S(1)}, bf16[64,256]{1,0:T(8,128)(2,1)S(1)}, u32[]{:S(2)}, u32[]{:S(2)}) %collective-permute-start.6) | collective-permute-done | bytes 32800 | tf_op jit(solution)/shard_map/ppermute | solution.py:346
  33.5 1.2 %collective-permute-done.7.refs_8_ = bf16[64,256]{1,0:T(8,128)(2,1)S(1)} collective-permute-done((bf16[64,256]{1,0:T(8,128)(2,1)S(1)}, bf16[64,256]{1,0:T(8,128)(2,1)S(1)}, u32[]{:S(2)}, u32[]{:S(2)}) %collective-permute-start.7) | collective-permute-done | bytes 32800 | tf_op jit(solution)/shard_map/ppermute | solution.py:337
  35.7 0.4 %collective-permute-start.18 = (bf16[128,256]{1,0:T(8,128)(2,1)S(1)}, bf16[128,256]{1,0:T(8,128)(2,1)S(1)}, u32[]{:S(2)}, u32[]{:S(2)}) collective-permute-start(bf16[128,256]{1,0:T(8,128)(2,1)S(1)} %shard_map.80), channel_id=1, source_target_pairs={{0,8},{8,0},{16,24},{24,16},{1,9},{9,1},{17,25},{25,17},{2,10},{10... | collective-permute-start | bytes 196616 | tf_op jit(solution)/shard_map/ppermute | solution.py:337
  36.1 0.5 %collective-permute-done.17.received_ref = bf16[128,256]{1,0:T(8,128)(2,1)S(1)} collective-permute-done((bf16[128,256]{1,0:T(8,128)(2,1)S(1)}, bf16[128,256]{1,0:T(8,128)(2,1)S(1)}, u32[]{:S(2)}, u32[]{:S(2)}) %collective-permute-start.17) | collective-permute-done | bytes 65568 | tf_op jit(solution)/shard_map/ppermute | solution.py:337
  36.6 0.8 %shard_map.79 = bf16[2,128,512]{2,1,0:T(8,128)(2,1)} custom-call(bf16[256,512]{1,0:T(8,128)(2,1)S(1)} %get-tuple-element.19.weights, f32[128,256]{1,0:T(8,128)S(1)} %get-tuple-element.23.partial_ref, bf16[256,256]{1,0:T(8,128)(2,1)S(1)} %collective-permute-done.16.other_ref, bf16[128,256]{1,0:T(8,128)(2,1)S(1)} %get-tuple-element.24.low_ref, ...), custom_call_target="tpu_custom_call" | custom-call | flops 16777216 | bytes 1048576 | tf_op jit(solution)/shard_map/pallas_call | solution.py:353
  37.4 0.6 %bitcast_dynamic-update-slice_fusion = bf16[2,128,512]{2,1,0:T(8,128)(2,1)} fusion(bf16[2,128,512]{2,1,0:T(8,128)(2,1)} %shard_map.79, s32[]{:T(128)S(6)} %select_n.11, bf16[128,256]{1,0:T(8,128)(2,1)S(1)} %collective-permute-done.18), kind=kLoop, calls=%fused_computation | loop fusion | bytes 131076 | tf_op jit(solution)/shard_map/dynamic_update_slice | solution.py:451
  (31 shorter events, 1.1 us)
Async XLA Ops:
  0.0 18.7 %copy-start = (bf16[2,128,512]{2,1,0:T(8,128)(2,1)S(1)}, bf16[2,128,512]{2,1,0:T(8,128)(2,1)}, u32[]{:S(2)}) copy-start(bf16[2,128,512]{2,1,0:T(8,128)(2,1)} %mine_ref.1) | copy-start | bytes 786436
  0.0 9.6 %collective-permute-start.9 = (bf16[2,128,512]{2,1,0:T(8,128)(2,1)}, bf16[2,128,512]{2,1,0:T(8,128)(2,1)S(1)}, u32[]{:S(2)}, u32[]{:S(2)}) collective-permute-start(bf16[2,128,512]{2,1,0:T(8,128)(2,1)} %mine_ref.1), channel_id=1, source_target_pairs={{0,16},{8,24},{16,0},{24,8},{1,17},{9,25},{17,1},{25,9},{2,18},{10... | collective-permute-start | bytes 786440 | tf_op jit(solution)/shard_map/ppermute | solution.py:334
  3.0 15.2 %collective-permute-start.8 = (bf16[2,128,512]{2,1,0:T(8,128)(2,1)}, bf16[2,128,512]{2,1,0:T(8,128)(2,1)S(1)}, u32[]{:S(2)}, u32[]{:S(2)}) collective-permute-start(bf16[2,128,512]{2,1,0:T(8,128)(2,1)} %mine_ref.1), channel_id=1, source_target_pairs={{0,8},{8,0},{16,24},{24,16},{1,9},{9,1},{17,25},{25,17},{2,10},{10... | collective-permute-start | bytes 786440 | tf_op jit(solution)/shard_map/ppermute | solution.py:337
  3.8 14.8 %copy-start.1 = (f32[512]{0:T(512)S(1)}, f32[512]{0:T(512)}, u32[]{:S(2)}) copy-start(f32[512]{0:T(512)} %param.8) | copy-start | bytes 6148
  3.9 14.8 %copy-start.2 = (s32[2,2]{1,0:T(2,128)S(1)}, s32[2,2]{1,0:T(2,128)}, u32[]{:S(2)}) copy-start(s32[2,2]{1,0:T(2,128)} %tracks_ref.1) | copy-start | bytes 52
  3.9 8.0 %collective-permute-start.11 = (bf16[64,768]{1,0:T(8,128)(2,1)S(1)}, bf16[64,768]{1,0:T(8,128)(2,1)S(1)}, u32[]{:S(2)}, u32[]{:S(2)}) collective-permute-start(bf16[64,768]{1,0:T(8,128)(2,1)S(1)} %slice.9), channel_id=1, source_target_pairs={{6,0},{7,1},{4,2},{5,3},{2,4},{3,5},{0,6},{1,7},{12,8},{13,9},{14,... | collective-permute-start | bytes 294920 | tf_op jit(solution)/shard_map/ppermute | solution.py:346
  9.6 9.1 %collective-permute-start.10 = (bf16[2,128,512]{2,1,0:T(8,128)(2,1)S(1)}, bf16[2,128,512]{2,1,0:T(8,128)(2,1)S(1)}, u32[]{:S(2)}, u32[]{:S(2)}) collective-permute-start(bf16[2,128,512]{2,1,0:T(8,128)(2,1)S(1)} %collective-permute-done.9.other_ref), channel_id=1, source_target_pairs={{0,8},{8,0},{16,24},{24,16},{1,9},{9,1},{17,25},{25,17},{2,10},{10... | collective-permute-start | bytes 786440 | tf_op jit(solution)/shard_map/ppermute | solution.py:337
  9.6 6.4 %collective-permute-start.2 = (bf16[64,1024]{1,0:T(8,128)(2,1)S(1)}, bf16[64,1024]{1,0:T(8,128)(2,1)S(1)}, u32[]{:S(2)}, u32[]{:S(2)}) collective-permute-start(bf16[64,1024]{1,0:T(8,128)(2,1)S(1)} %shard_map.73.refs_0_), channel_id=1, source_target_pairs={{1,0},{0,1},{3,2},{2,3},{5,4},{4,5},{7,6},{6,7},{11,8},{10,9},{9,1... | collective-permute-start | bytes 393224 | tf_op jit(solution)/shard_map/ppermute | solution.py:346
  11.2 4.7 %collective-permute-start.4 = (bf16[64,1024]{1,0:T(8,128)(2,1)S(1)}, bf16[64,1024]{1,0:T(8,128)(2,1)S(1)}, u32[]{:S(2)}, u32[]{:S(2)}) collective-permute-start(bf16[64,1024]{1,0:T(8,128)(2,1)S(1)} %shard_map.73.refs_0_), channel_id=1, source_target_pairs={{10,8},{11,9},{8,10},{9,11},{14,12},{15,13},{12,14},{13,15},{26,24... | collective-permute-start | bytes 393224 | tf_op jit(solution)/shard_map/ppermute | solution.py:346
  11.9 6.3 %collective-permute-start.13 = (bf16[64,768]{1,0:T(8,128)(2,1)S(1)}, bf16[64,768]{1,0:T(8,128)(2,1)S(1)}, u32[]{:S(2)}, u32[]{:S(2)}) collective-permute-start(bf16[64,768]{1,0:T(8,128)(2,1)S(1)} %collective-permute-done.11.refs_1_), channel_id=1, source_target_pairs={{1,0},{0,1},{3,2},{2,3},{5,4},{4,5},{7,6},{6,7},{9,8},{8,9},{11,10... | collective-permute-start | bytes 294920 | tf_op jit(solution)/shard_map/ppermute | solution.py:346
  16.0 3.5 %collective-permute-start.3 = (bf16[64,1024]{1,0:T(8,128)(2,1)S(1)}, bf16[64,1024]{1,0:T(8,128)(2,1)S(1)}, u32[]{:S(2)}, u32[]{:S(2)}) collective-permute-start(bf16[64,1024]{1,0:T(8,128)(2,1)S(1)} %collective-permute-done.2.refs_3_), channel_id=1, source_target_pairs={{0,8},{8,0},{16,24},{24,16},{1,9},{9,1},{17,25},{25,17},{2,10},{10... | collective-permute-start | bytes 393224 | tf_op jit(solution)/shard_map/ppermute | solution.py:337
  16.0 3.6 %collective-permute-start.5 = (bf16[64,1024]{1,0:T(8,128)(2,1)S(1)}, bf16[64,1024]{1,0:T(8,128)(2,1)S(1)}, u32[]{:S(2)}, u32[]{:S(2)}) collective-permute-start(bf16[64,1024]{1,0:T(8,128)(2,1)S(1)} %collective-permute-done.4.refs_5_), channel_id=1, source_target_pairs={{0,8},{8,0},{16,24},{24,16},{1,9},{9,1},{17,25},{25,17},{2,10},{10... | collective-permute-start | bytes 393224 | tf_op jit(solution)/shard_map/ppermute | solution.py:337
  18.2 1.3 %collective-permute-start.12 = (bf16[64,768]{1,0:T(8,128)(2,1)S(1)}, bf16[64,768]{1,0:T(8,128)(2,1)S(1)}, u32[]{:S(2)}, u32[]{:S(2)}) collective-permute-start(bf16[64,768]{1,0:T(8,128)(2,1)S(1)} %collective-permute-done.11.refs_1_), channel_id=1, source_target_pairs={{0,8},{8,0},{16,24},{24,16},{1,9},{9,1},{17,25},{25,17},{2,10},{10... | collective-permute-start | bytes 294920 | tf_op jit(solution)/shard_map/ppermute | solution.py:337
  18.2 1.5 %collective-permute-start.14 = (bf16[64,768]{1,0:T(8,128)(2,1)S(1)}, bf16[64,768]{1,0:T(8,128)(2,1)S(1)}, u32[]{:S(2)}, u32[]{:S(2)}) collective-permute-start(bf16[64,768]{1,0:T(8,128)(2,1)S(1)} %collective-permute-done.13.refs_7_), channel_id=1, source_target_pairs={{0,8},{8,0},{16,24},{24,16},{1,9},{9,1},{17,25},{25,17},{2,10},{10... | collective-permute-start | bytes 294920 | tf_op jit(solution)/shard_map/ppermute | solution.py:337
  20.6 14.1 %collective-permute-start.15 = (bf16[256,256]{1,0:T(8,128)(2,1)S(1)}, bf16[256,256]{1,0:T(8,128)(2,1)S(1)}, u32[]{:S(2)}, u32[]{:S(2)}) collective-permute-start(bf16[256,256]{1,0:T(8,128)(2,1)S(1)} %get-tuple-element.18.refs_9_), channel_id=1, source_target_pairs={{0,16},{8,24},{16,0},{24,8},{1,17},{9,25},{17,1},{25,9},{2,18},{10... | collective-permute-start | bytes 393224 | tf_op jit(solution)/shard_map/ppermute | solution.py:334
  23.3 12.2 %collective-permute-start.16 = (bf16[256,256]{1,0:T(8,128)(2,1)S(1)}, bf16[256,256]{1,0:T(8,128)(2,1)S(1)}, u32[]{:S(2)}, u32[]{:S(2)}) collective-permute-start(bf16[256,256]{1,0:T(8,128)(2,1)S(1)} %shard_map.77.mine_ref), channel_id=1, source_target_pairs={{0,16},{8,24},{16,0},{24,8},{1,17},{9,25},{17,1},{25,9},{2,18},{10... | collective-permute-start | bytes 393224 | tf_op jit(solution)/shard_map/ppermute | solution.py:334
  23.9 5.7 %collective-permute-start = (bf16[64,256]{1,0:T(8,128)(2,1)S(1)}, bf16[64,256]{1,0:T(8,128)(2,1)S(1)}, u32[]{:S(2)}, u32[]{:S(2)}) collective-permute-start(bf16[64,256]{1,0:T(8,128)(2,1)S(1)} %slice.8), channel_id=1, source_target_pairs={{6,0},{7,1},{4,2},{5,3},{2,4},{3,5},{0,6},{1,7},{12,8},{13,9},{14,... | collective-permute-start | bytes 98312 | tf_op jit(solution)/shard_map/ppermute | solution.py:346
  29.6 3.9 %collective-permute-start.6 = (bf16[64,256]{1,0:T(8,128)(2,1)S(1)}, bf16[64,256]{1,0:T(8,128)(2,1)S(1)}, u32[]{:S(2)}, u32[]{:S(2)}) collective-permute-start(bf16[64,256]{1,0:T(8,128)(2,1)S(1)} %collective-permute-done.refs_1_), channel_id=1, source_target_pairs={{1,0},{0,1},{3,2},{2,3},{5,4},{4,5},{7,6},{6,7},{9,8},{8,9},{11,10... | collective-permute-start | bytes 98312 | tf_op jit(solution)/shard_map/ppermute | solution.py:346
  31.1 2.4 %collective-permute-start.1 = (bf16[64,256]{1,0:T(8,128)(2,1)S(1)}, bf16[64,256]{1,0:T(8,128)(2,1)S(1)}, u32[]{:S(2)}, u32[]{:S(2)}) collective-permute-start(bf16[64,256]{1,0:T(8,128)(2,1)S(1)} %collective-permute-done.refs_1_), channel_id=1, source_target_pairs={{0,8},{8,0},{16,24},{24,16},{1,9},{9,1},{17,25},{25,17},{2,10},{10... | collective-permute-start | bytes 98312 | tf_op jit(solution)/shard_map/ppermute | solution.py:337
  33.5 1.2 %collective-permute-start.7 = (bf16[64,256]{1,0:T(8,128)(2,1)S(1)}, bf16[64,256]{1,0:T(8,128)(2,1)S(1)}, u32[]{:S(2)}, u32[]{:S(2)}) collective-permute-start(bf16[64,256]{1,0:T(8,128)(2,1)S(1)} %collective-permute-done.6.refs_7_), channel_id=1, source_target_pairs={{0,8},{8,0},{16,24},{24,16},{1,9},{9,1},{17,25},{25,17},{2,10},{10... | collective-permute-start | bytes 98312 | tf_op jit(solution)/shard_map/ppermute | solution.py:337
  35.3 1.3 %collective-permute-start.17 = (bf16[128,256]{1,0:T(8,128)(2,1)S(1)}, bf16[128,256]{1,0:T(8,128)(2,1)S(1)}, u32[]{:S(2)}, u32[]{:S(2)}) collective-permute-start(bf16[128,256]{1,0:T(8,128)(2,1)S(1)} %get-tuple-element.25), channel_id=1, source_target_pairs={{0,8},{8,0},{16,24},{24,16},{1,9},{9,1},{17,25},{25,17},{2,10},{10... | collective-permute-start | bytes 196616 | tf_op jit(solution)/shard_map/ppermute | solution.py:337
  35.7 1.8 %collective-permute-start.18 = (bf16[128,256]{1,0:T(8,128)(2,1)S(1)}, bf16[128,256]{1,0:T(8,128)(2,1)S(1)}, u32[]{:S(2)}, u32[]{:S(2)}) collective-permute-start(bf16[128,256]{1,0:T(8,128)(2,1)S(1)} %shard_map.80), channel_id=1, source_target_pairs={{0,8},{8,0},{16,24},{24,16},{1,9},{9,1},{17,25},{25,17},{2,10},{10... | collective-permute-start | bytes 196616 | tf_op jit(solution)/shard_map/ppermute | solution.py:337

commit v10 on v9

--- a/solution.py
+++ b/solution.py
@@ -237,7 +237,8 @@
         full = jnp.dot(
             normed, weights[:, n * span : (n + 1) * span], preferred_element_type=jnp.float32
         )
-        target[...] = (full.T if n == 2 else full).astype(jnp.bfloat16)
+        rounded = full.astype(jnp.bfloat16)
+        target[...] = rounded.T if n == 2 else rounded
 
 
 def low_kernel(sources, head_dim, bounds_ref, normed_ref, *refs):
@@ -274,7 +275,7 @@
     mine_ref, other_ref, kept_ref, given_ref, weights, placed = refs
     core, y = lax.axis_index("tm") % 2, lax.axis_index("tm") // 2
     place(sources, shards, placed, 3 * placed.shape[1])
-    weights[...] = placed[...].astype(jnp.float32).T.astype(weights.dtype)
+    weights[...] = placed[...].T
     for n, ref in enumerate((kept_ref, given_ref)):
         total = channel_terms(weights, mine_ref, y, core ^ n)
         total = total + channel_terms(weights, other_ref, y ^ 1, core ^ n)

time: 38.3 us -> 38.2 us (level)
  no operation moved by 1% of the time
where the time goes in v10:
time: 38.2 us; the launch traced here: 38 us
  starting transfers between devices  20.1 us (53%)
  waiting for transfers between devices  11.9 us (31%)
  Pallas kernels  5.18 us (14%)
  local copies, waits for them, and re-layouts  0.67 us (2%)
    ppermute x6, starting transfers between devices, fetch(): return lax.ppermute(value, ('tm', 'agent'), pairs)  11.6 us
    ppermute x6, waiting for transfers between devices, fetch(): return lax.ppermute(value, ('tm', 'agent'), pairs)  8.04 us
    pallas_call x8, Pallas kernels, kernel(): pl.pallas_call(body, out_shape=[jax.ShapeDtypeStruct(shape, dtype) for sh...  5.18 us
    ppermute x3, starting transfers between devices, across(): return lax.ppermute(value, 'tm', [(i, i ^ 2) for i in range(n_tm)])  5.15 us
    ppermute x10, starting transfers between devices, swap(): return lax.ppermute(value, 'tm', [(i, i ^ 1) for i in range(n_tm)])  3.37 us
    ppermute x3, waiting for transfers between devices, across(): return lax.ppermute(value, 'tm', [(i, i ^ 2) for i in range(n_tm)])  2.03 us
    ppermute x10, waiting for transfers between devices, swap(): return lax.ppermute(value, 'tm', [(i, i ^ 1) for i in range(n_tm)])  1.84 us
  transfers between devices with their start and end apart: 19, of which 7 were waited for; matrix products, arithmetic and copies ran while one was open for 0% of the time, Pallas kernels for 11%

profile of v10, /device:TPU:0, one launch (start us, length us, event | category | flops | bytes accessed | tf_op | source)
XLA Modules:
  0.0 38.0 jit_solution(8339867205087154729)
XLA Ops:
  0.0 3.0 %collective-permute-start.9 = (bf16[2,128,512]{2,1,0:T(8,128)(2,1)}, bf16[2,128,512]{2,1,0:T(8,128)(2,1)S(1)}, u32[]{:S(2)}, u32[]{:S(2)}) collective-permute-start(bf16[2,128,512]{2,1,0:T(8,128)(2,1)} %mine_ref.1), channel_id=1, source_target_pairs={{0,16},{8,24},{16,0},{24,8},{1,17},{9,25},{17,1},{25,9},{2,18},{10... | collective-permute-start | bytes 786440 | tf_op jit(solution)/shard_map/ppermute | solution.py:335
  3.0 0.8 %shard_map.73.refs_0_ = bf16[64,1024]{1,0:T(8,128)(2,1)S(1)} custom-call(bf16[64,512]{1,0:T(8,128)(2,1)} %refs_0_.1, bf16[64,512]{1,0:T(8,128)(2,1)} %refs_1_.1, bf16[64,512]{1,0:T(8,128)(2,1)} %refs_2_.1, bf16[64,512]{1,0:T(8,128)(2,1)} %refs_3_.1), custom_call_target="tpu_custom_call" | custom-call | bytes 1048576 | tf_op jit(solution)/shard_map/pallas_call | solution.py:354
  3.9 3.7 %collective-permute-start.11 = (bf16[64,768]{1,0:T(8,128)(2,1)S(1)}, bf16[64,768]{1,0:T(8,128)(2,1)S(1)}, u32[]{:S(2)}, u32[]{:S(2)}) collective-permute-start(bf16[64,768]{1,0:T(8,128)(2,1)S(1)} %slice.9), channel_id=1, source_target_pairs={{6,0},{7,1},{4,2},{5,3},{2,4},{3,5},{0,6},{1,7},{12,8},{13,9},{14,... | collective-permute-start | bytes 294920 | tf_op jit(solution)/shard_map/ppermute | solution.py:347
  7.6 2.0 %collective-permute-done.9.other_ref = bf16[2,128,512]{2,1,0:T(8,128)(2,1)S(1)} collective-permute-done((bf16[2,128,512]{2,1,0:T(8,128)(2,1)}, bf16[2,128,512]{2,1,0:T(8,128)(2,1)S(1)}, u32[]{:S(2)}, u32[]{:S(2)}) %collective-permute-start.9) | collective-permute-done | bytes 262176 | tf_op jit(solution)/shard_map/ppermute | solution.py:335
  9.6 1.6 %collective-permute-start.2 = (bf16[64,1024]{1,0:T(8,128)(2,1)S(1)}, bf16[64,1024]{1,0:T(8,128)(2,1)S(1)}, u32[]{:S(2)}, u32[]{:S(2)}) collective-permute-start(bf16[64,1024]{1,0:T(8,128)(2,1)S(1)} %shard_map.73.refs_0_), channel_id=1, source_target_pairs={{1,0},{0,1},{3,2},{2,3},{5,4},{4,5},{7,6},{6,7},{11,8},{10,9},{9,1... | collective-permute-start | bytes 393224 | tf_op jit(solution)/shard_map/ppermute | solution.py:347
  11.2 0.7 %collective-permute-start.4 = (bf16[64,1024]{1,0:T(8,128)(2,1)S(1)}, bf16[64,1024]{1,0:T(8,128)(2,1)S(1)}, u32[]{:S(2)}, u32[]{:S(2)}) collective-permute-start(bf16[64,1024]{1,0:T(8,128)(2,1)S(1)} %shard_map.73.refs_0_), channel_id=1, source_target_pairs={{10,8},{11,9},{8,10},{9,11},{14,12},{15,13},{12,14},{13,15},{26,24... | collective-permute-start | bytes 393224 | tf_op jit(solution)/shard_map/ppermute | solution.py:347
  11.9 0.8 %collective-permute-start.13 = (bf16[64,768]{1,0:T(8,128)(2,1)S(1)}, bf16[64,768]{1,0:T(8,128)(2,1)S(1)}, u32[]{:S(2)}, u32[]{:S(2)}) collective-permute-start(bf16[64,768]{1,0:T(8,128)(2,1)S(1)} %collective-permute-done.11.refs_1_), channel_id=1, source_target_pairs={{1,0},{0,1},{3,2},{2,3},{5,4},{4,5},{7,6},{6,7},{9,8},{8,9},{11,10... | collective-permute-start | bytes 294920 | tf_op jit(solution)/shard_map/ppermute | solution.py:347
  12.7 3.3 %collective-permute-done.2.refs_3_ = bf16[64,1024]{1,0:T(8,128)(2,1)S(1)} collective-permute-done((bf16[64,1024]{1,0:T(8,128)(2,1)S(1)}, bf16[64,1024]{1,0:T(8,128)(2,1)S(1)}, u32[]{:S(2)}, u32[]{:S(2)}) %collective-permute-start.2) | collective-permute-done | bytes 131104 | tf_op jit(solution)/shard_map/ppermute | solution.py:347
  16.0 2.2 %collective-permute-start.5 = (bf16[64,1024]{1,0:T(8,128)(2,1)S(1)}, bf16[64,1024]{1,0:T(8,128)(2,1)S(1)}, u32[]{:S(2)}, u32[]{:S(2)}) collective-permute-start(bf16[64,1024]{1,0:T(8,128)(2,1)S(1)} %collective-permute-done.4.refs_5_), channel_id=1, source_target_pairs={{0,8},{8,0},{16,24},{24,16},{1,9},{9,1},{17,25},{25,17},{2,10},{10... | collective-permute-start | bytes 393224 | tf_op jit(solution)/shard_map/ppermute | solution.py:338
  18.2 0.5 %collective-permute-start.14 = (bf16[64,768]{1,0:T(8,128)(2,1)S(1)}, bf16[64,768]{1,0:T(8,128)(2,1)S(1)}, u32[]{:S(2)}, u32[]{:S(2)}) collective-permute-start(bf16[64,768]{1,0:T(8,128)(2,1)S(1)} %collective-permute-done.13.refs_7_), channel_id=1, source_target_pairs={{0,8},{8,0},{16,24},{24,16},{1,9},{9,1},{17,25},{25,17},{2,10},{10... | collective-permute-start | bytes 294920 | tf_op jit(solution)/shard_map/ppermute | solution.py:338
  18.7 0.8 %shard_map.74 = (bf16[512,512]{1,0:T(8,128)(2,1)S(1)}, s32[2,8,128]{2,1,0:T(8,128)S(1)}) custom-call(s32[2,2]{1,0:T(2,128)S(1)} %copy-done.2, f32[1,512]{1,0:T(1,128)S(1)} %bitcast.3, bf16[2,128,512]{2,1,0:T(8,128)(2,1)S(1)} %copy-done, bf16[2,128,512]{2,1,0:T(8,128)(2,1)S(1)} %collective-permute-done.8.beside_ref, ...), custom_call_target="tpu_custom_call" | custom-call | flops 2097152 | bytes 1048576 | tf_op jit(solution)/shard_map/pallas_call | solution.py:354
  19.6 0.9 %shard_map.75 = (bf16[256,256]{1,0:T(8,128)(2,1)S(1)}, bf16[512,768]{1,0:T(8,128)(2,1)S(1)}, bf16[256,256]{1,0:T(8,128)(2,1)S(1)}, bf16[256,256]{1,0:T(8,128)(2,1)S(1)}) custom-call(s32[2,8,128]{2,1,0:T(8,128)S(1)} %get-tuple-element.16.bounds_ref, bf16[512,512]{1,0:T(8,128)(2,1)S(1)} %get-tuple-element.17.normed_ref, ...), custom_call_target="tpu_custom_call" | custom-call | flops 268435456 | bytes 1048576 | tf_op jit(solution)/shard_map/pallas_call | solution.py:354
  20.6 1.6 %collective-permute-start.15 = (bf16[256,256]{1,0:T(8,128)(2,1)S(1)}, bf16[256,256]{1,0:T(8,128)(2,1)S(1)}, u32[]{:S(2)}, u32[]{:S(2)}) collective-permute-start(bf16[256,256]{1,0:T(8,128)(2,1)S(1)} %get-tuple-element.18.refs_9_), channel_id=1, source_target_pairs={{0,16},{8,24},{16,0},{24,8},{1,17},{9,25},{17,1},{25,9},{2,18},{10... | collective-permute-start | bytes 393224 | tf_op jit(solution)/shard_map/ppermute | solution.py:335
  22.1 1.1 %shard_map.77.mine_ref = bf16[256,256]{1,0:T(8,128)(2,1)S(1)} custom-call(s32[2,8,128]{2,1,0:T(8,128)S(1)} %get-tuple-element.16.bounds_ref, bf16[512,512]{1,0:T(8,128)(2,1)S(1)} %get-tuple-element.17.normed_ref, bf16[512,768]{1,0:T(8,128)(2,1)S(1)} %get-tuple-element.20.weights, bf16[256,256]{1,0:T(8,128)(2,1)S(1)} %get-tuple-element.21.low_keys, ...), custom_call_target="tpu_custom_call" | custom-call | flops 335544320 | bytes 1048576 | tf_op jit(solution)/shard_map/pallas_call | solution.py:354
  23.3 0.6 %collective-permute-start.16 = (bf16[256,256]{1,0:T(8,128)(2,1)S(1)}, bf16[256,256]{1,0:T(8,128)(2,1)S(1)}, u32[]{:S(2)}, u32[]{:S(2)}) collective-permute-start(bf16[256,256]{1,0:T(8,128)(2,1)S(1)} %shard_map.77.mine_ref), channel_id=1, source_target_pairs={{0,16},{8,24},{16,0},{24,8},{1,17},{9,25},{17,1},{25,9},{2,18},{10... | collective-permute-start | bytes 393224 | tf_op jit(solution)/shard_map/ppermute | solution.py:335
  23.9 3.4 %collective-permute-start = (bf16[64,256]{1,0:T(8,128)(2,1)S(1)}, bf16[64,256]{1,0:T(8,128)(2,1)S(1)}, u32[]{:S(2)}, u32[]{:S(2)}) collective-permute-start(bf16[64,256]{1,0:T(8,128)(2,1)S(1)} %slice.8), channel_id=1, source_target_pairs={{6,0},{7,1},{4,2},{5,3},{2,4},{3,5},{0,6},{1,7},{12,8},{13,9},{14,... | collective-permute-start | bytes 98312 | tf_op jit(solution)/shard_map/ppermute | solution.py:347
  27.2 2.4 %collective-permute-done.refs_1_ = bf16[64,256]{1,0:T(8,128)(2,1)S(1)} collective-permute-done((bf16[64,256]{1,0:T(8,128)(2,1)S(1)}, bf16[64,256]{1,0:T(8,128)(2,1)S(1)}, u32[]{:S(2)}, u32[]{:S(2)}) %collective-permute-start) | collective-permute-done | bytes 32800 | tf_op jit(solution)/shard_map/ppermute | solution.py:347
  29.6 1.5 %collective-permute-start.6 = (bf16[64,256]{1,0:T(8,128)(2,1)S(1)}, bf16[64,256]{1,0:T(8,128)(2,1)S(1)}, u32[]{:S(2)}, u32[]{:S(2)}) collective-permute-start(bf16[64,256]{1,0:T(8,128)(2,1)S(1)} %collective-permute-done.refs_1_), channel_id=1, source_target_pairs={{1,0},{0,1},{3,2},{2,3},{5,4},{4,5},{7,6},{6,7},{9,8},{8,9},{11,10... | collective-permute-start | bytes 98312 | tf_op jit(solution)/shard_map/ppermute | solution.py:347
  31.1 2.4 %collective-permute-done.6.refs_7_ = bf16[64,256]{1,0:T(8,128)(2,1)S(1)} collective-permute-done((bf16[64,256]{1,0:T(8,128)(2,1)S(1)}, bf16[64,256]{1,0:T(8,128)(2,1)S(1)}, u32[]{:S(2)}, u32[]{:S(2)}) %collective-permute-start.6) | collective-permute-done | bytes 32800 | tf_op jit(solution)/shard_map/ppermute | solution.py:347
  33.5 1.2 %collective-permute-done.7.refs_8_ = bf16[64,256]{1,0:T(8,128)(2,1)S(1)} collective-permute-done((bf16[64,256]{1,0:T(8,128)(2,1)S(1)}, bf16[64,256]{1,0:T(8,128)(2,1)S(1)}, u32[]{:S(2)}, u32[]{:S(2)}) %collective-permute-start.7) | collective-permute-done | bytes 32800 | tf_op jit(solution)/shard_map/ppermute | solution.py:338
  35.6 0.4 %collective-permute-start.18 = (bf16[128,256]{1,0:T(8,128)(2,1)S(1)}, bf16[128,256]{1,0:T(8,128)(2,1)S(1)}, u32[]{:S(2)}, u32[]{:S(2)}) collective-permute-start(bf16[128,256]{1,0:T(8,128)(2,1)S(1)} %shard_map.80), channel_id=1, source_target_pairs={{0,8},{8,0},{16,24},{24,16},{1,9},{9,1},{17,25},{25,17},{2,10},{10... | collective-permute-start | bytes 196616 | tf_op jit(solution)/shard_map/ppermute | solution.py:338
  36.1 0.5 %collective-permute-done.17.received_ref = bf16[128,256]{1,0:T(8,128)(2,1)S(1)} collective-permute-done((bf16[128,256]{1,0:T(8,128)(2,1)S(1)}, bf16[128,256]{1,0:T(8,128)(2,1)S(1)}, u32[]{:S(2)}, u32[]{:S(2)}) %collective-permute-start.17) | collective-permute-done | bytes 65568 | tf_op jit(solution)/shard_map/ppermute | solution.py:338
  36.6 0.8 %shard_map.79 = bf16[2,128,512]{2,1,0:T(8,128)(2,1)} custom-call(bf16[256,512]{1,0:T(8,128)(2,1)S(1)} %get-tuple-element.19.weights, f32[128,256]{1,0:T(8,128)S(1)} %get-tuple-element.23.partial_ref, bf16[256,256]{1,0:T(8,128)(2,1)S(1)} %collective-permute-done.16.other_ref, bf16[128,256]{1,0:T(8,128)(2,1)S(1)} %get-tuple-element.24.low_ref, ...), custom_call_target="tpu_custom_call" | custom-call | flops 16777216 | bytes 1048576 | tf_op jit(solution)/shard_map/pallas_call | solution.py:354
  37.4 0.6 %bitcast_dynamic-update-slice_fusion = bf16[2,128,512]{2,1,0:T(8,128)(2,1)} fusion(bf16[2,128,512]{2,1,0:T(8,128)(2,1)} %shard_map.79, s32[]{:T(128)S(6)} %select_n.11, bf16[128,256]{1,0:T(8,128)(2,1)S(1)} %collective-permute-done.18), kind=kLoop, calls=%fused_computation | loop fusion | bytes 131076 | tf_op jit(solution)/shard_map/dynamic_update_slice | solution.py:452
  (31 shorter events, 1.1 us)
Async XLA Ops:
  0.0 18.7 %copy-start = (bf16[2,128,512]{2,1,0:T(8,128)(2,1)S(1)}, bf16[2,128,512]{2,1,0:T(8,128)(2,1)}, u32[]{:S(2)}) copy-start(bf16[2,128,512]{2,1,0:T(8,128)(2,1)} %mine_ref.1) | copy-start | bytes 786436
  0.0 9.6 %collective-permute-start.9 = (bf16[2,128,512]{2,1,0:T(8,128)(2,1)}, bf16[2,128,512]{2,1,0:T(8,128)(2,1)S(1)}, u32[]{:S(2)}, u32[]{:S(2)}) collective-permute-start(bf16[2,128,512]{2,1,0:T(8,128)(2,1)} %mine_ref.1), channel_id=1, source_target_pairs={{0,16},{8,24},{16,0},{24,8},{1,17},{9,25},{17,1},{25,9},{2,18},{10... | collective-permute-start | bytes 786440 | tf_op jit(solution)/shard_map/ppermute | solution.py:335
  3.0 15.2 %collective-permute-start.8 = (bf16[2,128,512]{2,1,0:T(8,128)(2,1)}, bf16[2,128,512]{2,1,0:T(8,128)(2,1)S(1)}, u32[]{:S(2)}, u32[]{:S(2)}) collective-permute-start(bf16[2,128,512]{2,1,0:T(8,128)(2,1)} %mine_ref.1), channel_id=1, source_target_pairs={{0,8},{8,0},{16,24},{24,16},{1,9},{9,1},{17,25},{25,17},{2,10},{10... | collective-permute-start | bytes 786440 | tf_op jit(solution)/shard_map/ppermute | solution.py:338
  3.8 14.8 %copy-start.1 = (f32[512]{0:T(512)S(1)}, f32[512]{0:T(512)}, u32[]{:S(2)}) copy-start(f32[512]{0:T(512)} %param.8) | copy-start | bytes 6148
  3.9 14.8 %copy-start.2 = (s32[2,2]{1,0:T(2,128)S(1)}, s32[2,2]{1,0:T(2,128)}, u32[]{:S(2)}) copy-start(s32[2,2]{1,0:T(2,128)} %tracks_ref.1) | copy-start | bytes 52
  3.9 8.0 %collective-permute-start.11 = (bf16[64,768]{1,0:T(8,128)(2,1)S(1)}, bf16[64,768]{1,0:T(8,128)(2,1)S(1)}, u32[]{:S(2)}, u32[]{:S(2)}) collective-permute-start(bf16[64,768]{1,0:T(8,128)(2,1)S(1)} %slice.9), channel_id=1, source_target_pairs={{6,0},{7,1},{4,2},{5,3},{2,4},{3,5},{0,6},{1,7},{12,8},{13,9},{14,... | collective-permute-start | bytes 294920 | tf_op jit(solution)/shard_map/ppermute | solution.py:347
  9.6 9.1 %collective-permute-start.10 = (bf16[2,128,512]{2,1,0:T(8,128)(2,1)S(1)}, bf16[2,128,512]{2,1,0:T(8,128)(2,1)S(1)}, u32[]{:S(2)}, u32[]{:S(2)}) collective-permute-start(bf16[2,128,512]{2,1,0:T(8,128)(2,1)S(1)} %collective-permute-done.9.other_ref), channel_id=1, source_target_pairs={{0,8},{8,0},{16,24},{24,16},{1,9},{9,1},{17,25},{25,17},{2,10},{10... | collective-permute-start | bytes 786440 | tf_op jit(solution)/shard_map/ppermute | solution.py:338
  9.6 6.4 %collective-permute-start.2 = (bf16[64,1024]{1,0:T(8,128)(2,1)S(1)}, bf16[64,1024]{1,0:T(8,128)(2,1)S(1)}, u32[]{:S(2)}, u32[]{:S(2)}) collective-permute-start(bf16[64,1024]{1,0:T(8,128)(2,1)S(1)} %shard_map.73.refs_0_), channel_id=1, source_target_pairs={{1,0},{0,1},{3,2},{2,3},{5,4},{4,5},{7,6},{6,7},{11,8},{10,9},{9,1... | collective-permute-start | bytes 393224 | tf_op jit(solution)/shard_map/ppermute | solution.py:347
  11.2 4.7 %collective-permute-start.4 = (bf16[64,1024]{1,0:T(8,128)(2,1)S(1)}, bf16[64,1024]{1,0:T(8,128)(2,1)S(1)}, u32[]{:S(2)}, u32[]{:S(2)}) collective-permute-start(bf16[64,1024]{1,0:T(8,128)(2,1)S(1)} %shard_map.73.refs_0_), channel_id=1, source_target_pairs={{10,8},{11,9},{8,10},{9,11},{14,12},{15,13},{12,14},{13,15},{26,24... | collective-permute-start | bytes 393224 | tf_op jit(solution)/shard_map/ppermute | solution.py:347
  11.9 6.3 %collective-permute-start.13 = (bf16[64,768]{1,0:T(8,128)(2,1)S(1)}, bf16[64,768]{1,0:T(8,128)(2,1)S(1)}, u32[]{:S(2)}, u32[]{:S(2)}) collective-permute-start(bf16[64,768]{1,0:T(8,128)(2,1)S(1)} %collective-permute-done.11.refs_1_), channel_id=1, source_target_pairs={{1,0},{0,1},{3,2},{2,3},{5,4},{4,5},{7,6},{6,7},{9,8},{8,9},{11,10... | collective-permute-start | bytes 294920 | tf_op jit(solution)/shard_map/ppermute | solution.py:347
  16.0 3.5 %collective-permute-start.3 = (bf16[64,1024]{1,0:T(8,128)(2,1)S(1)}, bf16[64,1024]{1,0:T(8,128)(2,1)S(1)}, u32[]{:S(2)}, u32[]{:S(2)}) collective-permute-start(bf16[64,1024]{1,0:T(8,128)(2,1)S(1)} %collective-permute-done.2.refs_3_), channel_id=1, source_target_pairs={{0,8},{8,0},{16,24},{24,16},{1,9},{9,1},{17,25},{25,17},{2,10},{10... | collective-permute-start | bytes 393224 | tf_op jit(solution)/shard_map/ppermute | solution.py:338
  16.0 3.6 %collective-permute-start.5 = (bf16[64,1024]{1,0:T(8,128)(2,1)S(1)}, bf16[64,1024]{1,0:T(8,128)(2,1)S(1)}, u32[]{:S(2)}, u32[]{:S(2)}) collective-permute-start(bf16[64,1024]{1,0:T(8,128)(2,1)S(1)} %collective-permute-done.4.refs_5_), channel_id=1, source_target_pairs={{0,8},{8,0},{16,24},{24,16},{1,9},{9,1},{17,25},{25,17},{2,10},{10... | collective-permute-start | bytes 393224 | tf_op jit(solution)/shard_map/ppermute | solution.py:338
  18.2 1.3 %collective-permute-start.12 = (bf16[64,768]{1,0:T(8,128)(2,1)S(1)}, bf16[64,768]{1,0:T(8,128)(2,1)S(1)}, u32[]{:S(2)}, u32[]{:S(2)}) collective-permute-start(bf16[64,768]{1,0:T(8,128)(2,1)S(1)} %collective-permute-done.11.refs_1_), channel_id=1, source_target_pairs={{0,8},{8,0},{16,24},{24,16},{1,9},{9,1},{17,25},{25,17},{2,10},{10... | collective-permute-start | bytes 294920 | tf_op jit(solution)/shard_map/ppermute | solution.py:338
  18.2 1.5 %collective-permute-start.14 = (bf16[64,768]{1,0:T(8,128)(2,1)S(1)}, bf16[64,768]{1,0:T(8,128)(2,1)S(1)}, u32[]{:S(2)}, u32[]{:S(2)}) collective-permute-start(bf16[64,768]{1,0:T(8,128)(2,1)S(1)} %collective-permute-done.13.refs_7_), channel_id=1, source_target_pairs={{0,8},{8,0},{16,24},{24,16},{1,9},{9,1},{17,25},{25,17},{2,10},{10... | collective-permute-start | bytes 294920 | tf_op jit(solution)/shard_map/ppermute | solution.py:338
  20.6 14.1 %collective-permute-start.15 = (bf16[256,256]{1,0:T(8,128)(2,1)S(1)}, bf16[256,256]{1,0:T(8,128)(2,1)S(1)}, u32[]{:S(2)}, u32[]{:S(2)}) collective-permute-start(bf16[256,256]{1,0:T(8,128)(2,1)S(1)} %get-tuple-element.18.refs_9_), channel_id=1, source_target_pairs={{0,16},{8,24},{16,0},{24,8},{1,17},{9,25},{17,1},{25,9},{2,18},{10... | collective-permute-start | bytes 393224 | tf_op jit(solution)/shard_map/ppermute | solution.py:335
  23.3 12.2 %collective-permute-start.16 = (bf16[256,256]{1,0:T(8,128)(2,1)S(1)}, bf16[256,256]{1,0:T(8,128)(2,1)S(1)}, u32[]{:S(2)}, u32[]{:S(2)}) collective-permute-start(bf16[256,256]{1,0:T(8,128)(2,1)S(1)} %shard_map.77.mine_ref), channel_id=1, source_target_pairs={{0,16},{8,24},{16,0},{24,8},{1,17},{9,25},{17,1},{25,9},{2,18},{10... | collective-permute-start | bytes 393224 | tf_op jit(solution)/shard_map/ppermute | solution.py:335
  23.9 5.7 %collective-permute-start = (bf16[64,256]{1,0:T(8,128)(2,1)S(1)}, bf16[64,256]{1,0:T(8,128)(2,1)S(1)}, u32[]{:S(2)}, u32[]{:S(2)}) collective-permute-start(bf16[64,256]{1,0:T(8,128)(2,1)S(1)} %slice.8), channel_id=1, source_target_pairs={{6,0},{7,1},{4,2},{5,3},{2,4},{3,5},{0,6},{1,7},{12,8},{13,9},{14,... | collective-permute-start | bytes 98312 | tf_op jit(solution)/shard_map/ppermute | solution.py:347
  29.6 3.9 %collective-permute-start.6 = (bf16[64,256]{1,0:T(8,128)(2,1)S(1)}, bf16[64,256]{1,0:T(8,128)(2,1)S(1)}, u32[]{:S(2)}, u32[]{:S(2)}) collective-permute-start(bf16[64,256]{1,0:T(8,128)(2,1)S(1)} %collective-permute-done.refs_1_), channel_id=1, source_target_pairs={{1,0},{0,1},{3,2},{2,3},{5,4},{4,5},{7,6},{6,7},{9,8},{8,9},{11,10... | collective-permute-start | bytes 98312 | tf_op jit(solution)/shard_map/ppermute | solution.py:347
  31.1 2.4 %collective-permute-start.1 = (bf16[64,256]{1,0:T(8,128)(2,1)S(1)}, bf16[64,256]{1,0:T(8,128)(2,1)S(1)}, u32[]{:S(2)}, u32[]{:S(2)}) collective-permute-start(bf16[64,256]{1,0:T(8,128)(2,1)S(1)} %collective-permute-done.refs_1_), channel_id=1, source_target_pairs={{0,8},{8,0},{16,24},{24,16},{1,9},{9,1},{17,25},{25,17},{2,10},{10... | collective-permute-start | bytes 98312 | tf_op jit(solution)/shard_map/ppermute | solution.py:338
  33.5 1.2 %collective-permute-start.7 = (bf16[64,256]{1,0:T(8,128)(2,1)S(1)}, bf16[64,256]{1,0:T(8,128)(2,1)S(1)}, u32[]{:S(2)}, u32[]{:S(2)}) collective-permute-start(bf16[64,256]{1,0:T(8,128)(2,1)S(1)} %collective-permute-done.6.refs_7_), channel_id=1, source_target_pairs={{0,8},{8,0},{16,24},{24,16},{1,9},{9,1},{17,25},{25,17},{2,10},{10... | collective-permute-start | bytes 98312 | tf_op jit(solution)/shard_map/ppermute | solution.py:338
  35.2 1.3 %collective-permute-start.17 = (bf16[128,256]{1,0:T(8,128)(2,1)S(1)}, bf16[128,256]{1,0:T(8,128)(2,1)S(1)}, u32[]{:S(2)}, u32[]{:S(2)}) collective-permute-start(bf16[128,256]{1,0:T(8,128)(2,1)S(1)} %get-tuple-element.25), channel_id=1, source_target_pairs={{0,8},{8,0},{16,24},{24,16},{1,9},{9,1},{17,25},{25,17},{2,10},{10... | collective-permute-start | bytes 196616 | tf_op jit(solution)/shard_map/ppermute | solution.py:338
  35.6 1.7 %collective-permute-start.18 = (bf16[128,256]{1,0:T(8,128)(2,1)S(1)}, bf16[128,256]{1,0:T(8,128)(2,1)S(1)}, u32[]{:S(2)}, u32[]{:S(2)}) collective-permute-start(bf16[128,256]{1,0:T(8,128)(2,1)S(1)} %shard_map.80), channel_id=1, source_target_pairs={{0,8},{8,0},{16,24},{24,16},{1,9},{9,1},{17,25},{25,17},{2,10},{10... | collective-permute-start | bytes 196616 | tf_op jit(solution)/shard_map/ppermute | solution.py:338
